TPU v7x, 512 devices: a whole 4x4x16 slice. The times are simulated.
512 devices in a mesh: fz: 32 (over y, x, core), fxy: 16 (over z).
Axes of the slice: x: 4, y: 4, z: 16, core: 2. Of those that a mesh axis runs over, the one named last changes fastest.
Arguments:
- e_field: float32 [3, 256, 256, 512], P(None, 'fz', 'fxy'), may hold values from -6 to 6
- h_field: float32 [3, 256, 256, 512], P(None, 'fz', 'fxy'), may hold values from -6 to 6
- e_decay: float32 [256, 256, 512], P('fz', 'fxy'), may hold values from 0.6 to 1
- e_gain: float32 [256, 256, 512], P('fz', 'fxy'), may hold values from 0.2 to 0.6
- port_cell: int32 [32, 1024], P('fz', 'fxy'), may hold values from 0 to 65535
- port_node: int32 [32, 1024], P('fz', 'fxy'), may hold values from 0 to 2047
- port_conductance: float32 [32, 1024], P('fz', 'fxy'), may hold values from 0.5 to 2
- inverse: float32 [32, 2048, 2048], P('fz', 'fxy'), may hold values from -1 to 2, as said below
- line_near: int32 [32, 128], P('fz'), may hold values from 0 to 2047
- line_far: int32 [32, 128], P('fz'), may hold values from 0 to 2047
- line_delay: int32 [32, 128], P('fz'), may hold values from 1 to 6
- line_imped: float32 [32, 128], P('fz'), may hold values from 0.5 to 4
- hist_near: float32 [32, 6, 128], P('fz'), may hold values from -6 to 6
- hist_far: float32 [32, 6, 128], P('fz'), may hold values from -6 to 6
Outputs:
- e_out: float32 [3, 256, 256, 512], P(None, 'fz', 'fxy')
- h_out: float32 [3, 256, 256, 512], P(None, 'fz', 'fxy')
- node_volt: float32 [32, 2048], P('fz', 'fxy')
- line_wave: float32 [32, 2, 128], P('fz')
Inputs may be any that keep to these rules, and one draw needn't show every extreme that they name: inverse[s] is symmetric for every s.
All inputs are finite; a program needn't handle non-finite values.
Results may differ from a plain program's by a relative error of at most 0.00029.
Values sent between devices are 32-bit elements; how exact they have to be, the bound alone decides.
No kernel may reach another device: no remote copies, remote signals or barrier semaphores. Data moves between devices by JAX's collectives and lax.ppermute only.
A program may use at most 64 MiB of HBM per device.

v0:
```python
import jax
import jax.numpy as jnp
from jax import lax
from jax.sharding import PartitionSpec as P

STEPS = 4


def shifted(value, axis, by):
    devices = lax.axis_size(axis)
    pairs = [(i, i + by) for i in range(devices) if 0 <= i + by < devices]
    return lax.ppermute(value, axis, pairs)


def copy_for_each(value, axis):
    devices = lax.axis_size(axis)
    return lax.all_to_all(
        jnp.broadcast_to(value[None], (devices, *value.shape)), axis, 0, 0, tiled=True
    )


def over_copies(value, axis):
    return copy_for_each(value, axis).sum(axis=0)


def joined_along(blocks, dim):
    shape = list(blocks.shape[1:])
    shape[dim] *= blocks.shape[0]
    return jnp.moveaxis(blocks, 0, dim).reshape(shape)


def gathered_copies(value, axis, dim):
    return joined_along(copy_for_each(value, axis), dim)


def forward_z(values, upper_face):
    return jnp.concatenate([values[1:], upper_face[None]], 0) - values


def forward_x(values, side_face):
    return jnp.concatenate([values[:, 1:], side_face[:, None]], 1) - values


def forward_y(values):
    return jnp.concatenate([values[:, :, 1:], jnp.zeros_like(values[:, :, :1])], 2) - values


def backward_z(values, lower_face):
    return values - jnp.concatenate([lower_face[None], values[:-1]], 0)


def backward_x(values, side_face):
    return values - jnp.concatenate([side_face[:, None], values[:, :-1]], 1)


def backward_y(values):
    return values - jnp.concatenate([jnp.zeros_like(values[:, :, :1]), values[:, :, :-1]], 2)


def curl_electric(e_field, upper_face, side_face):
    return jnp.stack(
        [
            forward_y(e_field[2]) - forward_z(e_field[1], upper_face[1]),
            forward_z(e_field[0], upper_face[0]) - forward_x(e_field[2], side_face[1]),
            forward_x(e_field[1], side_face[0]) - forward_y(e_field[0]),
        ]
    )


def curl_magnetic(h_field, lower_face, side_face):
    return jnp.stack(
        [
            backward_y(h_field[2]) - backward_z(h_field[1], lower_face[1]),
            backward_z(h_field[0], lower_face[0]) - backward_x(h_field[2], side_face[1]),
            backward_x(h_field[1], side_face[0]) - backward_y(h_field[0]),
        ]
    )


def local(
    e_field,
    h_field,
    e_decay,
    e_gain,
    port_cell,
    port_node,
    port_conductance,
    inverse,
    line_near,
    line_far,
    line_delay,
    line_imped,
    hist_near,
    hist_far,
):
    node_count = inverse.shape[2]
    port_cells = port_cell[0]
    port_targets = port_node[0]
    conductance = port_conductance[0]
    near_nodes = line_near[0]
    far_nodes = line_far[0]
    delays = line_delay[0]
    impedance = line_imped[0]
    depth = hist_near.shape[1]
    wave_near = hist_near[0, ::-1]
    wave_far = hist_far[0, ::-1]
    gain_flat = e_gain.reshape(-1)
    empty_nodes = jnp.zeros((node_count,), jnp.float32)
    for step_index in range(STEPS):
        position = (step_index - delays + depth)[None, :]
        incoming_a = jnp.take_along_axis(wave_far, position, axis=0)[0]
        incoming_b = jnp.take_along_axis(wave_near, position, axis=0)[0]
        far_sources = empty_nodes.at[far_nodes].add(-incoming_b)
        lower_face, received = shifted((h_field[0:2, -1], far_sources), "fz", 1)
        behind_face = shifted(h_field[1:3, :, -1], "fxy", 1)
        ez_ports = e_field[2].reshape(-1)[port_cells]
        weighted = conductance * ez_ports
        line_sources = empty_nodes.at[near_nodes].add(-incoming_a) + received
        partial_value = empty_nodes.at[port_targets].add(weighted)
        totals = over_copies(partial_value, "fxy") + line_sources
        local_volts = jnp.dot(inverse[0], totals, precision=lax.Precision.HIGHEST)
        volts = gathered_copies(local_volts, "fxy", 0)
        current = conductance * (ez_ports - volts[port_targets])
        e_field = e_decay * e_field + e_gain * curl_magnetic(h_field, lower_face, behind_face)
        vertical = e_field[2].reshape(-1).at[port_cells].add(-gain_flat[port_cells] * current)
        e_field = e_field.at[2].set(vertical.reshape(e_field.shape[1:]))
        out_near = -2.0 * volts[near_nodes] / impedance - incoming_a
        upper_face, volts_above = shifted((e_field[0:2, 0], volts), "fz", -1)
        beside_face = shifted(e_field[1:3, :, 0], "fxy", -1)
        out_far = -2.0 * volts_above[far_nodes] / impedance - incoming_b
        h_field = h_field - 0.5 * curl_electric(e_field, upper_face, beside_face)
        wave_near = jnp.concatenate([wave_near, out_near[None]], 0)
        wave_far = jnp.concatenate([wave_far, out_far[None]], 0)
    line_wave = jnp.stack([out_near, out_far], 0)[None]
    return (e_field, h_field, local_volts[None], line_wave)


def solution(mesh):
    placed = (
        P(None, "fz", "fxy", None),
        P(None, "fz", "fxy", None),
        P("fz", "fxy", None),
        P("fz", "fxy", None),
        P("fz", "fxy"),
        P("fz", "fxy"),
        P("fz", "fxy"),
        P("fz", "fxy", None),
        P("fz", None),
        P("fz", None),
        P("fz", None),
        P("fz", None),
        P("fz", None, None),
        P("fz", None, None),
    )
    return jax.shard_map(
        local,
        mesh=mesh,
        in_specs=placed,
        out_specs=(
            P(None, "fz", "fxy", None),
            P(None, "fz", "fxy", None),
            P("fz", "fxy"),
            P("fz", None, None),
        ),
        check_vma=False,
    )
```

profile of v0, /device:TPU:7, one launch (start us, length us, event | category | flops | bytes accessed | tf_op | source)
XLA Modules:
  0.0 322.5 jit_solution(11790371990267215752)
XLA Ops:
  6.1 1.3 scatter_custom_fusion.1
  7.4 3.7 %collective-permute-start.2 = (f32[2048]{0:T(1024)S(1)}, f32[2048]{0:T(1024)S(1)}, u32[]{:S(2)}, u32[]{:S(2)}) collective-permute-start(f32[2048]{0:T(1024)S(1)} %scatter_custom_fusion.1), channel_id=1, source_target_pairs={{0,16},{16,32},{32,48},{48,64},{64,80},{80,96},{96,112},{112,128},... | collective-permute-start | bytes 24584 | tf_op jit(solution)/shard_map/ppermute | solution.py:12
  11.2 3.5 %collective-permute-start.1 = (f32[2,8,512]{2,0,1:T(2,128)S(1)}, f32[2,8,512]{2,0,1:T(2,128)S(1)}, u32[]{:S(2)}, u32[]{:S(2)}) collective-permute-start(f32[2,8,512]{2,0,1:T(2,128)S(1)} %bitcast.541), channel_id=1, source_target_pairs={{0,1},{1,2},{2,3},{3,4},{4,5},{5,6},{6,7},{7,8},{8,9},{9,10},{10,1... | collective-permute-start | bytes 98312 | tf_op jit(solution)/shard_map/ppermute | solution.py:12
  14.7 2.2 collective-permute-start
  20.5 14.1 %all-to-all-start = ((f32[16,1,2048]{2,1,0:T(1,128)}), f32[16,1,2048]{2,1,0:T(1,128)}, u32[]{:S(2)}, u32[]{:S(2)}) async-start(f32[16,1,2048]{2,1,0:T(1,128)} %broadcast_in_dim.33), calls=%async_computation | async-start | bytes 262144 | tf_op jit(solution)/shard_map/all_to_all | solution.py:17
  39.7 7.1 %all-to-all-done = f32[16,1,2048]{2,1,0:T(1,128)} async-done(((f32[16,1,2048]{2,1,0:T(1,128)}), f32[16,1,2048]{2,1,0:T(1,128)}, u32[]{:S(2)}, u32[]{:S(2)}) %all-to-all-start) | async-done | bytes 131104 | tf_op jit(solution)/shard_map/all_to_all | solution.py:17
  47.8 1.2 scatter_fusion
  50.6 6.4 %all-to-all-start.1 = ((f32[16,1,128]{2,1,0:T(1,128)}), f32[16,1,128]{2,1,0:T(1,128)S(1)}, u32[]{:S(2)}, u32[]{:S(2)}) async-start(f32[16,1,128]{2,1,0:T(1,128)} %broadcast_in_dim.34), calls=%async_computation.1 | async-start | bytes 16384 | tf_op jit(solution)/shard_map/all_to_all | solution.py:17
  57.1 1.5 fusion.5
  58.7 9.6 %all-to-all-done.1 = f32[16,1,128]{2,1,0:T(1,128)S(1)} async-done(((f32[16,1,128]{2,1,0:T(1,128)}), f32[16,1,128]{2,1,0:T(1,128)S(1)}, u32[]{:S(2)}, u32[]{:S(2)}) %all-to-all-start.1) | async-done | bytes 8224 | tf_op jit(solution)/shard_map/all_to_all | solution.py:17
  68.3 3.9 %collective-permute-start.8 = (f32[2048]{0:T(1024)S(1)}, f32[2048]{0:T(1024)S(1)}, u32[]{:S(2)}, u32[]{:S(2)}) collective-permute-start(f32[2048]{0:T(1024)S(1)} %bitcast.499), channel_id=1, source_target_pairs={{16,0},{32,16},{48,32},{64,48},{80,64},{96,80},{112,96},{128,112},... | collective-permute-start | bytes 24584 | tf_op jit(solution)/shard_map/ppermute | solution.py:12
  77.4 1.7 gather_fusion.4
  80.9 4.2 %all-to-all-start.2 = ((f32[16,1,2048]{2,1,0:T(1,128)}), f32[16,1,2048]{2,1,0:T(1,128)}, u32[]{:S(2)}, u32[]{:S(2)}) async-start(f32[16,1,2048]{2,1,0:T(1,128)} %broadcast_in_dim.35), calls=%async_computation.2 | async-start | bytes 262144 | tf_op jit(solution)/shard_map/all_to_all | solution.py:17
  85.7 1.3 collective-permute-start.4
  87.0 1.9 collective-permute-start.3
  88.9 1.3 gather_fusion.5
  94.0 1.4 scatter_custom_fusion.5
  95.4 5.9 %collective-permute-start.7 = (f32[2048]{0:T(1024)S(1)}, f32[2048]{0:T(1024)S(1)}, u32[]{:S(2)}, u32[]{:S(2)}) collective-permute-start(f32[2048]{0:T(1024)S(1)} %scatter_custom_fusion.5), channel_id=1, source_target_pairs={{0,16},{16,32},{32,48},{48,64},{64,80},{80,96},{96,112},{112,128},... | collective-permute-start | bytes 24584 | tf_op jit(solution)/shard_map/ppermute | solution.py:12
  106.1 4.0 %collective-permute-start.6 = (f32[2,8,512]{2,0,1:T(2,128)S(1)}, f32[2,8,512]{2,0,1:T(2,128)S(1)}, u32[]{:S(2)}, u32[]{:S(2)}) collective-permute-start(f32[2,8,512]{2,0,1:T(2,128)S(1)} %bitcast.542), channel_id=1, source_target_pairs={{0,1},{1,2},{2,3},{3,4},{4,5},{5,6},{6,7},{7,8},{8,9},{9,10},{10,1... | collective-permute-start | bytes 98312 | tf_op jit(solution)/shard_map/ppermute | solution.py:12
  110.2 2.2 collective-permute-start.5
  112.4 1.3 collective-permute-done.5
  117.2 1.4 scatter_fusion.2
  120.2 11.3 %all-to-all-start.3 = ((f32[16,1,128]{2,1,0:T(1,128)}), f32[16,1,128]{2,1,0:T(1,128)S(1)}, u32[]{:S(2)}, u32[]{:S(2)}) async-start(f32[16,1,128]{2,1,0:T(1,128)} %broadcast_in_dim.36), calls=%async_computation.3 | async-start | bytes 16384 | tf_op jit(solution)/shard_map/all_to_all | solution.py:17
  131.6 1.4 fusion.7
  133.1 9.7 %all-to-all-done.3 = f32[16,1,128]{2,1,0:T(1,128)S(1)} async-done(((f32[16,1,128]{2,1,0:T(1,128)}), f32[16,1,128]{2,1,0:T(1,128)S(1)}, u32[]{:S(2)}, u32[]{:S(2)}) %all-to-all-start.3) | async-done | bytes 8224 | tf_op jit(solution)/shard_map/all_to_all | solution.py:17
  143.8 2.9 collective-permute-start.14
  150.3 1.8 gather_fusion.8
  154.7 4.2 %all-to-all-start.4 = ((f32[16,1,2048]{2,1,0:T(1,128)}), f32[16,1,2048]{2,1,0:T(1,128)}, u32[]{:S(2)}, u32[]{:S(2)}) async-start(f32[16,1,2048]{2,1,0:T(1,128)} %broadcast_in_dim.37), calls=%async_computation.4 | async-start | bytes 262144 | tf_op jit(solution)/shard_map/all_to_all | solution.py:17
  159.6 1.3 collective-permute-start.10
  160.9 1.9 collective-permute-start.9
  162.8 1.3 gather_fusion.9
  168.7 2.0 scatter_custom_fusion.9
  170.7 6.7 %collective-permute-start.13 = (f32[2048]{0:T(1024)}, f32[2048]{0:T(1024)}, u32[]{:S(2)}, u32[]{:S(2)}) collective-permute-start(f32[2048]{0:T(1024)} %scatter_custom_fusion.9), channel_id=1, source_target_pairs={{0,16},{16,32},{32,48},{48,64},{64,80},{80,96},{96,112},{112,128},... | collective-permute-start | bytes 24584 | tf_op jit(solution)/shard_map/ppermute | solution.py:12
  181.8 4.3 %collective-permute-start.12 = (f32[2,8,512]{2,0,1:T(2,128)S(1)}, f32[2,8,512]{2,0,1:T(2,128)S(1)}, u32[]{:S(2)}, u32[]{:S(2)}) collective-permute-start(f32[2,8,512]{2,0,1:T(2,128)S(1)} %bitcast.543), channel_id=1, source_target_pairs={{0,1},{1,2},{2,3},{3,4},{4,5},{5,6},{6,7},{7,8},{8,9},{9,10},{10,1... | collective-permute-start | bytes 98312 | tf_op jit(solution)/shard_map/ppermute | solution.py:12
  186.1 2.7 collective-permute-start.11
  188.9 1.3 collective-permute-done.11
  193.8 1.2 scatter_fusion.4
  196.5 11.6 %all-to-all-start.5 = ((f32[16,1,128]{2,1,0:T(1,128)}), f32[16,1,128]{2,1,0:T(1,128)S(1)}, u32[]{:S(2)}, u32[]{:S(2)}) async-start(f32[16,1,128]{2,1,0:T(1,128)} %broadcast_in_dim.38), calls=%async_computation.5 | async-start | bytes 16384 | tf_op jit(solution)/shard_map/all_to_all | solution.py:17
  208.2 1.4 fusion.9
  209.7 9.8 %all-to-all-done.5 = f32[16,1,128]{2,1,0:T(1,128)S(1)} async-done(((f32[16,1,128]{2,1,0:T(1,128)}), f32[16,1,128]{2,1,0:T(1,128)S(1)}, u32[]{:S(2)}, u32[]{:S(2)}) %all-to-all-start.5) | async-done | bytes 8224 | tf_op jit(solution)/shard_map/all_to_all | solution.py:17
  220.5 2.5 collective-permute-start.20
  227.6 1.3 gather_fusion.12
  231.5 4.2 %all-to-all-start.6 = ((f32[16,1,2048]{2,1,0:T(1,128)}), f32[16,1,2048]{2,1,0:T(1,128)}, u32[]{:S(2)}, u32[]{:S(2)}) async-start(f32[16,1,2048]{2,1,0:T(1,128)} %broadcast_in_dim.39), calls=%async_computation.6 | async-start | bytes 262144 | tf_op jit(solution)/shard_map/all_to_all | solution.py:17
  236.4 1.4 collective-permute-start.16
  237.8 2.1 collective-permute-start.15
  240.0 1.3 gather_fusion.13
  242.7 1.3 gather_fusion.23
  244.0 1.3 gather_fusion.24
  246.3 1.4 scatter_custom_fusion.13
  247.7 7.0 %collective-permute-start.19 = (f32[2048]{0:T(1024)S(1)}, f32[2048]{0:T(1024)S(1)}, u32[]{:S(2)}, u32[]{:S(2)}) collective-permute-start(f32[2048]{0:T(1024)S(1)} %scatter_custom_fusion.13), channel_id=1, source_target_pairs={{0,16},{16,32},{32,48},{48,64},{64,80},{80,96},{96,112},{112,128},... | collective-permute-start | bytes 24584 | tf_op jit(solution)/shard_map/ppermute | solution.py:12
  259.9 4.3 %collective-permute-start.18 = (f32[2,8,512]{2,0,1:T(2,128)S(1)}, f32[2,8,512]{2,0,1:T(2,128)S(1)}, u32[]{:S(2)}, u32[]{:S(2)}) collective-permute-start(f32[2,8,512]{2,0,1:T(2,128)S(1)} %bitcast.544), channel_id=1, source_target_pairs={{0,1},{1,2},{2,3},{3,4},{4,5},{5,6},{6,7},{7,8},{8,9},{9,10},{10,1... | collective-permute-start | bytes 98312 | tf_op jit(solution)/shard_map/ppermute | solution.py:12
  264.2 2.7 collective-permute-start.17
  267.0 1.3 collective-permute-done.17
  271.1 1.2 scatter_fusion.6
  274.4 11.6 %all-to-all-start.7 = ((f32[16,1,128]{2,1,0:T(1,128)}), f32[16,1,128]{2,1,0:T(1,128)S(1)}, u32[]{:S(2)}, u32[]{:S(2)}) async-start(f32[16,1,128]{2,1,0:T(1,128)} %broadcast_in_dim.40), calls=%async_computation.7 | async-start | bytes 16384 | tf_op jit(solution)/shard_map/all_to_all | solution.py:17
  286.0 1.4 fusion.11
  287.6 9.8 %all-to-all-done.7 = f32[16,1,128]{2,1,0:T(1,128)S(1)} async-done(((f32[16,1,128]{2,1,0:T(1,128)}), f32[16,1,128]{2,1,0:T(1,128)S(1)}, u32[]{:S(2)}, u32[]{:S(2)}) %all-to-all-start.7) | async-done | bytes 8224 | tf_op jit(solution)/shard_map/all_to_all | solution.py:17
  298.4 2.5 collective-permute-start.23
  303.2 1.3 gather_fusion.15
  306.0 1.4 collective-permute-start.22
  307.4 1.9 collective-permute-start.21
  309.3 1.3 gather_fusion.16
  311.3 5.2 %collective-permute-done.21 = f32[2,16,512]{2,1,0:T(8,128)} collective-permute-done((f32[2,16,512]{2,1,0:T(8,128)S(1)}, f32[2,16,512]{2,1,0:T(8,128)}, u32[]{:S(2)}, u32[]{:S(2)}) %collective-permute-start.21) | collective-permute-done | bytes 65568 | tf_op jit(solution)/shard_map/ppermute | solution.py:12
  321.1 1.3 fusion.12
  (446 shorter events, 90.3 us)
Async XLA Ops:
  0.6 48.4 %copy-start = (f32[1,128,2048]{2,1,0:T(8,128)S(1)}, f32[1,128,2048]{2,1,0:T(8,128)}, u32[]{:S(2)}) copy-start(f32[1,128,2048]{2,1,0:T(8,128)} %param.37) | copy-start | bytes 3145732
  0.6 10.4 %copy-start.1 = (f32[3,8,16,512]{3,2,1,0:T(8,128)S(1)}, f32[3,8,16,512]{3,2,1,0:T(8,128)}, u32[]{:S(2)}) copy-start(f32[3,8,16,512]{3,2,1,0:T(8,128)} %param.31) | copy-start | bytes 2359300
  6.1 28.5 %copy-start.79 = (s32[128]{0:T(128)}, s32[128]{0:T(128)S(1)}, u32[]{:S(2)}) copy-start(s32[128]{0:T(128)S(1)} %get-tuple-element.170) | copy-start | bytes 1540
  7.4 40.4 %collective-permute-start.2 = (f32[2048]{0:T(1024)S(1)}, f32[2048]{0:T(1024)S(1)}, u32[]{:S(2)}, u32[]{:S(2)}) collective-permute-start(f32[2048]{0:T(1024)S(1)} %scatter_custom_fusion.1), channel_id=1, source_target_pairs={{0,16},{16,32},{32,48},{48,64},{64,80},{80,96},{96,112},{112,128},... | collective-permute-start | bytes 24584 | tf_op jit(solution)/shard_map/ppermute | solution.py:12
  11.1 5.8 %copy-start.106 = (s32[1,64]{1,0:T(1,128)S(1)}, s32[1,64]{1,0:T(1,128)}, u32[]{:S(2)}) copy-start(s32[1,64]{1,0:T(1,128)} %param.34) | copy-start | bytes 772
  11.2 5.8 %copy-start.107 = (s32[1,64]{1,0:T(1,128)S(1)}, s32[1,64]{1,0:T(1,128)}, u32[]{:S(2)}) copy-start(s32[1,64]{1,0:T(1,128)} %param.35) | copy-start | bytes 772
  11.2 26.6 %collective-permute-start.1 = (f32[2,8,512]{2,0,1:T(2,128)S(1)}, f32[2,8,512]{2,0,1:T(2,128)S(1)}, u32[]{:S(2)}, u32[]{:S(2)}) collective-permute-start(f32[2,8,512]{2,0,1:T(2,128)S(1)} %bitcast.541), channel_id=1, source_target_pairs={{0,1},{1,2},{2,3},{3,4},{4,5},{5,6},{6,7},{7,8},{8,9},{9,10},{10,1... | collective-permute-start | bytes 98312 | tf_op jit(solution)/shard_map/ppermute | solution.py:12
  14.7 23.1 %collective-permute-start = (f32[2,16,512]{2,1,0:T(8,128)S(1)}, f32[2,16,512]{2,1,0:T(8,128)S(1)}, u32[]{:S(2)}, u32[]{:S(2)}) collective-permute-start(f32[2,16,512]{2,1,0:T(8,128)S(1)} %slice_bitcast_fusion.43), channel_id=1, source_target_pairs={{0,16},{16,32},{32,48},{48,64},{64,80},{80,96},{96,112},{112,128},... | collective-permute-start | bytes 196616 | tf_op jit(solution)/shard_map/ppermute | solution.py:12
  17.0 18.2 %copy-start.80 = (s32[64]{0:T(128)}, s32[64]{0:T(128)S(1)}, u32[]{:S(2)}) copy-start(s32[64]{0:T(128)S(1)} %get-tuple-element.169) | copy-start | bytes 772
  17.0 57.1 %copy-start.51 = (s32[1024]{0:T(1024)}, s32[1024]{0:T(1024)S(1)}, u32[]{:S(2)}) copy-start(s32[1024]{0:T(1024)S(1)} %pad_clamp_fusion.3) | copy-start | bytes 12292
  20.5 26.3 %all-to-all-start = ((f32[16,1,2048]{2,1,0:T(1,128)}), f32[16,1,2048]{2,1,0:T(1,128)}, u32[]{:S(2)}, u32[]{:S(2)}) async-start(f32[16,1,2048]{2,1,0:T(1,128)} %broadcast_in_dim.33), calls=%async_computation | async-start | bytes 262144 | tf_op jit(solution)/shard_map/all_to_all | solution.py:17
  35.2 37.1 %copy-start.53 = (s32[1024]{0:T(1024)}, s32[1024]{0:T(1024)S(1)}, u32[]{:S(2)}) copy-start(s32[1024]{0:T(1024)S(1)} %pad_clamp_fusion.2) | copy-start | bytes 12292
  36.0 11.8 %copy-start.43 = (s32[128]{0:T(128)}, s32[128]{0:T(128)S(1)}, u32[]{:S(2)}) copy-start(s32[128]{0:T(128)S(1)} %fusion.76) | copy-start | bytes 1540
  36.0 41.3 %copy-start.52 = (s32[1024]{0:T(1024)}, s32[1024]{0:T(1024)S(1)}, u32[]{:S(2)}) copy-start(s32[1024]{0:T(1024)S(1)} %pad_clamp_fusion.1) | copy-start | bytes 12292
  37.8 35.3 %copy-start.48 = (f32[64]{0:T(128)}, f32[64]{0:T(128)S(1)}, u32[]{:S(2)}) copy-start(f32[64]{0:T(128)S(1)} %gather_fusion) | copy-start | bytes 772
  49.1 8.0 %copy-start.27 = (f32[8,16,512]{2,1,0:T(8,128)S(1)}, f32[8,16,512]{2,1,0:T(8,128)}, u32[]{:S(2)}) copy-start(f32[8,16,512]{2,1,0:T(8,128)} %param.32) | copy-start | bytes 786436
  50.6 17.7 %all-to-all-start.1 = ((f32[16,1,128]{2,1,0:T(1,128)}), f32[16,1,128]{2,1,0:T(1,128)S(1)}, u32[]{:S(2)}, u32[]{:S(2)}) async-start(f32[16,1,128]{2,1,0:T(1,128)} %broadcast_in_dim.34), calls=%async_computation.1 | async-start | bytes 16384 | tf_op jit(solution)/shard_map/all_to_all | solution.py:17
  68.3 20.6 %collective-permute-start.8 = (f32[2048]{0:T(1024)S(1)}, f32[2048]{0:T(1024)S(1)}, u32[]{:S(2)}, u32[]{:S(2)}) collective-permute-start(f32[2048]{0:T(1024)S(1)} %bitcast.499), channel_id=1, source_target_pairs={{16,0},{32,16},{48,32},{64,48},{80,64},{96,80},{112,96},{128,112},... | collective-permute-start | bytes 24584 | tf_op jit(solution)/shard_map/ppermute | solution.py:12
  75.0 29.1 %copy-start.2 = (f32[3,8,16,512]{3,2,1,0:T(8,128)}, f32[3,8,16,512]{3,2,1,0:T(8,128)S(1)}, u32[]{:S(2)}) copy-start(f32[3,8,16,512]{3,2,1,0:T(8,128)S(1)} %constant_dynamic-update-slice_fusion.3) | copy-start | bytes 2359300
  80.9 34.7 %all-to-all-start.2 = ((f32[16,1,2048]{2,1,0:T(1,128)}), f32[16,1,2048]{2,1,0:T(1,128)}, u32[]{:S(2)}, u32[]{:S(2)}) async-start(f32[16,1,2048]{2,1,0:T(1,128)} %broadcast_in_dim.35), calls=%async_computation.2 | async-start | bytes 262144 | tf_op jit(solution)/shard_map/all_to_all | solution.py:17
  85.6 4.6 %copy-start.77 = (f32[128]{0:T(128)S(1)}, f32[128]{0:T(128)}, u32[]{:S(2)}) copy-start(f32[128]{0:T(128)} %copy-done.76) | copy-start | bytes 1540
  85.6 4.6 %copy-start.88 = (pred[1,128]{1,0:T(4,128)(4,1)S(1)}, pred[1,128]{1,0:T(4,128)(4,1)}, u32[]{:S(2)}) copy-start(pred[1,128]{1,0:T(4,128)(4,1)} %copy-done.87) | copy-start | bytes 388
  85.6 4.6 %copy-start.102 = (f32[128]{0:T(128)S(1)}, f32[128]{0:T(128)}, u32[]{:S(2)}) copy-start(f32[128]{0:T(128)} %copy-done.101) | copy-start | bytes 1540
  85.6 4.6 %copy-start.104 = (f32[128]{0:T(128)S(1)}, f32[128]{0:T(128)}, u32[]{:S(2)}) copy-start(f32[128]{0:T(128)} %gather_fusion.4) | copy-start | bytes 1540
  85.7 15.6 %collective-permute-start.4 = (f32[2,8,512]{2,1,0:T(8,128)}, f32[2,8,512]{2,1,0:T(8,128)}, u32[]{:S(2)}, u32[]{:S(2)}) collective-permute-start(f32[2,8,512]{2,1,0:T(8,128)} %bitcast.477), channel_id=1, source_target_pairs={{1,0},{2,1},{3,2},{4,3},{5,4},{6,5},{7,6},{8,7},{9,8},{10,9},{11,1... | collective-permute-start | bytes 98312 | tf_op jit(solution)/shard_map/ppermute | solution.py:12
  87.0 15.1 %collective-permute-start.3 = (f32[2,16,512]{2,1,0:T(8,128)S(1)}, f32[2,16,512]{2,1,0:T(8,128)}, u32[]{:S(2)}, u32[]{:S(2)}) collective-permute-start(f32[2,16,512]{2,1,0:T(8,128)S(1)} %slice_bitcast_fusion.42), channel_id=1, source_target_pairs={{16,0},{32,16},{48,32},{64,48},{80,64},{96,80},{112,96},{128,112},... | collective-permute-start | bytes 196616 | tf_op jit(solution)/shard_map/ppermute | solution.py:12
  95.3 7.5 %copy-start.37 = (f32[1,8,15,512]{3,2,1,0:T(8,128)S(1)}, f32[1,8,15,512]{3,2,1,0:T(8,128)}, u32[]{:S(2)}) copy-start(f32[1,8,15,512]{3,2,1,0:T(8,128)} %slice_bitcast_fusion.12) | copy-start | bytes 737284
  95.4 21.2 %collective-permute-start.7 = (f32[2048]{0:T(1024)S(1)}, f32[2048]{0:T(1024)S(1)}, u32[]{:S(2)}, u32[]{:S(2)}) collective-permute-start(f32[2048]{0:T(1024)S(1)} %scatter_custom_fusion.5), channel_id=1, source_target_pairs={{0,16},{16,32},{32,48},{48,64},{64,80},{80,96},{96,112},{112,128},... | collective-permute-start | bytes 24584 | tf_op jit(solution)/shard_map/ppermute | solution.py:12
  106.1 6.2 %collective-permute-start.6 = (f32[2,8,512]{2,0,1:T(2,128)S(1)}, f32[2,8,512]{2,0,1:T(2,128)S(1)}, u32[]{:S(2)}, u32[]{:S(2)}) collective-permute-start(f32[2,8,512]{2,0,1:T(2,128)S(1)} %bitcast.542), channel_id=1, source_target_pairs={{0,1},{1,2},{2,3},{3,4},{4,5},{5,6},{6,7},{7,8},{8,9},{9,10},{10,1... | collective-permute-start | bytes 98312 | tf_op jit(solution)/shard_map/ppermute | solution.py:12
  110.2 3.5 %collective-permute-start.5 = (f32[2,16,512]{2,1,0:T(8,128)S(1)}, f32[2,16,512]{2,1,0:T(8,128)S(1)}, u32[]{:S(2)}, u32[]{:S(2)}) collective-permute-start(f32[2,16,512]{2,1,0:T(8,128)S(1)} %slice_bitcast_fusion.41), channel_id=1, source_target_pairs={{0,16},{16,32},{32,48},{48,64},{64,80},{80,96},{96,112},{112,128},... | collective-permute-start | bytes 196616 | tf_op jit(solution)/shard_map/ppermute | solution.py:12
  118.7 12.9 %copy-start.3 = (f32[3,8,16,512]{3,2,1,0:T(8,128)S(1)}, f32[3,8,16,512]{3,2,1,0:T(8,128)}, u32[]{:S(2)}) copy-start(f32[3,8,16,512]{3,2,1,0:T(8,128)} %copy-done.2) | copy-start | bytes 2359300
  120.2 22.6 %all-to-all-start.3 = ((f32[16,1,128]{2,1,0:T(1,128)}), f32[16,1,128]{2,1,0:T(1,128)S(1)}, u32[]{:S(2)}, u32[]{:S(2)}) async-start(f32[16,1,128]{2,1,0:T(1,128)} %broadcast_in_dim.36), calls=%async_computation.3 | async-start | bytes 16384 | tf_op jit(solution)/shard_map/all_to_all | solution.py:17
  143.8 18.9 %collective-permute-start.14 = (f32[2048]{0:T(1024)S(1)}, f32[2048]{0:T(1024)S(1)}, u32[]{:S(2)}, u32[]{:S(2)}) collective-permute-start(f32[2048]{0:T(1024)S(1)} %bitcast.497), channel_id=1, source_target_pairs={{16,0},{32,16},{48,32},{64,48},{80,64},{96,80},{112,96},{128,112},... | collective-permute-start | bytes 24584 | tf_op jit(solution)/shard_map/ppermute | solution.py:12
  154.7 37.3 %all-to-all-start.4 = ((f32[16,1,2048]{2,1,0:T(1,128)}), f32[16,1,2048]{2,1,0:T(1,128)}, u32[]{:S(2)}, u32[]{:S(2)}) async-start(f32[16,1,2048]{2,1,0:T(1,128)} %broadcast_in_dim.37), calls=%async_computation.4 | async-start | bytes 262144 | tf_op jit(solution)/shard_map/all_to_all | solution.py:17
  159.5 4.6 %copy-start.73 = (f32[128]{0:T(128)S(1)}, f32[128]{0:T(128)}, u32[]{:S(2)}) copy-start(f32[128]{0:T(128)} %copy-done.72) | copy-start | bytes 1540
  159.5 4.6 %copy-start.84 = (pred[1,128]{1,0:T(4,128)(4,1)S(1)}, pred[1,128]{1,0:T(4,128)(4,1)}, u32[]{:S(2)}) copy-start(pred[1,128]{1,0:T(4,128)(4,1)} %copy-done.83) | copy-start | bytes 388
  159.5 4.6 %copy-start.98 = (f32[128]{0:T(128)S(1)}, f32[128]{0:T(128)}, u32[]{:S(2)}) copy-start(f32[128]{0:T(128)} %copy-done.97) | copy-start | bytes 1540
  159.5 4.6 %copy-start.103 = (f32[128]{0:T(128)S(1)}, f32[128]{0:T(128)}, u32[]{:S(2)}) copy-start(f32[128]{0:T(128)} %gather_fusion.8) | copy-start | bytes 1540
  159.6 17.8 %collective-permute-start.10 = (f32[2,8,512]{2,1,0:T(8,128)}, f32[2,8,512]{2,1,0:T(8,128)}, u32[]{:S(2)}, u32[]{:S(2)}) collective-permute-start(f32[2,8,512]{2,1,0:T(8,128)} %bitcast.476), channel_id=1, source_target_pairs={{1,0},{2,1},{3,2},{4,3},{5,4},{6,5},{7,6},{8,7},{9,8},{10,9},{11,1... | collective-permute-start | bytes 98312 | tf_op jit(solution)/shard_map/ppermute | solution.py:12
  160.9 17.3 %collective-permute-start.9 = (f32[2,16,512]{2,1,0:T(8,128)S(1)}, f32[2,16,512]{2,1,0:T(8,128)}, u32[]{:S(2)}, u32[]{:S(2)}) collective-permute-start(f32[2,16,512]{2,1,0:T(8,128)S(1)} %slice_bitcast_fusion.40), channel_id=1, source_target_pairs={{16,0},{32,16},{48,32},{64,48},{80,64},{96,80},{112,96},{128,112},... | collective-permute-start | bytes 196616 | tf_op jit(solution)/shard_map/ppermute | solution.py:12
  170.6 8.3 %copy-start.42 = (f32[1,7,16,512]{3,2,1,0:T(8,128)S(1)}, f32[1,7,16,512]{3,2,1,0:T(8,128)}, u32[]{:S(2)}) copy-start(f32[1,7,16,512]{3,2,1,0:T(8,128)} %get-tuple-element.95) | copy-start | bytes 688132
  170.7 22.4 %collective-permute-start.13 = (f32[2048]{0:T(1024)}, f32[2048]{0:T(1024)}, u32[]{:S(2)}, u32[]{:S(2)}) collective-permute-start(f32[2048]{0:T(1024)} %scatter_custom_fusion.9), channel_id=1, source_target_pairs={{0,16},{16,32},{32,48},{48,64},{64,80},{80,96},{96,112},{112,128},... | collective-permute-start | bytes 24584 | tf_op jit(solution)/shard_map/ppermute | solution.py:12
  181.8 7.0 %collective-permute-start.12 = (f32[2,8,512]{2,0,1:T(2,128)S(1)}, f32[2,8,512]{2,0,1:T(2,128)S(1)}, u32[]{:S(2)}, u32[]{:S(2)}) collective-permute-start(f32[2,8,512]{2,0,1:T(2,128)S(1)} %bitcast.543), channel_id=1, source_target_pairs={{0,1},{1,2},{2,3},{3,4},{4,5},{5,6},{6,7},{7,8},{8,9},{9,10},{10,1... | collective-permute-start | bytes 98312 | tf_op jit(solution)/shard_map/ppermute | solution.py:12
  186.1 4.0 %collective-permute-start.11 = (f32[2,16,512]{2,1,0:T(8,128)S(1)}, f32[2,16,512]{2,1,0:T(8,128)S(1)}, u32[]{:S(2)}, u32[]{:S(2)}) collective-permute-start(f32[2,16,512]{2,1,0:T(8,128)S(1)} %slice_bitcast_fusion.39), channel_id=1, source_target_pairs={{0,16},{16,32},{32,48},{48,64},{64,80},{80,96},{96,112},{112,128},... | collective-permute-start | bytes 196616 | tf_op jit(solution)/shard_map/ppermute | solution.py:12
  196.5 23.0 %all-to-all-start.5 = ((f32[16,1,128]{2,1,0:T(1,128)}), f32[16,1,128]{2,1,0:T(1,128)S(1)}, u32[]{:S(2)}, u32[]{:S(2)}) async-start(f32[16,1,128]{2,1,0:T(1,128)} %broadcast_in_dim.38), calls=%async_computation.5 | async-start | bytes 16384 | tf_op jit(solution)/shard_map/all_to_all | solution.py:17
  220.5 19.4 %collective-permute-start.20 = (f32[2048]{0:T(1024)S(1)}, f32[2048]{0:T(1024)S(1)}, u32[]{:S(2)}, u32[]{:S(2)}) collective-permute-start(f32[2048]{0:T(1024)S(1)} %bitcast.494), channel_id=1, source_target_pairs={{16,0},{32,16},{48,32},{64,48},{80,64},{96,80},{112,96},{128,112},... | collective-permute-start | bytes 24584 | tf_op jit(solution)/shard_map/ppermute | solution.py:12
  231.5 38.6 %all-to-all-start.6 = ((f32[16,1,2048]{2,1,0:T(1,128)}), f32[16,1,2048]{2,1,0:T(1,128)}, u32[]{:S(2)}, u32[]{:S(2)}) async-start(f32[16,1,2048]{2,1,0:T(1,128)} %broadcast_in_dim.39), calls=%async_computation.6 | async-start | bytes 262144 | tf_op jit(solution)/shard_map/all_to_all | solution.py:17
  236.4 4.9 %copy-start.65 = (f32[1,128]{1,0:T(1,128)S(1)}, f32[1,128]{1,0:T(1,128)}, u32[]{:S(2)}) copy-start(f32[1,128]{1,0:T(1,128)} %param.41) | copy-start | bytes 1540
  236.4 4.9 %copy-start.71 = (f32[128]{0:T(128)S(1)}, f32[128]{0:T(128)}, u32[]{:S(2)}) copy-start(f32[128]{0:T(128)} %copy-done.70) | copy-start | bytes 1540
  236.4 4.9 %copy-start.82 = (pred[1,128]{1,0:T(4,128)(4,1)S(1)}, pred[1,128]{1,0:T(4,128)(4,1)}, u32[]{:S(2)}) copy-start(pred[1,128]{1,0:T(4,128)(4,1)} %copy-done.81) | copy-start | bytes 388
  236.4 4.9 %copy-start.96 = (f32[128]{0:T(128)S(1)}, f32[128]{0:T(128)}, u32[]{:S(2)}) copy-start(f32[128]{0:T(128)} %copy-done.95) | copy-start | bytes 1540
  236.4 18.4 %collective-permute-start.16 = (f32[2,8,512]{2,0,1:T(2,128)}, f32[2,8,512]{2,0,1:T(2,128)S(1)}, u32[]{:S(2)}, u32[]{:S(2)}) collective-permute-start(f32[2,8,512]{2,0,1:T(2,128)} %bitcast.480), channel_id=1, source_target_pairs={{1,0},{2,1},{3,2},{4,3},{5,4},{6,5},{7,6},{8,7},{9,8},{10,9},{11,1... | collective-permute-start | bytes 98312 | tf_op jit(solution)/shard_map/ppermute | solution.py:12
  237.8 17.0 %collective-permute-start.15 = (f32[2,16,512]{2,1,0:T(8,128)S(1)}, f32[2,16,512]{2,1,0:T(8,128)}, u32[]{:S(2)}, u32[]{:S(2)}) collective-permute-start(f32[2,16,512]{2,1,0:T(8,128)S(1)} %slice_bitcast_fusion.38), channel_id=1, source_target_pairs={{16,0},{32,16},{48,32},{64,48},{80,64},{96,80},{112,96},{128,112},... | collective-permute-start | bytes 196616 | tf_op jit(solution)/shard_map/ppermute | solution.py:12
  247.7 23.4 %collective-permute-start.19 = (f32[2048]{0:T(1024)S(1)}, f32[2048]{0:T(1024)S(1)}, u32[]{:S(2)}, u32[]{:S(2)}) collective-permute-start(f32[2048]{0:T(1024)S(1)} %scatter_custom_fusion.13), channel_id=1, source_target_pairs={{0,16},{16,32},{32,48},{48,64},{64,80},{80,96},{96,112},{112,128},... | collective-permute-start | bytes 24584 | tf_op jit(solution)/shard_map/ppermute | solution.py:12
  259.9 7.0 %collective-permute-start.18 = (f32[2,8,512]{2,0,1:T(2,128)S(1)}, f32[2,8,512]{2,0,1:T(2,128)S(1)}, u32[]{:S(2)}, u32[]{:S(2)}) collective-permute-start(f32[2,8,512]{2,0,1:T(2,128)S(1)} %bitcast.544), channel_id=1, source_target_pairs={{0,1},{1,2},{2,3},{3,4},{4,5},{5,6},{6,7},{7,8},{8,9},{9,10},{10,1... | collective-permute-start | bytes 98312 | tf_op jit(solution)/shard_map/ppermute | solution.py:12
  264.2 4.0 %collective-permute-start.17 = (f32[2,16,512]{2,1,0:T(8,128)S(1)}, f32[2,16,512]{2,1,0:T(8,128)S(1)}, u32[]{:S(2)}, u32[]{:S(2)}) collective-permute-start(f32[2,16,512]{2,1,0:T(8,128)S(1)} %slice_bitcast_fusion.37), channel_id=1, source_target_pairs={{0,16},{16,32},{32,48},{48,64},{64,80},{80,96},{96,112},{112,128},... | collective-permute-start | bytes 196616 | tf_op jit(solution)/shard_map/ppermute | solution.py:12
  274.4 23.0 %all-to-all-start.7 = ((f32[16,1,128]{2,1,0:T(1,128)}), f32[16,1,128]{2,1,0:T(1,128)S(1)}, u32[]{:S(2)}, u32[]{:S(2)}) async-start(f32[16,1,128]{2,1,0:T(1,128)} %broadcast_in_dim.40), calls=%async_computation.7 | async-start | bytes 16384 | tf_op jit(solution)/shard_map/all_to_all | solution.py:17
  298.4 10.9 %collective-permute-start.23 = (f32[2048]{0:T(1024)S(1)}, f32[2048]{0:T(1024)S(1)}, u32[]{:S(2)}, u32[]{:S(2)}) collective-permute-start(f32[2048]{0:T(1024)S(1)} %bitcast.503), channel_id=1, source_target_pairs={{16,0},{32,16},{48,32},{64,48},{80,64},{96,80},{112,96},{128,112},... | collective-permute-start | bytes 24584 | tf_op jit(solution)/shard_map/ppermute | solution.py:12
  302.2 16.4 %copy-start.4 = (f32[3,8,16,512]{3,2,1,0:T(8,128)}, f32[3,8,16,512]{3,2,1,0:T(8,128)S(1)}, u32[]{:S(2)}) copy-start(f32[3,8,16,512]{3,2,1,0:T(8,128)S(1)} %constant_dynamic-update-slice_fusion) | copy-start | bytes 2359300
  306.0 4.6 %copy-start.75 = (f32[128]{0:T(128)S(1)}, f32[128]{0:T(128)}, u32[]{:S(2)}) copy-start(f32[128]{0:T(128)} %copy-done.74) | copy-start | bytes 1540
  306.0 4.7 %copy-start.86 = (pred[1,128]{1,0:T(4,128)(4,1)S(1)}, pred[1,128]{1,0:T(4,128)(4,1)}, u32[]{:S(2)}) copy-start(pred[1,128]{1,0:T(4,128)(4,1)} %copy-done.85) | copy-start | bytes 388
  306.0 4.7 %copy-start.100 = (f32[128]{0:T(128)S(1)}, f32[128]{0:T(128)}, u32[]{:S(2)}) copy-start(f32[128]{0:T(128)} %copy-done.99) | copy-start | bytes 1540
  306.0 5.3 %collective-permute-start.22 = (f32[2,8,512]{2,0,1:T(2,128)}, f32[2,8,512]{2,0,1:T(2,128)S(1)}, u32[]{:S(2)}, u32[]{:S(2)}) collective-permute-start(f32[2,8,512]{2,0,1:T(2,128)} %bitcast.478), channel_id=1, source_target_pairs={{1,0},{2,1},{3,2},{4,3},{5,4},{6,5},{7,6},{8,7},{9,8},{10,9},{11,1... | collective-permute-start | bytes 98312 | tf_op jit(solution)/shard_map/ppermute | solution.py:12
  307.4 9.1 %collective-permute-start.21 = (f32[2,16,512]{2,1,0:T(8,128)S(1)}, f32[2,16,512]{2,1,0:T(8,128)}, u32[]{:S(2)}, u32[]{:S(2)}) collective-permute-start(f32[2,16,512]{2,1,0:T(8,128)S(1)} %slice_bitcast_fusion.36), channel_id=1, source_target_pairs={{16,0},{32,16},{48,32},{64,48},{80,64},{96,80},{112,96},{128,112},... | collective-permute-start | bytes 196616 | tf_op jit(solution)/shard_map/ppermute | solution.py:12
  (78 other events, 106.8 us)
where the time goes:
time: 326 us; the launch traced here: 322 us
  starting transfers between devices  142 us (44%)
  local copies, waits for them, and re-layouts  71.8 us (22%)
  waiting for transfers between devices  55.1 us (17%)
  other arithmetic  46.9 us (14%)
  matrix products  3.64 us (1%)
    ppermute x24, starting transfers between devices, shifted(): return lax.ppermute(value, axis, pairs)  74.5 us
    all_to_all x8, starting transfers between devices, copy_for_each(): lax.all_to_all(jnp.broadcast_to(value[None], (devices, *value.shape)), ax...  67.5 us
    all_to_all x8, waiting for transfers between devices, copy_for_each(): lax.all_to_all(jnp.broadcast_to(value[None], (devices, *value.shape)), ax...  46 us
    unnamed x231, local copies, waits for them, and re-layouts  20.9 us
    ppermute x24, waiting for transfers between devices, shifted(): return lax.ppermute(value, axis, pairs)  9.08 us
  transfers between devices with their start and end apart: 32, of which 9 were waited for; matrix products, arithmetic and copies ran while one was open for 25% of the time, Pallas kernels for 0%

commit v1 on v0

v1 whole, which is shorter than its diff:
```python
import functools

import jax
import jax.numpy as jnp
from jax import lax
from jax.experimental import pallas as pl
from jax.experimental.pallas import tpu as pltpu
from jax.sharding import PartitionSpec as P

STEPS = 4
F32 = jnp.float32
BF16 = jnp.bfloat16
NZ = 8
NX = 16
NY = 512
GX = 24
NF = 32
NB = 16
HALF = 64
LANES = 128
DEPTH = 6
VMEM = pl.BlockSpec(memory_space=pltpu.VMEM)
NT = (((1,), (1,)), ((), ()))


def call(kernel, outs, *args, alias=None, name=None):
    return pl.pallas_call(
        kernel,
        out_shape=[jax.ShapeDtypeStruct(s, d) for s, d in outs],
        in_specs=[VMEM] * len(args),
        out_specs=[VMEM] * len(outs),
        input_output_aliases=alias or {},
        name=name,
        compiler_params=pltpu.CompilerParams(vmem_limit_bytes=40 << 20),
    )(*args)


def shifted(value, axis, by):
    devices = lax.axis_size(axis)
    pairs = [(i, i + by) for i in range(devices) if 0 <= i + by < devices]
    return lax.ppermute(value, axis, pairs)


def exchanged(value):
    return lax.all_to_all(value, "fxy", 0, 0, tiled=True)


def iota(shape, dim):
    return lax.broadcasted_iota(jnp.int32, shape, dim)


def split3(value):
    high = value.astype(BF16)
    rest = value - high.astype(F32)
    middle = rest.astype(BF16)
    low = (rest - middle.astype(F32)).astype(BF16)
    return high, middle, low


def dot3(value, onehot, dims=(((1,), (0,)), ((), ()))):
    rows = value.shape[0]
    parts = jnp.concatenate(split3(value), 0)
    product = lax.dot_general(parts, onehot, dims, preferred_element_type=F32)
    return product[:rows] + (product[rows : 2 * rows] + product[2 * rows :])


def next_y(f):
    rolled = pltpu.roll(f, NY - 1, 1)
    return jnp.where(iota(f.shape, 1) == NY - 1, 0.0, rolled)


def last_y(f):
    rolled = pltpu.roll(f, 1, 1)
    return jnp.where(iota(f.shape, 1) == 0, 0.0, rolled)


def next_x(f):
    return jnp.concatenate([f[1:], f[:1]], 0)


def last_x(f):
    return jnp.concatenate([f[GX - 1 :], f[: GX - 1]], 0)


def column():
    return lax.axis_index("fxy")


def row():
    return lax.axis_index("fz")


def half_mask():
    lane = iota((1, LANES), 1)
    return (lane // HALF == column() // 8).astype(F32)


def own_onehots(cell):
    mine = half_mask() > 0.5
    rows = iota((NZ * NX, LANES), 0) == cell // NY
    at_row = jnp.where(rows & mine, 1.0, 0.0).astype(BF16)
    at_y = jnp.where(iota((NY, LANES), 0) == cell % NY, 1.0, 0.0).astype(BF16)
    return at_row, at_y


def at_ports(field, at_row, at_y):
    picked = dot3(field, at_y)
    return jnp.sum(picked * at_row.astype(F32), 0, keepdims=True)


def hist_at(hist, position):
    out = jnp.zeros((1, LANES), F32)
    for k in range(DEPTH + STEPS):
        out = jnp.where(position == k, hist[k : k + 1], out)
    return out


def k_first(e_ref, h_ref, g_ref, cell_ref, node_ref, cond_ref, far_ref, delay_ref, imped_ref, near_hist_ref, pay_ref, up_ref, right_ref):
    def packed(ref):
        value = ref[...].astype(F32)
        return jnp.concatenate([value, value], 1) * half_mask()

    cell = packed(cell_ref)
    at_row, at_y = own_onehots(cell.astype(jnp.int32))
    ez = at_ports(e_ref[2].reshape(NZ * NX, NY), at_row, at_y)
    gain = at_ports(g_ref[...].reshape(NZ * NX, NY), at_row, at_y)
    rows = [packed(node_ref), cell, packed(cond_ref), ez, gain, jnp.zeros((3, LANES), F32)]
    pay_ref[...] = jnp.broadcast_to(jnp.concatenate(rows, 0)[None], (NB, 8, LANES))
    up_ref[0:NX] = h_ref[0, NZ - 1]
    up_ref[NX : 2 * NX] = h_ref[1, NZ - 1]
    static = [far_ref[...].astype(F32), delay_ref[...].astype(F32), imped_ref[...], jnp.zeros((5, LANES), F32)]
    hist = [near_hist_ref[0], jnp.zeros((2, LANES), F32)]
    up_ref[2 * NX :, 0:LANES] = jnp.concatenate(static, 0)
    up_ref[2 * NX :, LANES : 2 * LANES] = jnp.concatenate(hist, 0)
    up_ref[2 * NX :, 2 * LANES :] = jnp.zeros((8, NY - 2 * LANES), F32)
    for c in range(2):
        for z in range(NZ):
            right_ref[c * NZ + z : c * NZ + z + 1] = h_ref[1 + c, z, NX - 1 : NX]


def curl_z(h_ref, z):
    hx, hy = h_ref[0, z + 1], h_ref[1, z + 1]
    return ((hy - last_x(hy)) - (hx - last_y(hx)))[:NX]


def update_exy(old_ref, e_ref, h_ref, d_ref, g_ref, base):
    for z in range(NZ):
        hz = h_ref[2, z + 1]
        own = hz[:NX]
        curl_x = (own - last_y(own)) - (h_ref[1, z + 1, :NX] - h_ref[1, z, :NX])
        curl_y = (h_ref[0, z + 1, :NX] - h_ref[0, z, :NX]) - (hz - last_x(hz))[:NX]
        d, g = d_ref[z], g_ref[z]
        e_ref[0, z + 1, :NX] = d * old_ref[0, z + base, :NX] + g * curl_x
        e_ref[1, z + 1, :NX] = d * old_ref[1, z + base, :NX] + g * curl_y


def update_ez(old_ref, e_ref, h_ref, d_ref, g_ref, base):
    for z in range(NZ):
        e_ref[2, z + 1, :NX] = d_ref[z] * old_ref[2, z + base, :NX] + g_ref[z] * curl_z(h_ref, z)


def send_x(e_ref, right_ref, left_ref):
    for z in range(NZ):
        for c in range(3):
            right_ref[c * NZ + z : c * NZ + z + 1] = e_ref[c, z + 1, NX - 1 : NX]
        for c in range(2):
            left_ref[c * NZ + z : c * NZ + z + 1] = e_ref[1 + c, z + 1, 0:1]


def k_start(e_in, h_in, d_ref, g_ref, cell_ref, up_ref, right_ref, e_ref, h_ref, pre_ref, xr_ref, xl_ref):
    first = iota((8, NY), 0)
    for z in range(NZ):
        for c in range(3):
            h_ref[c, z + 1, :NX] = h_in[c, z]
            if c:
                ghost = right_ref[(c - 1) * NZ + z : (c - 1) * NZ + z + 1]
                h_ref[c, z + 1, NX:] = jnp.where(first == 7, ghost, 0.0)
            else:
                h_ref[c, z + 1, NX:] = jnp.zeros((8, NY), F32)
    for c in range(3):
        h_ref[c, 0] = jnp.zeros((GX, NY), F32)
        e_ref[c, 0] = jnp.zeros((GX, NY), F32)
        e_ref[c, NZ + 1] = jnp.zeros((GX, NY), F32)
    h_ref[0, 0, :NX] = up_ref[0:NX]
    h_ref[1, 0, :NX] = up_ref[NX : 2 * NX]
    update_ez(e_in, e_ref, h_ref, d_ref, g_ref, 0)
    update_exy(e_in, e_ref, h_ref, d_ref, g_ref, 0)
    cell = cell_ref[...]
    at_row, at_y = own_onehots(jnp.concatenate([cell, cell], 1))
    pre = at_ports(e_ref[2, 1 : NZ + 1, :NX].reshape(NZ * NX, NY), at_row, at_y)
    pre_ref[...] = jnp.broadcast_to(pre, (8, LANES))
    send_x(e_ref, xr_ref, xl_ref)


def own_volts(w, lines, node, inverse_ref, onehot_ref):
    high = node // LANES
    sources = jnp.zeros((NB, LANES), F32)
    values = jnp.concatenate([w, lines], 0)
    for t in range(10):
        spread = jnp.where(iota((NB, LANES), 0) == high[t : t + 1], values[t : t + 1], 0.0)
        sources = sources + dot3(spread, onehot_ref[t], NT)
    total = jnp.zeros((LANES, LANES), F32)
    for t in range(NB):
        total = total + inverse_ref[0, :, t * LANES : (t + 1) * LANES] * sources[t : t + 1]
    return jnp.sum(total.T, 0, keepdims=True)


def node_values(volts, node, onehot_ref):
    high = node // LANES
    rows = []
    for t in range(10):
        picked = dot3(volts, onehot_ref[t])
        rows.append(jnp.sum(jnp.where(iota((NB, LANES), 0) == high[t : t + 1], picked, 0.0), 0, keepdims=True))
    return jnp.concatenate(rows, 0)


def line_inputs(static, hist, n):
    own = n - static[4:5].astype(jnp.int32) + DEPTH
    below = n - static[5:6].astype(jnp.int32) + DEPTH
    return hist_at(hist[16:32], own), hist_at(hist[32:48], below), hist_at(hist[0:16], own)


def payload(pay_ref, volts, pre):
    rows = jnp.concatenate([volts, pre, jnp.zeros((6, LANES), F32)], 0)
    pay_ref[...] = jnp.broadcast_to(rows[None], (NB, 8, LANES))


def k_tables(
    got_ref, up_ref, near_ref, delay_ref, imped_ref, near_hist_ref, far_hist_ref, inverse_ref, pre_ref, pay_ref, port_ref, onehot_ref, static_ref, hist_ref
):
    def packed(f):
        return got_ref[0:8, f, :] + got_ref[8:16, f, :]

    far_below = up_ref[2 * NX : 2 * NX + 1, 0:LANES]
    delay_below = up_ref[2 * NX + 1 : 2 * NX + 2, 0:LANES]
    imped_below = jnp.where(row() == 0, 1.0, up_ref[2 * NX + 2 : 2 * NX + 3, 0:LANES])
    near = near_ref[...].astype(F32)
    node = jnp.concatenate([packed(0), near, far_below, jnp.zeros((6, LANES), F32)], 0)
    port_ref[0:16] = node
    device = iota((8, LANES), 0) + 8 * (iota((8, LANES), 1) // HALF)
    port_ref[16:24] = packed(1) + (device * (NZ * NX * NY)).astype(F32)
    port_ref[24:32] = packed(2)
    port_ref[32:40] = packed(4)
    static = jnp.concatenate([near, far_below, imped_ref[...], imped_below, delay_ref[...].astype(F32), delay_below, jnp.zeros((2, LANES), F32)], 0)
    static_ref[...] = static
    hist_ref[...] = jnp.zeros((48, LANES), F32)
    for k in range(DEPTH):
        hist_ref[k : k + 1] = near_hist_ref[0, DEPTH - 1 - k : DEPTH - k]
        hist_ref[16 + k : 17 + k] = far_hist_ref[0, DEPTH - 1 - k : DEPTH - k]
        hist_ref[32 + k : 33 + k] = up_ref[2 * NX + DEPTH - 1 - k : 2 * NX + DEPTH - k, LANES : 2 * LANES]
    nodes = node.astype(jnp.int32)
    for t in range(10):
        onehot_ref[t] = jnp.where(iota((LANES, LANES), 0) == nodes[t : t + 1] % LANES, 1.0, 0.0).astype(BF16)
    into_near, into_below, _ = line_inputs(static, hist_ref[...], 0)
    ez = packed(3)
    port_ref[40:48] = ez
    w = packed(2) * ez
    volts = own_volts(w, -jnp.concatenate([into_near, into_below], 0), nodes, inverse_ref, onehot_ref)
    payload(pay_ref, volts, pre_ref[0:1])


def k_cells(port_ref, at_row_ref, at_y_ref):
    j = column()
    lane_high = iota((1, LANES), 1) // HALF
    for k in range(3):
        block = j + (k - 1)
        packed_row = jnp.where(block < 0, block + 8, block % 8)
        where = port_ref[pl.ds(16 + packed_row, 1), :].astype(jnp.int32)
        cell = where % (NZ * NX * NY)
        inside = (lane_high == block // 8) & (block >= 0) & (block < NB)
        x = (cell // NY) % NX + (k - 1) * NX
        position = jnp.where((x >= 0) & (x <= NX), x, jnp.where(x == -1, GX - 1, -1))
        target = jnp.where(inside & (position >= 0), (cell // (NX * NY)) * GX + position, -1)
        at_row_ref[:, k * LANES : (k + 1) * LANES] = jnp.where(iota((NZ * GX, LANES), 0) == target, 1.0, 0.0).astype(BF16)
        at_y_ref[:, k * LANES : (k + 1) * LANES] = jnp.where(iota((NY, LANES), 0) == cell % NY, 1.0, 0.0).astype(BF16)


def k_currents(
    n, last, got_ref, port_ref, ez_ref, onehot_ref, static_ref, hist_ref, at_row_ref, at_y_ref, xr_ref, xl_ref, e_in, e_ref, ez_out, wave_ref, *sends
):
    volts = got_ref[:, 0, :]
    pre = got_ref[0:8, 1, :] + got_ref[8:16, 1, :]
    node = port_ref[0:16].astype(jnp.int32)
    at_nodes = node_values(volts, node, onehot_ref)
    where = port_ref[16:24]
    cond = port_ref[24:32]
    current = cond * (ez_ref[...] - at_nodes[0:8])
    shared = current
    for k in range(1, LANES):
        same = pltpu.roll(where, k, 1) == where
        shared = shared + jnp.where(same, pltpu.roll(current, k, 1), 0.0)
    gain = port_ref[32:40]
    ez_out[...] = pre - gain * shared

    static = static_ref[...]
    into_near, into_below, into_own = line_inputs(static, hist_ref[...], n)
    out_near = -2.0 * at_nodes[8:9] / static[2:3] - into_near
    out_below = -2.0 * at_nodes[9:10] / static[3:4] - into_below
    top = jnp.where(row() == NF - 1, -into_own, 0.0)
    wave_ref[...] = jnp.concatenate([out_near, top, jnp.zeros((6, LANES), F32)], 0)

    first = iota((8, NY), 0)
    for z in range(NZ):
        for c in range(3):
            ghost = jnp.where(first == 7, xr_ref[c * NZ + z : c * NZ + z + 1], 0.0)
            if c:
                ghost = jnp.where(first == 0, xl_ref[(c - 1) * NZ + z : (c - 1) * NZ + z + 1], ghost)
            e_ref[c, z + 1, NX:] = ghost
    j = column()
    drop = gain * current
    block_rows = []
    for k in range(3):
        block = j + (k - 1)
        packed_row = jnp.where(block < 0, block + 8, block % 8)
        mask = iota((8, LANES), 0) == packed_row
        block_rows.append(jnp.sum(jnp.where(mask, drop, 0.0), 0, keepdims=True))
    drops = jnp.concatenate(block_rows, 1)
    at_row = at_row_ref[...]
    parts = jnp.concatenate([at_row * part for part in split3(drops)], 0)
    spread = lax.dot_general(parts, at_y_ref[...], NT, preferred_element_type=F32)
    rows = NZ * GX
    spread = spread[:rows] + (spread[rows : 2 * rows] + spread[2 * rows :])
    for z in range(NZ):
        e_ref[2, z + 1] = e_ref[2, z + 1] - spread[z * GX : (z + 1) * GX]

    down_ref = sends[-1]
    down_ref[0:GX] = e_ref[0, 1]
    down_ref[GX : GX + NX] = e_ref[1, 1, :NX]
    down_ref[GX + NX :] = jnp.zeros((8, NY), F32)
    down_ref[GX + NX : GX + NX + 1, 0:LANES] = out_below
    if not last:
        up_ref = sends[0]
        up_ref[0:NX] = e_ref[0, NZ, :NX]
        up_ref[NX : 2 * NX] = e_ref[1, NZ, :NX]
        up_ref[2 * NX : 2 * NX + GX] = e_ref[2, NZ]
        up_ref[2 * NX + GX :] = jnp.zeros((8, NY), F32)
        up_ref[2 * NX + GX : 2 * NX + GX + 1, 0:LANES] = out_near


def update_h(e_ref, h_ref, layer):
    scale = jnp.where((iota((GX, 1), 0) >= NX) & (column() == 0), 0.0, 0.5)
    ex, ey, ez = e_ref[0, layer], e_ref[1, layer], e_ref[2, layer]
    if layer == 0:
        scale = jnp.where(row() == 0, 0.0, scale)
    h_ref[0, layer] = h_ref[0, layer] - scale * ((next_y(ez) - ez) - (e_ref[1, layer + 1] - ey))
    h_ref[1, layer] = h_ref[1, layer] - scale * ((e_ref[0, layer + 1] - ex) - (next_x(ez) - ez))
    if layer:
        h_ref[2, layer] = h_ref[2, layer] - scale * ((next_x(ey) - ey) - (next_y(ex) - ex))


def k_inner_h(e_ref, h_in, h_ref):
    for layer in range(1, NZ):
        update_h(e_ref, h_ref, layer)


def edge_h(e_ref, h_ref, down_ref):
    e_ref[0, NZ + 1] = down_ref[0:GX]
    e_ref[1, NZ + 1, :NX] = down_ref[GX : GX + NX]
    update_h(e_ref, h_ref, NZ)


def k_volts(
    n, up_ref, down_ref, d_ref, g_ref, ez_ref, wave_ref, port_ref, onehot_ref, static_ref, inverse_ref, cell_ref, e_in, h_in, hist_in, e_ref, h_ref, hist_ref, pay_ref
):
    e_ref[0, 0, :NX] = up_ref[0:NX]
    e_ref[1, 0, :NX] = up_ref[NX : 2 * NX]
    e_ref[2, 0] = up_ref[2 * NX : 2 * NX + GX]
    update_h(e_ref, h_ref, 0)
    edge_h(e_ref, h_ref, down_ref)
    at = n - 1 + DEPTH
    hist_ref[at : at + 1] = wave_ref[0:1]
    hist_ref[16 + at : 17 + at] = down_ref[GX + NX : GX + NX + 1, 0:LANES] + wave_ref[1:2]
    hist_ref[32 + at : 33 + at] = up_ref[2 * NX + GX : 2 * NX + GX + 1, 0:LANES]
    into_near, into_below, _ = line_inputs(static_ref[...], hist_ref[...], n)
    lines = -jnp.concatenate([into_near, into_below], 0)
    w = port_ref[24:32] * ez_ref[...]
    volts = own_volts(w, lines, port_ref[0:16].astype(jnp.int32), inverse_ref, onehot_ref)
    update_ez(e_ref, e_ref, h_ref, d_ref, g_ref, 1)
    cell = cell_ref[...]
    at_row, at_y = own_onehots(jnp.concatenate([cell, cell], 1))
    pre = at_ports(e_ref[2, 1 : NZ + 1, :NX].reshape(NZ * NX, NY), at_row, at_y)
    payload(pay_ref, volts, pre)


def k_exy(h_ref, d_ref, g_ref, e_in, e_ref, xr_ref, xl_ref):
    update_exy(e_ref, e_ref, h_ref, d_ref, g_ref, 1)
    send_x(e_ref, xr_ref, xl_ref)


def k_last(down_ref, wave_ref, e_in, h_in, e_out, h_out, wave_out, e_ref, h_ref):
    edge_h(e_in, h_in, down_ref)
    for c in range(3):
        for z in range(NZ):
            e_out[c, z] = e_in[c, z + 1, :NX]
            h_out[c, z] = h_in[c, z + 1, :NX]
    above = down_ref[GX + NX : GX + NX + 1, 0:LANES] + wave_ref[1:2]
    wave_out[...] = jnp.concatenate([wave_ref[0:1], above], 0)[None]


def local(
    e_field,
    h_field,
    e_decay,
    e_gain,
    port_cell,
    port_node,
    port_conductance,
    inverse,
    line_near,
    line_far,
    line_delay,
    line_imped,
    hist_near,
    hist_far,
):
    e_shape = (3, NZ + 2, GX, NY)
    h_shape = (3, NZ + 1, GX, NY)
    pay_shape = (NB, 8, LANES)
    xr_shape, xl_shape = (3 * NZ, NY), (2 * NZ, NY)
    up_shape, down_shape = (2 * NX + GX + 8, NY), (NX + GX + 8, NY)

    pay, up, right = call(
        k_first,
        [(pay_shape, F32), ((2 * NX + 8, NY), F32), ((2 * NZ, NY), F32)],
        e_field, h_field, e_gain, port_cell, port_node, port_conductance, line_far, line_delay, line_imped, hist_near,
        name="first",
    )
    got = exchanged(pay)
    up = shifted(up, "fz", 1)
    right = shifted(right, "fxy", 1)
    e, h, pre, xr, xl = call(
        k_start,
        [(e_shape, F32), (h_shape, F32), ((8, LANES), F32), (xr_shape, F32), (xl_shape, F32)],
        e_field, h_field, e_decay, e_gain, port_cell, up, right,
        name="start",
    )
    pay, port, onehot, static, hist = call(
        k_tables,
        [(pay_shape, F32), ((48, LANES), F32), ((10, LANES, LANES), BF16), ((8, LANES), F32), ((48, LANES), F32)],
        got, up, line_near, line_delay, line_imped, hist_near, hist_far, inverse, pre,
        name="tables",
    )
    ez = port[40:48]
    at_row, at_y = call(k_cells, [((NZ * GX, 3 * LANES), BF16), ((NY, 3 * LANES), BF16)], port, name="cells")
    for n in range(STEPS):
        last = n == STEPS - 1
        if last:
            node_volt = pay[0, 0:1]
        got = exchanged(pay)
        xr = shifted(xr, "fxy", 1)
        xl = shifted(xl, "fxy", -1)
        sends = ([] if last else [(up_shape, F32)]) + [(down_shape, F32)]
        e, ez, wave, *sends = call(
            functools.partial(k_currents, n, last),
            [(e_shape, F32), ((8, LANES), F32), ((8, LANES), F32), *sends],
            got, port, ez, onehot, static, hist, at_row, at_y, xr, xl, e,
            alias={10: 0},
            name="currents",
        )
        down = shifted(sends[-1], "fz", -1)
        if not last:
            up = shifted(sends[0], "fz", 1)
        (h,) = call(k_inner_h, [(h_shape, F32)], e, h, alias={1: 0}, name="inner_h")
        if last:
            break
        e, h, hist, pay = call(
            functools.partial(k_volts, n + 1),
            [(e_shape, F32), (h_shape, F32), ((48, LANES), F32), (pay_shape, F32)],
            up, down, e_decay, e_gain, ez, wave, port, onehot, static, inverse, port_cell, e, h, hist,
            alias={11: 0, 12: 1, 13: 2},
            name="volts",
        )
        e, xr, xl = call(k_exy, [(e_shape, F32), (xr_shape, F32), (xl_shape, F32)], h, e_decay, e_gain, e, alias={3: 0}, name="exy")
    field = (3, NZ, NX, NY)
    e_out, h_out, line_wave, _, _ = call(
        k_last,
        [(field, F32), (field, F32), ((1, 2, LANES), F32), (e_shape, F32), (h_shape, F32)],
        down, wave, e, h,
        alias={2: 3, 3: 4},
        name="last",
    )
    return e_out, h_out, node_volt, line_wave


def solution(mesh):
    placed = (
        P(None, "fz", "fxy", None),
        P(None, "fz", "fxy", None),
        P("fz", "fxy", None),
        P("fz", "fxy", None),
        P("fz", "fxy"),
        P("fz", "fxy"),
        P("fz", "fxy"),
        P("fz", "fxy", None),
        P("fz", None),
        P("fz", None),
        P("fz", None),
        P("fz", None),
        P("fz", None, None),
        P("fz", None, None),
    )
    return jax.shard_map(
        local,
        mesh=mesh,
        in_specs=placed,
        out_specs=(
            P(None, "fz", "fxy", None),
            P(None, "fz", "fxy", None),
            P("fz", "fxy"),
            P("fz", None, None),
        ),
        check_vma=False,
    )
```

time: 326 us -> 209 us (0.64)
  other arithmetic: 46.9 us -> 0 us
  starting transfers between devices: 142 us -> 104 us
  local copies, waits for them, and re-layouts: 71.8 us -> 45.6 us
  Pallas kernels: 0 us -> 14.2 us
  waiting for transfers between devices: 55.1 us -> 41.8 us
  matrix products: 3.64 us -> 0 us
    all_to_all x8 -> x5, waiting for transfers between devices: 46 us -> 6.02 us  [exchanged(): return lax.all_to_all(value, 'fxy', 0, 0, tiled=True)]
    ppermute x24 -> x17, starting transfers between devices: 74.5 us -> 45.1 us  [shifted(): return lax.ppermute(value, axis, pairs)]
    gather x25 -> x0, local copies, waits for them, and re-layouts: 27.6 us -> none  [the longest x4 6.09 us: local(): out_near = -2.0 * volts[near_nodes] / impedance - incoming_a]
    ppermute x24 -> x17, waiting for transfers between devices: 9.08 us -> 35.7 us  [shifted(): return lax.ppermute(value, axis, pairs)]
    unnamed x231 -> x146, local copies, waits for them, and re-layouts: 20.9 us -> 44.4 us
    scatter-add x16 -> x0, other arithmetic: 19.3 us -> none  [the longest x4 5.98 us: local(): far_sources = empty_nodes.at[far_nodes].add(-incoming_b)]
    pallas_call x0 -> x19, Pallas kernels: none -> 14.2 us  [call(): pl.pallas_call(kernel, out_shape=[jax.ShapeDtypeStruct(s, d) for s, d in...]
    slice x46 -> x1, local copies, waits for them, and re-layouts: 12 us -> 0.01 us  [local(): ez = port[40:48]]
  transfers between devices with their start and end apart: 32 -> 22, of which waited for: 9 -> 13; matrix products, arithmetic and copies ran while one was open for 25% -> 1% of each run, Pallas kernels for 0% -> 1%
where the time goes in v1:
time: 209 us; the launch traced here: 206 us
  starting transfers between devices  104 us (50%)
  local copies, waits for them, and re-layouts  45.6 us (22%)
  waiting for transfers between devices  41.8 us (20%)
  Pallas kernels  14.2 us (7%)
    all_to_all x5, starting transfers between devices, exchanged(): return lax.all_to_all(value, 'fxy', 0, 0, tiled=True)  58.6 us
    ppermute x17, starting transfers between devices, shifted(): return lax.ppermute(value, axis, pairs)  45.1 us
    unnamed x146, local copies, waits for them, and re-layouts  44.4 us
    ppermute x17, waiting for transfers between devices, shifted(): return lax.ppermute(value, axis, pairs)  35.7 us
    pallas_call x19, Pallas kernels, call(): pl.pallas_call(kernel, out_shape=[jax.ShapeDtypeStruct(s, d) for s, d in...  14.2 us
    all_to_all x5, waiting for transfers between devices, exchanged(): return lax.all_to_all(value, 'fxy', 0, 0, tiled=True)  6.02 us
  transfers between devices with their start and end apart: 22, of which 13 were waited for; matrix products, arithmetic and copies ran while one was open for 1% of the time, Pallas kernels for 1%

profile of v1, /device:TPU:7, one launch (start us, length us, event | category | flops | bytes accessed | tf_op | source)
XLA Modules:
  0.0 206.4 jit_solution(8972703150233905966)
XLA Ops:
  1.3 0.9 copy-done
  2.3 1.1 copy-done.18
  3.4 1.1 copy-done.20
  8.5 1.1 first.1
  9.6 15.0 %all-to-all-start = ((f32[16,8,128]{2,1,0:T(8,128)}), f32[16,8,128]{2,1,0:T(8,128)S(1)}, u32[]{:S(2)}, u32[]{:S(2)}) async-start(f32[16,8,128]{2,1,0:T(8,128)} %get-tuple-element.61), calls=%async_computation | async-start | bytes 131072 | tf_op jit(solution)/shard_map/all_to_all | solution.py:45
  24.7 4.0 %collective-permute-start = (f32[40,512]{1,0:T(8,128)S(1)}, f32[40,512]{1,0:T(8,128)S(1)}, u32[]{:S(2)}, u32[]{:S(2)}) collective-permute-start(f32[40,512]{1,0:T(8,128)S(1)} %get-tuple-element.62), channel_id=1, source_target_pairs={{0,16},{16,32},{32,48},{48,64},{64,80},{80,96},{96,112},{112,128},... | collective-permute-start | bytes 245768 | tf_op jit(solution)/shard_map/ppermute | solution.py:41
  28.6 3.5 %collective-permute-start.1 = (f32[16,512]{1,0:T(8,128)S(1)}, f32[16,512]{1,0:T(8,128)S(1)}, u32[]{:S(2)}, u32[]{:S(2)}) collective-permute-start(f32[16,512]{1,0:T(8,128)S(1)} %get-tuple-element.63), channel_id=1, source_target_pairs={{0,1},{1,2},{2,3},{3,4},{4,5},{5,6},{6,7},{7,8},{8,9},{9,10},{10,1... | collective-permute-start | bytes 98312 | tf_op jit(solution)/shard_map/ppermute | solution.py:41
  32.2 1.0 collective-permute-done.1.right_ref
  33.2 1.1 copy-done.19
  34.3 1.1 copy-done.21
  37.9 1.2 copy-done.2
  39.1 0.8 copy-done.37
  41.7 13.1 %all-to-all-start.1 = ((f32[16,8,128]{2,1,0:T(8,128)}), f32[16,8,128]{2,1,0:T(8,128)}, u32[]{:S(2)}, u32[]{:S(2)}) async-start(f32[16,8,128]{2,1,0:T(8,128)} %copy-done.39), calls=%async_computation.1 | async-start | bytes 131072 | tf_op jit(solution)/shard_map/all_to_all | solution.py:45
  54.8 3.2 %collective-permute-start.2 = (f32[24,512]{1,0:T(8,128)}, f32[24,512]{1,0:T(8,128)S(1)}, u32[]{:S(2)}, u32[]{:S(2)}) collective-permute-start(f32[24,512]{1,0:T(8,128)} %copy-done.69), channel_id=1, source_target_pairs={{0,1},{1,2},{2,3},{3,4},{4,5},{5,6},{6,7},{7,8},{8,9},{9,10},{10,1... | collective-permute-start | bytes 147464 | tf_op jit(solution)/shard_map/ppermute | solution.py:41
  58.1 1.3 collective-permute-start.3
  61.0 2.3 %collective-permute-done.3.xl_ref = f32[16,512]{1,0:T(8,128)S(1)} collective-permute-done((f32[16,512]{1,0:T(8,128)}, f32[16,512]{1,0:T(8,128)S(1)}, u32[]{:S(2)}, u32[]{:S(2)}) %collective-permute-start.3) | collective-permute-done | bytes 32800 | tf_op jit(solution)/shard_map/ppermute | solution.py:41
  64.6 2.0 all-to-all-done.1.got_ref
  66.6 1.0 copy-done.14
  69.0 0.8 copy-done.45
  69.8 0.8 copy-done.53
  70.6 1.6 currents.4
  72.2 5.1 %collective-permute-start.4 = (f32[64,512]{1,0:T(8,128)S(1)}, f32[64,512]{1,0:T(8,128)S(1)}, u32[]{:S(2)}, u32[]{:S(2)}) collective-permute-start(f32[64,512]{1,0:T(8,128)S(1)} %get-tuple-element.75), channel_id=1, source_target_pairs={{0,16},{16,32},{32,48},{48,64},{64,80},{80,96},{96,112},{112,128},... | collective-permute-start | bytes 393224 | tf_op jit(solution)/shard_map/ppermute | solution.py:41
  77.3 1.9 collective-permute-start.5
  79.5 5.8 %collective-permute-done.5.down_ref = f32[48,512]{1,0:T(8,128)S(1)} collective-permute-done((f32[48,512]{1,0:T(8,128)S(1)}, f32[48,512]{1,0:T(8,128)S(1)}, u32[]{:S(2)}, u32[]{:S(2)}) %collective-permute-start.5) | collective-permute-done | bytes 98336 | tf_op jit(solution)/shard_map/ppermute | solution.py:41
  87.2 9.2 %all-to-all-start.2 = ((f32[16,8,128]{2,1,0:T(8,128)}), f32[16,8,128]{2,1,0:T(8,128)}, u32[]{:S(2)}, u32[]{:S(2)}) async-start(f32[16,8,128]{2,1,0:T(8,128)} %copy-done.40), calls=%async_computation.2 | async-start | bytes 131072 | tf_op jit(solution)/shard_map/all_to_all | solution.py:45
  96.5 0.9 copy-done.8
  97.7 3.2 %collective-permute-start.6 = (f32[24,512]{1,0:T(8,128)S(1)}, f32[24,512]{1,0:T(8,128)S(1)}, u32[]{:S(2)}, u32[]{:S(2)}) collective-permute-start(f32[24,512]{1,0:T(8,128)S(1)} %get-tuple-element.85), channel_id=1, source_target_pairs={{0,1},{1,2},{2,3},{3,4},{4,5},{5,6},{6,7},{7,8},{8,9},{9,10},{10,1... | collective-permute-start | bytes 147464 | tf_op jit(solution)/shard_map/ppermute | solution.py:41
  100.9 1.3 collective-permute-start.7
  102.2 3.8 %collective-permute-done.7.xl_ref = f32[16,512]{1,0:T(8,128)S(1)} collective-permute-done((f32[16,512]{1,0:T(8,128)S(1)}, f32[16,512]{1,0:T(8,128)S(1)}, u32[]{:S(2)}, u32[]{:S(2)}) %collective-permute-start.7) | collective-permute-done | bytes 32800 | tf_op jit(solution)/shard_map/ppermute | solution.py:41
  107.2 1.1 all-to-all-done.2.got_ref
  108.3 1.0 copy-done.15
  110.7 0.8 copy-done.47
  111.5 0.8 copy-done.55
  112.3 1.6 currents.5
  113.9 3.1 %collective-permute-start.8 = (f32[64,512]{1,0:T(8,128)S(1)}, f32[64,512]{1,0:T(8,128)S(1)}, u32[]{:S(2)}, u32[]{:S(2)}) collective-permute-start(f32[64,512]{1,0:T(8,128)S(1)} %get-tuple-element.88), channel_id=1, source_target_pairs={{0,16},{16,32},{32,48},{48,64},{64,80},{80,96},{96,112},{112,128},... | collective-permute-start | bytes 393224 | tf_op jit(solution)/shard_map/ppermute | solution.py:41
  117.0 1.9 collective-permute-start.9
  119.3 5.8 %collective-permute-done.9.down_ref = f32[48,512]{1,0:T(8,128)S(1)} collective-permute-done((f32[48,512]{1,0:T(8,128)S(1)}, f32[48,512]{1,0:T(8,128)S(1)}, u32[]{:S(2)}, u32[]{:S(2)}) %collective-permute-start.9) | collective-permute-done | bytes 98336 | tf_op jit(solution)/shard_map/ppermute | solution.py:41
  127.0 10.8 %all-to-all-start.3 = ((f32[16,8,128]{2,1,0:T(8,128)}), f32[16,8,128]{2,1,0:T(8,128)}, u32[]{:S(2)}, u32[]{:S(2)}) async-start(f32[16,8,128]{2,1,0:T(8,128)} %copy-done.41), calls=%async_computation.3 | async-start | bytes 131072 | tf_op jit(solution)/shard_map/all_to_all | solution.py:45
  137.8 0.9 copy-done.10
  139.0 3.2 %collective-permute-start.10 = (f32[24,512]{1,0:T(8,128)S(1)}, f32[24,512]{1,0:T(8,128)S(1)}, u32[]{:S(2)}, u32[]{:S(2)}) collective-permute-start(f32[24,512]{1,0:T(8,128)S(1)} %get-tuple-element.97), channel_id=1, source_target_pairs={{0,1},{1,2},{2,3},{3,4},{4,5},{5,6},{6,7},{7,8},{8,9},{9,10},{10,1... | collective-permute-start | bytes 147464 | tf_op jit(solution)/shard_map/ppermute | solution.py:41
  142.2 1.3 collective-permute-start.11
  143.5 3.4 %collective-permute-done.11.xl_ref = f32[16,512]{1,0:T(8,128)S(1)} collective-permute-done((f32[16,512]{1,0:T(8,128)S(1)}, f32[16,512]{1,0:T(8,128)S(1)}, u32[]{:S(2)}, u32[]{:S(2)}) %collective-permute-start.11) | collective-permute-done | bytes 32800 | tf_op jit(solution)/shard_map/ppermute | solution.py:41
  148.1 1.5 all-to-all-done.3.got_ref
  149.6 1.0 copy-done.16
  152.1 0.8 copy-done.49
  152.9 0.8 copy-done.57
  153.6 1.6 currents.6
  155.2 3.7 %collective-permute-start.12 = (f32[64,512]{1,0:T(8,128)S(1)}, f32[64,512]{1,0:T(8,128)S(1)}, u32[]{:S(2)}, u32[]{:S(2)}) collective-permute-start(f32[64,512]{1,0:T(8,128)S(1)} %get-tuple-element.100), channel_id=1, source_target_pairs={{0,16},{16,32},{32,48},{48,64},{64,80},{80,96},{96,112},{112,128},... | collective-permute-start | bytes 393224 | tf_op jit(solution)/shard_map/ppermute | solution.py:41
  158.9 1.9 collective-permute-start.13
  161.2 5.8 %collective-permute-done.13.down_ref = f32[48,512]{1,0:T(8,128)S(1)} collective-permute-done((f32[48,512]{1,0:T(8,128)S(1)}, f32[48,512]{1,0:T(8,128)S(1)}, u32[]{:S(2)}, u32[]{:S(2)}) %collective-permute-start.13) | collective-permute-done | bytes 98336 | tf_op jit(solution)/shard_map/ppermute | solution.py:41
  168.9 10.3 %all-to-all-start.4 = ((f32[16,8,128]{2,1,0:T(8,128)}), f32[16,8,128]{2,1,0:T(8,128)}, u32[]{:S(2)}, u32[]{:S(2)}) async-start(f32[16,8,128]{2,1,0:T(8,128)} %copy-done.38), calls=%async_computation.4 | async-start | bytes 131072 | tf_op jit(solution)/shard_map/all_to_all | solution.py:45
  179.2 0.9 copy-done.12
  180.4 3.2 %collective-permute-start.14 = (f32[24,512]{1,0:T(8,128)S(1)}, f32[24,512]{1,0:T(8,128)S(1)}, u32[]{:S(2)}, u32[]{:S(2)}) collective-permute-start(f32[24,512]{1,0:T(8,128)S(1)} %get-tuple-element.109), channel_id=1, source_target_pairs={{0,1},{1,2},{2,3},{3,4},{4,5},{5,6},{6,7},{7,8},{8,9},{9,10},{10,1... | collective-permute-start | bytes 147464 | tf_op jit(solution)/shard_map/ppermute | solution.py:41
  183.6 1.3 collective-permute-start.15
  184.9 3.4 %collective-permute-done.15.xl_ref = f32[16,512]{1,0:T(8,128)S(1)} collective-permute-done((f32[16,512]{1,0:T(8,128)S(1)}, f32[16,512]{1,0:T(8,128)S(1)}, u32[]{:S(2)}, u32[]{:S(2)}) %collective-permute-start.15) | collective-permute-done | bytes 32800 | tf_op jit(solution)/shard_map/ppermute | solution.py:41
  189.5 1.5 all-to-all-done.4.got_ref
  191.0 1.0 copy-done.17
  193.4 0.8 copy-done.43
  194.2 0.8 copy-done.51
  195.0 2.1 currents.7
  197.1 1.9 collective-permute-start.16
  199.0 1.2 slice_bitcast_fusion
  200.5 4.6 %collective-permute-done.16.down_ref = f32[48,512]{1,0:T(8,128)S(1)} collective-permute-done((f32[48,512]{1,0:T(8,128)S(1)}, f32[48,512]{1,0:T(8,128)S(1)}, u32[]{:S(2)}, u32[]{:S(2)}) %collective-permute-start.16) | collective-permute-done | bytes 98336 | tf_op jit(solution)/shard_map/ppermute | solution.py:41
  205.1 1.3 last.1
  (147 shorter events, 28.9 us)
Async XLA Ops:
  0.6 31.5 %copy-start.71 = (f32[1,6,128]{2,0,1:T(1,128)S(1)}, f32[1,6,128]{2,0,1:T(1,128)}, u32[]{:S(2)}) copy-start(f32[1,6,128]{2,0,1:T(1,128)} %param.27) | copy-start | bytes 9220
  1.3 0.9 copy-start
  2.3 1.1 copy-start.18
  3.4 1.1 copy-start.20
  8.5 24.7 %copy-start.1 = (f32[8,16,512]{2,1,0:T(8,128)S(1)}, f32[8,16,512]{2,1,0:T(8,128)}, u32[]{:S(2)}) copy-start(f32[8,16,512]{2,1,0:T(8,128)} %g_ref.15) | copy-start | bytes 786436
  8.5 24.7 %copy-start.6 = (f32[8,16,512]{2,1,0:T(8,128)S(1)}, f32[8,16,512]{2,1,0:T(8,128)}, u32[]{:S(2)}) copy-start(f32[8,16,512]{2,1,0:T(8,128)} %d_ref.13) | copy-start | bytes 786436
  9.6 28.3 %copy-start.62 = (s32[1,128]{1,0:T(1,128)S(1)}, s32[1,128]{1,0:T(1,128)}, u32[]{:S(2)}) copy-start(s32[1,128]{1,0:T(1,128)} %delay_ref.3) | copy-start | bytes 1540
  9.6 28.3 %copy-start.64 = (f32[1,128]{1,0:T(1,128)S(1)}, f32[1,128]{1,0:T(1,128)}, u32[]{:S(2)}) copy-start(f32[1,128]{1,0:T(1,128)} %imped_ref.3) | copy-start | bytes 1540
  9.6 28.3 %copy-start.65 = (s32[1,128]{1,0:T(1,128)S(1)}, s32[1,128]{1,0:T(1,128)}, u32[]{:S(2)}) copy-start(s32[1,128]{1,0:T(1,128)} %near_ref.1) | copy-start | bytes 1540
  9.6 27.7 %all-to-all-start = ((f32[16,8,128]{2,1,0:T(8,128)}), f32[16,8,128]{2,1,0:T(8,128)S(1)}, u32[]{:S(2)}, u32[]{:S(2)}) async-start(f32[16,8,128]{2,1,0:T(8,128)} %get-tuple-element.61), calls=%async_computation | async-start | bytes 131072 | tf_op jit(solution)/shard_map/all_to_all | solution.py:45
  24.7 8.5 %collective-permute-start = (f32[40,512]{1,0:T(8,128)S(1)}, f32[40,512]{1,0:T(8,128)S(1)}, u32[]{:S(2)}, u32[]{:S(2)}) collective-permute-start(f32[40,512]{1,0:T(8,128)S(1)} %get-tuple-element.62), channel_id=1, source_target_pairs={{0,16},{16,32},{32,48},{48,64},{64,80},{80,96},{96,112},{112,128},... | collective-permute-start | bytes 245768 | tf_op jit(solution)/shard_map/ppermute | solution.py:41
  28.6 4.6 %collective-permute-start.1 = (f32[16,512]{1,0:T(8,128)S(1)}, f32[16,512]{1,0:T(8,128)S(1)}, u32[]{:S(2)}, u32[]{:S(2)}) collective-permute-start(f32[16,512]{1,0:T(8,128)S(1)} %get-tuple-element.63), channel_id=1, source_target_pairs={{0,1},{1,2},{2,3},{3,4},{4,5},{5,6},{6,7},{7,8},{8,9},{9,10},{10,1... | collective-permute-start | bytes 98312 | tf_op jit(solution)/shard_map/ppermute | solution.py:41
  33.2 1.1 copy-start.19
  34.3 1.1 copy-start.21
  37.9 1.2 copy-start.2
  39.1 0.8 copy-start.37
  41.7 17.6 %copy-start.22 = (f32[48,128]{1,0:T(8,128)}, f32[48,128]{1,0:T(8,128)S(1)}, u32[]{:S(2)}) copy-start(f32[48,128]{1,0:T(8,128)S(1)} %get-tuple-element.66.port_ref) | copy-start | bytes 73732
  41.7 24.8 %all-to-all-start.1 = ((f32[16,8,128]{2,1,0:T(8,128)}), f32[16,8,128]{2,1,0:T(8,128)}, u32[]{:S(2)}, u32[]{:S(2)}) async-start(f32[16,8,128]{2,1,0:T(8,128)} %copy-done.39), calls=%async_computation.1 | async-start | bytes 131072 | tf_op jit(solution)/shard_map/all_to_all | solution.py:45
  54.8 9.1 %collective-permute-start.2 = (f32[24,512]{1,0:T(8,128)}, f32[24,512]{1,0:T(8,128)S(1)}, u32[]{:S(2)}, u32[]{:S(2)}) collective-permute-start(f32[24,512]{1,0:T(8,128)} %copy-done.69), channel_id=1, source_target_pairs={{0,1},{1,2},{2,3},{3,4},{4,5},{5,6},{6,7},{7,8},{8,9},{9,10},{10,1... | collective-permute-start | bytes 147464 | tf_op jit(solution)/shard_map/ppermute | solution.py:41
  58.1 5.3 %collective-permute-start.3 = (f32[16,512]{1,0:T(8,128)}, f32[16,512]{1,0:T(8,128)S(1)}, u32[]{:S(2)}, u32[]{:S(2)}) collective-permute-start(f32[16,512]{1,0:T(8,128)} %copy-done.70), channel_id=1, source_target_pairs={{1,0},{2,1},{3,2},{4,3},{5,4},{6,5},{7,6},{8,7},{9,8},{10,9},{11,1... | collective-permute-start | bytes 98312 | tf_op jit(solution)/shard_map/ppermute | solution.py:41
  59.4 0.7 copy-start.23
  60.3 0.7 copy-start.13
  66.6 1.0 copy-start.14
  67.6 0.7 copy-start.24
  68.3 0.7 copy-start.29
  69.0 0.8 copy-start.45
  69.8 0.8 copy-start.53
  72.2 13.1 %collective-permute-start.4 = (f32[64,512]{1,0:T(8,128)S(1)}, f32[64,512]{1,0:T(8,128)S(1)}, u32[]{:S(2)}, u32[]{:S(2)}) collective-permute-start(f32[64,512]{1,0:T(8,128)S(1)} %get-tuple-element.75), channel_id=1, source_target_pairs={{0,16},{16,32},{32,48},{48,64},{64,80},{80,96},{96,112},{112,128},... | collective-permute-start | bytes 393224 | tf_op jit(solution)/shard_map/ppermute | solution.py:41
  77.3 8.0 %collective-permute-start.5 = (f32[48,512]{1,0:T(8,128)S(1)}, f32[48,512]{1,0:T(8,128)S(1)}, u32[]{:S(2)}, u32[]{:S(2)}) collective-permute-start(f32[48,512]{1,0:T(8,128)S(1)} %get-tuple-element.76), channel_id=1, source_target_pairs={{16,0},{32,16},{48,32},{64,48},{80,64},{96,80},{112,96},{128,112},... | collective-permute-start | bytes 294920 | tf_op jit(solution)/shard_map/ppermute | solution.py:41
  79.2 6.1 %copy-start.3 = (f32[1,128,2048]{2,1,0:T(8,128)S(1)}, f32[1,128,2048]{2,1,0:T(8,128)}, u32[]{:S(2)}) copy-start(f32[1,128,2048]{2,1,0:T(8,128)} %inverse_ref.7) | copy-start | bytes 3145732
  79.2 6.1 %copy-start.7 = (f32[8,16,512]{2,1,0:T(8,128)S(1)}, f32[8,16,512]{2,1,0:T(8,128)}, u32[]{:S(2)}) copy-start(f32[8,16,512]{2,1,0:T(8,128)} %d_ref.13) | copy-start | bytes 786436
  79.2 6.1 %copy-start.59 = (s32[1,64]{1,0:T(1,128)S(1)}, s32[1,64]{1,0:T(1,128)}, u32[]{:S(2)}) copy-start(s32[1,64]{1,0:T(1,128)} %cell_ref.9) | copy-start | bytes 772
  87.2 21.0 %all-to-all-start.2 = ((f32[16,8,128]{2,1,0:T(8,128)}), f32[16,8,128]{2,1,0:T(8,128)}, u32[]{:S(2)}, u32[]{:S(2)}) async-start(f32[16,8,128]{2,1,0:T(8,128)} %copy-done.40), calls=%async_computation.2 | async-start | bytes 131072 | tf_op jit(solution)/shard_map/all_to_all | solution.py:45
  96.5 1.0 copy-start.8
  97.7 8.9 %collective-permute-start.6 = (f32[24,512]{1,0:T(8,128)S(1)}, f32[24,512]{1,0:T(8,128)S(1)}, u32[]{:S(2)}, u32[]{:S(2)}) collective-permute-start(f32[24,512]{1,0:T(8,128)S(1)} %get-tuple-element.85), channel_id=1, source_target_pairs={{0,1},{1,2},{2,3},{3,4},{4,5},{5,6},{6,7},{7,8},{8,9},{9,10},{10,1... | collective-permute-start | bytes 147464 | tf_op jit(solution)/shard_map/ppermute | solution.py:41
  100.9 5.1 %collective-permute-start.7 = (f32[16,512]{1,0:T(8,128)S(1)}, f32[16,512]{1,0:T(8,128)S(1)}, u32[]{:S(2)}, u32[]{:S(2)}) collective-permute-start(f32[16,512]{1,0:T(8,128)S(1)} %get-tuple-element.86), channel_id=1, source_target_pairs={{1,0},{2,1},{3,2},{4,3},{5,4},{6,5},{7,6},{8,7},{9,8},{10,9},{11,1... | collective-permute-start | bytes 98312 | tf_op jit(solution)/shard_map/ppermute | solution.py:41
  108.3 1.0 copy-start.15
  110.7 0.8 copy-start.47
  111.5 0.8 copy-start.55
  113.9 11.2 %collective-permute-start.8 = (f32[64,512]{1,0:T(8,128)S(1)}, f32[64,512]{1,0:T(8,128)S(1)}, u32[]{:S(2)}, u32[]{:S(2)}) collective-permute-start(f32[64,512]{1,0:T(8,128)S(1)} %get-tuple-element.88), channel_id=1, source_target_pairs={{0,16},{16,32},{32,48},{48,64},{64,80},{80,96},{96,112},{112,128},... | collective-permute-start | bytes 393224 | tf_op jit(solution)/shard_map/ppermute | solution.py:41
  117.0 8.0 %collective-permute-start.9 = (f32[48,512]{1,0:T(8,128)S(1)}, f32[48,512]{1,0:T(8,128)S(1)}, u32[]{:S(2)}, u32[]{:S(2)}) collective-permute-start(f32[48,512]{1,0:T(8,128)S(1)} %get-tuple-element.89), channel_id=1, source_target_pairs={{16,0},{32,16},{48,32},{64,48},{80,64},{96,80},{112,96},{128,112},... | collective-permute-start | bytes 294920 | tf_op jit(solution)/shard_map/ppermute | solution.py:41
  118.9 6.1 %copy-start.4 = (f32[1,128,2048]{2,1,0:T(8,128)S(1)}, f32[1,128,2048]{2,1,0:T(8,128)}, u32[]{:S(2)}) copy-start(f32[1,128,2048]{2,1,0:T(8,128)} %inverse_ref.7) | copy-start | bytes 3145732
  118.9 6.1 %copy-start.9 = (f32[8,16,512]{2,1,0:T(8,128)S(1)}, f32[8,16,512]{2,1,0:T(8,128)}, u32[]{:S(2)}) copy-start(f32[8,16,512]{2,1,0:T(8,128)} %d_ref.13) | copy-start | bytes 786436
  127.0 22.6 %all-to-all-start.3 = ((f32[16,8,128]{2,1,0:T(8,128)}), f32[16,8,128]{2,1,0:T(8,128)}, u32[]{:S(2)}, u32[]{:S(2)}) async-start(f32[16,8,128]{2,1,0:T(8,128)} %copy-done.41), calls=%async_computation.3 | async-start | bytes 131072 | tf_op jit(solution)/shard_map/all_to_all | solution.py:45
  137.8 1.0 copy-start.10
  139.0 8.5 %collective-permute-start.10 = (f32[24,512]{1,0:T(8,128)S(1)}, f32[24,512]{1,0:T(8,128)S(1)}, u32[]{:S(2)}, u32[]{:S(2)}) collective-permute-start(f32[24,512]{1,0:T(8,128)S(1)} %get-tuple-element.97), channel_id=1, source_target_pairs={{0,1},{1,2},{2,3},{3,4},{4,5},{5,6},{6,7},{7,8},{8,9},{9,10},{10,1... | collective-permute-start | bytes 147464 | tf_op jit(solution)/shard_map/ppermute | solution.py:41
  142.2 4.7 %collective-permute-start.11 = (f32[16,512]{1,0:T(8,128)S(1)}, f32[16,512]{1,0:T(8,128)S(1)}, u32[]{:S(2)}, u32[]{:S(2)}) collective-permute-start(f32[16,512]{1,0:T(8,128)S(1)} %get-tuple-element.98), channel_id=1, source_target_pairs={{1,0},{2,1},{3,2},{4,3},{5,4},{6,5},{7,6},{8,7},{9,8},{10,9},{11,1... | collective-permute-start | bytes 98312 | tf_op jit(solution)/shard_map/ppermute | solution.py:41
  149.6 1.0 copy-start.16
  152.1 0.8 copy-start.49
  152.9 0.8 copy-start.57
  155.2 11.7 %collective-permute-start.12 = (f32[64,512]{1,0:T(8,128)S(1)}, f32[64,512]{1,0:T(8,128)S(1)}, u32[]{:S(2)}, u32[]{:S(2)}) collective-permute-start(f32[64,512]{1,0:T(8,128)S(1)} %get-tuple-element.100), channel_id=1, source_target_pairs={{0,16},{16,32},{32,48},{48,64},{64,80},{80,96},{96,112},{112,128},... | collective-permute-start | bytes 393224 | tf_op jit(solution)/shard_map/ppermute | solution.py:41
  158.9 8.0 %collective-permute-start.13 = (f32[48,512]{1,0:T(8,128)S(1)}, f32[48,512]{1,0:T(8,128)S(1)}, u32[]{:S(2)}, u32[]{:S(2)}) collective-permute-start(f32[48,512]{1,0:T(8,128)S(1)} %get-tuple-element.101), channel_id=1, source_target_pairs={{16,0},{32,16},{48,32},{64,48},{80,64},{96,80},{112,96},{128,112},... | collective-permute-start | bytes 294920 | tf_op jit(solution)/shard_map/ppermute | solution.py:41
  160.8 6.1 %copy-start.5 = (f32[1,128,2048]{2,1,0:T(8,128)S(1)}, f32[1,128,2048]{2,1,0:T(8,128)}, u32[]{:S(2)}) copy-start(f32[1,128,2048]{2,1,0:T(8,128)} %inverse_ref.7) | copy-start | bytes 3145732
  160.8 6.1 %copy-start.11 = (f32[8,16,512]{2,1,0:T(8,128)S(1)}, f32[8,16,512]{2,1,0:T(8,128)}, u32[]{:S(2)}) copy-start(f32[8,16,512]{2,1,0:T(8,128)} %d_ref.13) | copy-start | bytes 786436
  160.8 6.1 %copy-start.60 = (s32[1,64]{1,0:T(1,128)S(1)}, s32[1,64]{1,0:T(1,128)}, u32[]{:S(2)}) copy-start(s32[1,64]{1,0:T(1,128)} %cell_ref.9) | copy-start | bytes 772
  168.9 22.1 %all-to-all-start.4 = ((f32[16,8,128]{2,1,0:T(8,128)}), f32[16,8,128]{2,1,0:T(8,128)}, u32[]{:S(2)}, u32[]{:S(2)}) async-start(f32[16,8,128]{2,1,0:T(8,128)} %copy-done.38), calls=%async_computation.4 | async-start | bytes 131072 | tf_op jit(solution)/shard_map/all_to_all | solution.py:45
  179.2 1.0 copy-start.12
  180.4 8.5 %collective-permute-start.14 = (f32[24,512]{1,0:T(8,128)S(1)}, f32[24,512]{1,0:T(8,128)S(1)}, u32[]{:S(2)}, u32[]{:S(2)}) collective-permute-start(f32[24,512]{1,0:T(8,128)S(1)} %get-tuple-element.109), channel_id=1, source_target_pairs={{0,1},{1,2},{2,3},{3,4},{4,5},{5,6},{6,7},{7,8},{8,9},{9,10},{10,1... | collective-permute-start | bytes 147464 | tf_op jit(solution)/shard_map/ppermute | solution.py:41
  183.6 4.7 %collective-permute-start.15 = (f32[16,512]{1,0:T(8,128)S(1)}, f32[16,512]{1,0:T(8,128)S(1)}, u32[]{:S(2)}, u32[]{:S(2)}) collective-permute-start(f32[16,512]{1,0:T(8,128)S(1)} %get-tuple-element.110), channel_id=1, source_target_pairs={{1,0},{2,1},{3,2},{4,3},{5,4},{6,5},{7,6},{8,7},{9,8},{10,9},{11,1... | collective-permute-start | bytes 98312 | tf_op jit(solution)/shard_map/ppermute | solution.py:41
  191.0 1.0 copy-start.17
  192.0 0.7 copy-start.27
  193.4 0.8 copy-start.43
  194.2 0.8 copy-start.51
  197.1 8.0 %collective-permute-start.16 = (f32[48,512]{1,0:T(8,128)S(1)}, f32[48,512]{1,0:T(8,128)S(1)}, u32[]{:S(2)}, u32[]{:S(2)}) collective-permute-start(f32[48,512]{1,0:T(8,128)S(1)} %get-tuple-element.112), channel_id=1, source_target_pairs={{16,0},{32,16},{48,32},{64,48},{80,64},{96,80},{112,96},{128,112},... | collective-permute-start | bytes 294920 | tf_op jit(solution)/shard_map/ppermute | solution.py:41
  (30 other events, 19.4 us)

commit v2 on v1

v2 whole, which is shorter than its diff:
```python
import functools

import jax
import jax.numpy as jnp
from jax import lax
from jax.experimental import pallas as pl
from jax.experimental.pallas import tpu as pltpu
from jax.sharding import PartitionSpec as P

STEPS = 4
F32 = jnp.float32
BF16 = jnp.bfloat16
NZ = 8
NX = 16
NY = 512
GX = 24
NF = 32
NB = 16
HALF = 64
LANES = 128
DEPTH = 6
VMEM = pl.BlockSpec(memory_space=pltpu.VMEM)
ANY = pl.BlockSpec(memory_space=pl.ANY)
NT = (((1,), (1,)), ((), ()))
NODE, WHERE, COND, GAIN, EZ, STATIC, OWN, FROM_ABOVE, FROM_BELOW, WAVE, ROWS = 0, 16, 24, 32, 40, 48, 56, 72, 88, 104, 112
E_SHAPE = (3, NZ + 2, GX, NY)
H_SHAPE = (3, NZ + 1, GX, NY)
PAY_SHAPE = (NB, 2, LANES)
XR_SHAPE, XL_SHAPE = (3 * NZ, NY), (2 * NZ, NY)
UP_SHAPE, DOWN_SHAPE = (2 * NX + GX + 8, NY), (NX + GX + 8, NY)
FIELD = (3, NZ, NX, NY)


def call(kernel, outs, *args, alias=None, name=None, far=(), far_out=(), scratch=()):
    return pl.pallas_call(
        kernel,
        out_shape=[jax.ShapeDtypeStruct(s, F32) for s in outs],
        in_specs=[ANY if k in far else VMEM for k in range(len(args))],
        out_specs=[ANY if k in far_out else VMEM for k in range(len(outs))],
        scratch_shapes=list(scratch),
        input_output_aliases=alias or {},
        name=name,
        compiler_params=pltpu.CompilerParams(vmem_limit_bytes=40 << 20),
    )(*args)


def shifted(value, axis, by):
    devices = lax.axis_size(axis)
    pairs = [(i, i + by) for i in range(devices) if 0 <= i + by < devices]
    return lax.ppermute(value, axis, pairs)


def exchanged(value):
    return lax.all_to_all(value, "fxy", 0, 0, tiled=True)


def iota(shape, dim):
    return lax.broadcasted_iota(jnp.int32, shape, dim)


def column():
    return lax.axis_index("fxy")


def row():
    return lax.axis_index("fz")


def split3(value):
    high = value.astype(BF16)
    rest = value - high.astype(F32)
    middle = rest.astype(BF16)
    low = (rest - middle.astype(F32)).astype(BF16)
    return high, middle, low


def dot3(value, onehot, dims=(((1,), (0,)), ((), ()))):
    rows = value.shape[0]
    parts = jnp.concatenate(split3(value), 0)
    product = lax.dot_general(parts, onehot, dims, preferred_element_type=F32)
    return product[:rows] + (product[rows : 2 * rows] + product[2 * rows :])


def ones_where(condition):
    return jnp.where(condition, 1.0, 0.0).astype(BF16)


def next_y(f):
    rolled = pltpu.roll(f, NY - 1, 1)
    return jnp.where(iota(f.shape, 1) == NY - 1, 0.0, rolled)


def last_y(f):
    rolled = pltpu.roll(f, 1, 1)
    return jnp.where(iota(f.shape, 1) == 0, 0.0, rolled)


def next_x(f):
    return jnp.concatenate([f[1:], f[:1]], 0)


def last_x(f):
    return jnp.concatenate([f[GX - 1 :], f[: GX - 1]], 0)


def copies(pairs, sems):
    started = [pltpu.make_async_copy(a, b, sems.at[k]) for k, (a, b) in enumerate(pairs)]
    for copy in started:
        copy.start()
    return started


def wait(started):
    for copy in started:
        copy.wait()


def lower(got_ref, f):
    lane = iota((8, LANES), 1)
    return jnp.where(lane < HALF, got_ref[0:8, f, :], pltpu.roll(got_ref[8:16, f, :], HALF, 1))


def upper(got_ref, f):
    lane = iota((8, LANES), 1)
    return jnp.where(lane < HALF, pltpu.roll(got_ref[0:8, f, :], HALF, 1), got_ref[8:16, f, :])


def own_ports(cell):
    cell = jnp.concatenate([cell, cell], 1)
    mine = iota((1, LANES), 1) < HALF
    at_row = ones_where((iota((NZ * NX, LANES), 0) == cell // NY) & mine)
    at_y = ones_where(iota((NY, LANES), 0) == cell % NY)
    return at_row, at_y


def at_ports(field, ports):
    at_row, at_y = ports
    return jnp.sum(dot3(field, at_y) * at_row.astype(F32), 0, keepdims=True)


def hist_at(hist, position):
    out = jnp.zeros((1, LANES), F32)
    for k in range(DEPTH + STEPS):
        out = jnp.where(position == k, hist[k : k + 1], out)
    return out


def k_first(
    e_ref, h_ref, cell_ref, node_ref, cond_ref, far_ref, delay_ref, imped_ref, near_hist_ref,
    pay_ref, up_ref, right_ref,
    ez, side, cell, node, cond, far, delay, imped, hist, sems,
):
    pairs = [
        (cell_ref, cell), (node_ref, node), (cond_ref, cond), (e_ref.at[2], ez),
        (far_ref, far), (delay_ref, delay), (imped_ref, imped), (near_hist_ref, hist),
        (h_ref.at[0, NZ - 1], up_ref.at[0:NX]), (h_ref.at[1, NZ - 1], up_ref.at[NX : 2 * NX]),
        (h_ref.at[1:3, :, NX - 8 : NX], side),
    ]
    started = copies(pairs, sems)
    up_ref[2 * NX :] = jnp.zeros((8, NY), F32)
    wait(started[:4])
    here = at_ports(ez[...].reshape(NZ * NX, NY), own_ports(cell[...]))
    first = jnp.concatenate([node[...], cell[...]], 1).astype(F32)
    second = jnp.concatenate([cond[...], here[:, :HALF]], 1)
    pay_ref[...] = jnp.broadcast_to(jnp.concatenate([first, second], 0)[None], PAY_SHAPE)
    wait(started[4:])
    up_ref[2 * NX : 2 * NX + 1, 0:LANES] = far[...].astype(F32)
    up_ref[2 * NX + 1 : 2 * NX + 2, 0:LANES] = delay[...].astype(F32)
    up_ref[2 * NX + 2 : 2 * NX + 3, 0:LANES] = imped[...]
    for k in range(DEPTH):
        up_ref[2 * NX + k : 2 * NX + k + 1, LANES : 2 * LANES] = hist[k]
    for c in range(2):
        for z in range(NZ):
            right_ref[c * NZ + z : c * NZ + z + 1] = side[c, z, 7:8]


def update_e(e_ref, h_ref, d_ref, g_ref):
    for z in range(NZ):
        hx, hy, hz = h_ref[0, z + 1], h_ref[1, z + 1], h_ref[2, z + 1]
        own = hz[:NX]
        curl_x = (own - last_y(own)) - (hy[:NX] - h_ref[1, z, :NX])
        curl_y = (hx[:NX] - h_ref[0, z, :NX]) - (hz - last_x(hz))[:NX]
        curl_z = (hy - last_x(hy))[:NX] - (hx[:NX] - last_y(hx[:NX]))
        d, g = d_ref[z], g_ref[z]
        for c, curl in enumerate((curl_x, curl_y, curl_z)):
            e_ref[c, z + 1, :NX] = d * e_ref[c, z + 1, :NX] + g * curl


def send_x(e_ref, right_ref, left_ref):
    for z in range(NZ):
        for c in range(3):
            right_ref[c * NZ + z : c * NZ + z + 1] = e_ref[c, z + 1, NX - 1 : NX]
        for c in range(2):
            left_ref[c * NZ + z : c * NZ + z + 1] = e_ref[1 + c, z + 1, 0:1]


def own_rows(ref):
    return ref.at[:, 1 : NZ + 1, 0:NX]


def k_start(
    e_in, h_in, d_in, g_in, cell_in, up_ref, right_ref, e_ref, h_ref, pre_ref, xr_ref, xl_ref, d_ref, g_ref, cell_ref, sems
):
    pairs = [(e_in, own_rows(e_ref)), (h_in, own_rows(h_ref)), (d_in, d_ref), (g_in, g_ref), (cell_in, cell_ref)]
    started = copies(pairs, sems)
    first = iota((8, NY), 0)
    for z in range(NZ):
        h_ref[0, z + 1, NX:] = jnp.zeros((8, NY), F32)
        for c in range(2):
            ghost = right_ref[c * NZ + z : c * NZ + z + 1]
            h_ref[1 + c, z + 1, NX:] = jnp.where(first == 7, ghost, 0.0)
    for c in range(3):
        h_ref[c, 0] = jnp.zeros((GX, NY), F32)
        e_ref[c, 0] = jnp.zeros((GX, NY), F32)
        e_ref[c, NZ + 1] = jnp.zeros((GX, NY), F32)
    h_ref[0, 0, :NX] = up_ref[0:NX]
    h_ref[1, 0, :NX] = up_ref[NX : 2 * NX]
    wait(started)
    update_e(e_ref, h_ref, d_ref, g_ref)
    ports = own_ports(cell_ref[...])
    pre = at_ports(e_ref[2, 1 : NZ + 1, :NX].reshape(NZ * NX, NY), ports)
    gain = at_ports(g_ref[...].reshape(NZ * NX, NY), ports)
    pre_ref[...] = jnp.broadcast_to(pre + pltpu.roll(gain, HALF, 1), (8, LANES))
    send_x(e_ref, xr_ref, xl_ref)


def low_onehots(node):
    return [ones_where(iota((LANES, LANES), 0) == node[t : t + 1] % LANES) for t in range(10)]


def own_volts(w, lines, node, inverse_ref):
    high = node // LANES
    sources = jnp.zeros((NB, LANES), F32)
    values = jnp.concatenate([w, lines], 0)
    onehots = low_onehots(node)
    for t in range(10):
        spread = jnp.where(iota((NB, LANES), 0) == high[t : t + 1], values[t : t + 1], 0.0)
        sources = sources + dot3(spread, onehots[t], NT)
    total = jnp.zeros((LANES, LANES), F32)
    for t in range(NB):
        total = total + inverse_ref[0, :, t * LANES : (t + 1) * LANES] * sources[t : t + 1]
    return jnp.sum(total.T, 0, keepdims=True)


def node_values(volts, node):
    high = node // LANES
    rows = []
    onehots = low_onehots(node)
    for t in range(10):
        picked = dot3(volts, onehots[t])
        rows.append(jnp.sum(jnp.where(iota((NB, LANES), 0) == high[t : t + 1], picked, 0.0), 0, keepdims=True))
    return jnp.concatenate(rows, 0)


def line_inputs(state_ref, n):
    own = n - state_ref[STATIC + 4 : STATIC + 5].astype(jnp.int32) + DEPTH
    below = n - state_ref[STATIC + 5 : STATIC + 6].astype(jnp.int32) + DEPTH
    return (
        hist_at(state_ref[FROM_ABOVE : FROM_ABOVE + 16], own),
        hist_at(state_ref[FROM_BELOW : FROM_BELOW + 16], below),
        hist_at(state_ref[OWN : OWN + 16], own),
    )


def next_volts(state_ref, inverse_ref, n):
    into_near, into_below, _ = line_inputs(state_ref, n)
    lines = -jnp.concatenate([into_near, into_below], 0)
    w = state_ref[COND : COND + 8] * state_ref[EZ : EZ + 8]
    return own_volts(w, lines, state_ref[NODE : NODE + 16].astype(jnp.int32), inverse_ref)


def payload(pay_ref, volts, pre):
    pay_ref[...] = jnp.broadcast_to(jnp.concatenate([volts, pre], 0)[None], PAY_SHAPE)


def k_tables(
    got_ref, up_ref, pre_ref, near_in, delay_in, imped_in, near_hist_in, far_hist_in, inverse_in,
    pay_ref, state_ref,
    near_ref, delay_ref, imped_ref, near_hist_ref, far_hist_ref, inverse_ref, sems,
):
    pairs = [
        (near_in, near_ref), (delay_in, delay_ref), (imped_in, imped_ref),
        (near_hist_in, near_hist_ref), (far_hist_in, far_hist_ref), (inverse_in, inverse_ref),
    ]
    started = copies(pairs, sems)
    state_ref[...] = jnp.zeros((ROWS, LANES), F32)
    state_ref[NODE : NODE + 8] = lower(got_ref, 0)
    device = iota((8, LANES), 0) + 8 * (iota((8, LANES), 1) // HALF)
    state_ref[WHERE : WHERE + 8] = upper(got_ref, 0) + (device * (NZ * NX * NY)).astype(F32)
    state_ref[COND : COND + 8] = lower(got_ref, 1)
    state_ref[EZ : EZ + 8] = upper(got_ref, 1)
    far_below = up_ref[2 * NX : 2 * NX + 1, 0:LANES]
    imped_below = jnp.where(row() == 0, 1.0, up_ref[2 * NX + 2 : 2 * NX + 3, 0:LANES])
    wait(started[:5])
    near = near_ref[...].astype(F32)
    static = [near, far_below, imped_ref[...], imped_below, delay_ref[...].astype(F32), up_ref[2 * NX + 1 : 2 * NX + 2, 0:LANES]]
    state_ref[NODE + 8 : NODE + 10] = jnp.concatenate(static[:2], 0)
    state_ref[STATIC : STATIC + 6] = jnp.concatenate(static, 0)
    for k in range(DEPTH):
        back = DEPTH - 1 - k
        state_ref[OWN + k : OWN + k + 1] = near_hist_ref[back]
        state_ref[FROM_ABOVE + k : FROM_ABOVE + k + 1] = far_hist_ref[back]
        state_ref[FROM_BELOW + k : FROM_BELOW + k + 1] = up_ref[2 * NX + back : 2 * NX + back + 1, LANES : 2 * LANES]
    wait(started[5:])
    payload(pay_ref, next_volts(state_ref, inverse_ref, 0), pre_ref[0:1])


def block_row(k):
    block = column() + k
    return jnp.where(block < 0, block + 8, block % 8), block // 8, (block >= 0) & (block < NB)


def spread_currents(e_ref, where, drop):
    row_parts, at_y = [], []
    for k in (-1, 0, 1):
        packed, half, exists = block_row(k)
        pick = iota((8, LANES), 0) == packed
        cell = jnp.sum(jnp.where(pick, where, 0.0), 0, keepdims=True).astype(jnp.int32) % (NZ * NX * NY)
        values = jnp.sum(jnp.where(pick, drop, 0.0), 0, keepdims=True)
        x = (cell // NY) % NX + k * NX
        position = jnp.where((x >= 0) & (x <= NX), x, jnp.where(x == -1, GX - 1, -1))
        inside = (iota((1, LANES), 1) // HALF == half) & exists & (position >= 0)
        target = jnp.where(inside, (cell // (NX * NY)) * GX + position, -1)
        at_row = ones_where(iota((NZ * GX, LANES), 0) == target)
        row_parts.append(jnp.concatenate([at_row * part for part in split3(values)], 0))
        at_y.append(ones_where(iota((NY, LANES), 0) == cell % NY))
    spread = lax.dot_general(jnp.concatenate(row_parts, 1), jnp.concatenate(at_y, 1), NT, preferred_element_type=F32)
    rows = NZ * GX
    spread = spread[:rows] + (spread[rows : 2 * rows] + spread[2 * rows :])
    for z in range(NZ):
        e_ref[2, z + 1] = e_ref[2, z + 1] - spread[z * GX : (z + 1) * GX]


def k_currents(n, last, got_ref, xr_ref, xl_ref, e_in, state_in, e_ref, state_ref, *sends):
    pre = lower(got_ref, 1)
    if n == 0:
        state_ref[GAIN : GAIN + 8] = upper(got_ref, 1)
    at_nodes = node_values(got_ref[:, 0, :], state_ref[NODE : NODE + 16].astype(jnp.int32))
    where = state_ref[WHERE : WHERE + 8]
    current = state_ref[COND : COND + 8] * (state_ref[EZ : EZ + 8] - at_nodes[0:8])
    shared = current
    for k in range(1, LANES):
        same = pltpu.roll(where, k, 1) == where
        shared = shared + jnp.where(same, pltpu.roll(current, k, 1), 0.0)
    gain = state_ref[GAIN : GAIN + 8]
    state_ref[EZ : EZ + 8] = pre - gain * shared

    into_near, into_below, into_own = line_inputs(state_ref, n)
    out_near = -2.0 * at_nodes[8:9] / state_ref[STATIC + 2 : STATIC + 3] - into_near
    out_below = -2.0 * at_nodes[9:10] / state_ref[STATIC + 3 : STATIC + 4] - into_below
    top = jnp.where(row() == NF - 1, -into_own, 0.0)
    state_ref[WAVE : WAVE + 2] = jnp.concatenate([out_near, top], 0)

    first = iota((8, NY), 0)
    for z in range(NZ):
        for c in range(3):
            ghost = jnp.where(first == 7, xr_ref[c * NZ + z : c * NZ + z + 1], 0.0)
            if c:
                ghost = jnp.where(first == 0, xl_ref[(c - 1) * NZ + z : (c - 1) * NZ + z + 1], ghost)
            e_ref[c, z + 1, NX:] = ghost
    spread_currents(e_ref, where, gain * current)

    down_ref = sends[-1]
    down_ref[0:GX] = e_ref[0, 1]
    down_ref[GX : GX + NX] = e_ref[1, 1, :NX]
    down_ref[GX + NX :] = jnp.zeros((8, NY), F32)
    down_ref[GX + NX : GX + NX + 1, 0:LANES] = out_below
    if not last:
        up_ref = sends[0]
        up_ref[0:NX] = e_ref[0, NZ, :NX]
        up_ref[NX : 2 * NX] = e_ref[1, NZ, :NX]
        up_ref[2 * NX : 2 * NX + GX] = e_ref[2, NZ]
        up_ref[2 * NX + GX :] = jnp.zeros((8, NY), F32)
        up_ref[2 * NX + GX : 2 * NX + GX + 1, 0:LANES] = out_near


def new_h(e_ref, h_ref, layer, ex_above, ey_above):
    scale = jnp.where((iota((GX, 1), 0) >= NX) & (column() == 0), 0.0, 0.5)
    ex, ey, ez = e_ref[0, layer], e_ref[1, layer], e_ref[2, layer]
    if layer == 0:
        scale = jnp.where(row() == 0, 0.0, scale)
    hx = h_ref[0, layer] - scale * ((next_y(ez) - ez) - (ey_above - ey))
    hy = h_ref[1, layer] - scale * ((ex_above - ex) - (next_x(ez) - ez))
    hz = h_ref[2, layer] - scale * ((next_x(ey) - ey) - (next_y(ex) - ex))
    return hx, hy, hz


def update_h(e_ref, h_ref, layer):
    for c, value in enumerate(new_h(e_ref, h_ref, layer, e_ref[0, layer + 1], e_ref[1, layer + 1])):
        h_ref[c, layer] = value


def k_inner_h(e_ref, h_in, h_ref):
    for layer in range(1, NZ):
        update_h(e_ref, h_ref, layer)


def k_inner_last(e_ref, h_in, h_ref, e_out, h_out, sems):
    first = copies([(own_rows(e_ref), e_out)], sems)
    for layer in range(1, NZ):
        update_h(e_ref, h_ref, layer)
    second = pltpu.make_async_copy(h_ref.at[:, 1:NZ, 0:NX], h_out.at[:, 0 : NZ - 1], sems.at[1])
    second.start()
    wait(first)
    second.wait()


def k_volts(n, last, up_ref, down_ref, d_ref, g_ref, inverse_ref, cell_ref, e_in, h_in, state_in, e_ref, h_ref, state_ref, pay_ref, xr_ref, xl_ref, *volts_ref):
    at = n - 1 + DEPTH
    wave = down_ref[GX + NX : GX + NX + 1, 0:LANES] + state_ref[WAVE + 1 : WAVE + 2]
    state_ref[OWN + at : OWN + at + 1] = state_ref[WAVE : WAVE + 1]
    state_ref[FROM_ABOVE + at : FROM_ABOVE + at + 1] = wave
    state_ref[FROM_BELOW + at : FROM_BELOW + at + 1] = up_ref[2 * NX + GX : 2 * NX + GX + 1, 0:LANES]
    volts = next_volts(state_ref, inverse_ref, n)
    if last:
        volts_ref[0][...] = volts
    e_ref[0, 0, :NX] = up_ref[0:NX]
    e_ref[1, 0, :NX] = up_ref[NX : 2 * NX]
    e_ref[2, 0] = up_ref[2 * NX : 2 * NX + GX]
    e_ref[0, NZ + 1] = down_ref[0:GX]
    e_ref[1, NZ + 1, :NX] = down_ref[GX : GX + NX]
    update_h(e_ref, h_ref, 0)
    update_h(e_ref, h_ref, NZ)
    update_e(e_ref, h_ref, d_ref, g_ref)
    pre = at_ports(e_ref[2, 1 : NZ + 1, :NX].reshape(NZ * NX, NY), own_ports(cell_ref[...]))
    payload(pay_ref, volts, pre)
    send_x(e_ref, xr_ref, xl_ref)


def k_last(down_ref, state_ref, e_ref, h_ref, h_in, h_out, wave_out, layer_ref, sem):
    ey_above = jnp.concatenate([down_ref[GX : GX + NX], jnp.zeros((8, NY), F32)], 0)
    for c, value in enumerate(new_h(e_ref, h_ref, NZ, down_ref[0:GX], ey_above)):
        layer_ref[c] = value[:NX]
    copy = pltpu.make_async_copy(layer_ref, h_out.at[:, NZ - 1], sem)
    copy.start()
    above = down_ref[GX + NX : GX + NX + 1, 0:LANES] + state_ref[WAVE + 1 : WAVE + 2]
    wave_out[...] = jnp.concatenate([state_ref[WAVE : WAVE + 1], above], 0)[None]
    copy.wait()


def local(
    e_field,
    h_field,
    e_decay,
    e_gain,
    port_cell,
    port_node,
    port_conductance,
    inverse,
    line_near,
    line_far,
    line_delay,
    line_imped,
    hist_near,
    hist_far,
):
    hist_near = jnp.transpose(hist_near, (1, 0, 2))
    hist_far = jnp.transpose(hist_far, (1, 0, 2))
    hist_shape = pltpu.VMEM((DEPTH, 1, LANES), F32)
    line = pltpu.VMEM((1, LANES), F32)
    line_int = pltpu.VMEM((1, LANES), jnp.int32)
    ports_int = pltpu.VMEM((1, HALF), jnp.int32)
    block = pltpu.VMEM((NZ, NX, NY), F32)

    pay, up, right = call(
        k_first,
        [PAY_SHAPE, (2 * NX + 8, NY), (2 * NZ, NY)],
        e_field, h_field, port_cell, port_node, port_conductance, line_far, line_delay, line_imped, hist_near,
        far=range(9),
        scratch=[
            block, pltpu.VMEM((2, NZ, 8, NY), F32), ports_int, ports_int, pltpu.VMEM((1, HALF), F32),
            line_int, line_int, line, hist_shape, pltpu.SemaphoreType.DMA((11,)),
        ],
        name="first",
    )
    got = exchanged(pay)
    up = shifted(up, "fz", 1)
    right = shifted(right, "fxy", 1)
    e, h, pre, xr, xl = call(
        k_start,
        [E_SHAPE, H_SHAPE, (8, LANES), XR_SHAPE, XL_SHAPE],
        e_field, h_field, e_decay, e_gain, port_cell, up, right,
        far=range(5),
        scratch=[block, block, ports_int, pltpu.SemaphoreType.DMA((5,))],
        name="start",
    )
    pay, state = call(
        k_tables,
        [PAY_SHAPE, (ROWS, LANES)],
        got, up, pre, line_near, line_delay, line_imped, hist_near, hist_far, inverse,
        far=range(3, 9),
        scratch=[
            line_int, line_int, line, hist_shape, hist_shape,
            pltpu.VMEM((1, LANES, NB * LANES), F32), pltpu.SemaphoreType.DMA((6,)),
        ],
        name="tables",
    )
    for n in range(STEPS):
        last = n == STEPS - 1
        got = exchanged(pay)
        xr = shifted(xr, "fxy", 1)
        xl = shifted(xl, "fxy", -1)
        e, state, *sends = call(
            functools.partial(k_currents, n, last),
            [E_SHAPE, (ROWS, LANES)] + ([] if last else [UP_SHAPE]) + [DOWN_SHAPE],
            got, xr, xl, e, state,
            alias={3: 0, 4: 1},
            name="currents",
        )
        down = shifted(sends[-1], "fz", -1)
        if last:
            break
        up = shifted(sends[0], "fz", 1)
        (h,) = call(k_inner_h, [H_SHAPE], e, h, alias={1: 0}, name="inner_h")
        e, h, state, pay, xr, xl, *node_volt = call(
            functools.partial(k_volts, n + 1, n + 1 == STEPS - 1),
            [E_SHAPE, H_SHAPE, (ROWS, LANES), PAY_SHAPE, XR_SHAPE, XL_SHAPE] + ([(1, LANES)] if n + 1 == STEPS - 1 else []),
            up, down, e_decay, e_gain, inverse, port_cell, e, h, state,
            alias={6: 0, 7: 1, 8: 2},
            name="volts",
        )
    h, e_out, h_out = call(
        k_inner_last,
        [H_SHAPE, FIELD, FIELD],
        e, h,
        alias={1: 0},
        far_out=(1, 2),
        scratch=[pltpu.SemaphoreType.DMA((2,))],
        name="inner_last",
    )
    h_out, line_wave = call(
        k_last,
        [FIELD, (1, 2, LANES)],
        down, state, e, h, h_out,
        alias={4: 0},
        far=(4,),
        far_out=(0,),
        scratch=[pltpu.VMEM((3, NX, NY), F32), pltpu.SemaphoreType.DMA],
        name="last",
    )
    return e_out, h_out, node_volt[0], line_wave


def solution(mesh):
    placed = (
        P(None, "fz", "fxy", None),
        P(None, "fz", "fxy", None),
        P("fz", "fxy", None),
        P("fz", "fxy", None),
        P("fz", "fxy"),
        P("fz", "fxy"),
        P("fz", "fxy"),
        P("fz", "fxy", None),
        P("fz", None),
        P("fz", None),
        P("fz", None),
        P("fz", None),
        P("fz", None, None),
        P("fz", None, None),
    )
    return jax.shard_map(
        local,
        mesh=mesh,
        in_specs=placed,
        out_specs=(
            P(None, "fz", "fxy", None),
            P(None, "fz", "fxy", None),
            P("fz", "fxy"),
            P("fz", None, None),
        ),
        check_vma=False,
    )
```

time: 209 us -> 179 us (0.86)
  local copies, waits for them, and re-layouts: 45.6 us -> 12.3 us
  waiting for transfers between devices: 41.8 us -> 53.9 us
  starting transfers between devices: 104 us -> 96.1 us
    unnamed x146 -> x52, local copies, waits for them, and re-layouts: 44.4 us -> 12.3 us
    all_to_all x5, waiting for transfers between devices: 6.02 us -> 15.8 us  [exchanged(): return lax.all_to_all(value, 'fxy', 0, 0, tiled=True)]
    all_to_all x5, starting transfers between devices: 58.6 us -> 51.7 us  [exchanged(): return lax.all_to_all(value, 'fxy', 0, 0, tiled=True)]
    ppermute x17, waiting for transfers between devices: 35.7 us -> 38.1 us  [shifted(): return lax.ppermute(value, axis, pairs)]
    pallas_call x19 -> x15, Pallas kernels: 14.2 us -> 14 us  [call(): pl.pallas_call(kernel, out_shape=[jax.ShapeDtypeStruct(s, F32) for s in o...]
  transfers between devices with their start and end apart: 22 -> 22, of which waited for: 13 -> 14; matrix products, arithmetic and copies ran while one was open for 1% -> 0% of each run, Pallas kernels for 1% -> 2%
where the time goes in v2:
time: 179 us; the launch traced here: 177 us
  starting transfers between devices  96.1 us (54%)
  waiting for transfers between devices  53.9 us (30%)
  Pallas kernels  14 us (8%)
  local copies, waits for them, and re-layouts  12.3 us (7%)
    all_to_all x5, starting transfers between devices, exchanged(): return lax.all_to_all(value, 'fxy', 0, 0, tiled=True)  51.7 us
    ppermute x17, starting transfers between devices, shifted(): return lax.ppermute(value, axis, pairs)  44.5 us
    ppermute x17, waiting for transfers between devices, shifted(): return lax.ppermute(value, axis, pairs)  38.1 us
    all_to_all x5, waiting for transfers between devices, exchanged(): return lax.all_to_all(value, 'fxy', 0, 0, tiled=True)  15.8 us
    pallas_call x15, Pallas kernels, call(): pl.pallas_call(kernel, out_shape=[jax.ShapeDtypeStruct(s, F32) for s in o...  14 us
    unnamed x52, local copies, waits for them, and re-layouts  12.3 us
  transfers between devices with their start and end apart: 22, of which 14 were waited for; matrix products, arithmetic and copies ran while one was open for 0% of the time, Pallas kernels for 2%

profile of v2, /device:TPU:7, one launch (start us, length us, event | category | flops | bytes accessed | tf_op | source)
XLA Modules:
  0.0 177.4 jit_solution(17179535981828112516)
XLA Ops:
  0.7 1.2 copy-done.6
  1.8 1.1 copy-done.8
  3.0 0.7 copy-done.10
  3.6 0.7 copy-done.12
  4.3 0.7 copy-done.15
  5.0 0.7 copy-done.17
  5.6 0.7 copy-done.20
  6.3 0.7 copy-done.21
  6.9 0.7 copy-done.22
  7.6 1.3 first.1
  8.9 3.8 %collective-permute-start = (f32[40,512]{1,0:T(8,128)S(1)}, f32[40,512]{1,0:T(8,128)S(1)}, u32[]{:S(2)}, u32[]{:S(2)}) collective-permute-start(f32[40,512]{1,0:T(8,128)S(1)} %get-tuple-element.54), channel_id=1, source_target_pairs={{0,16},{16,32},{32,48},{48,64},{64,80},{80,96},{96,112},{112,128},... | collective-permute-start | bytes 245768 | tf_op jit(solution)/shard_map/ppermute | solution.py:50
  12.8 14.9 %all-to-all-start = ((f32[16,2,128]{2,1,0:T(2,128)}), f32[16,2,128]{2,1,0:T(2,128)S(1)}, u32[]{:S(2)}, u32[]{:S(2)}) async-start(f32[16,2,128]{2,1,0:T(2,128)} %get-tuple-element.53), calls=%async_computation | async-start | bytes 32768 | tf_op jit(solution)/shard_map/all_to_all | solution.py:54
  27.7 3.3 %collective-permute-start.1 = (f32[16,512]{1,0:T(8,128)S(1)}, f32[16,512]{1,0:T(8,128)S(1)}, u32[]{:S(2)}, u32[]{:S(2)}) collective-permute-start(f32[16,512]{1,0:T(8,128)S(1)} %get-tuple-element.55), channel_id=1, source_target_pairs={{0,1},{1,2},{2,3},{3,4},{4,5},{5,6},{6,7},{7,8},{8,9},{9,10},{10,1... | collective-permute-start | bytes 98312 | tf_op jit(solution)/shard_map/ppermute | solution.py:50
  31.0 1.2 collective-permute-done.1.right_ref
  32.2 1.1 copy-done.7
  33.3 1.1 copy-done.9
  34.5 0.9 start.1
  35.4 0.6 copy-done.23
  36.0 3.1 %all-to-all-done.got_ref = f32[16,2,128]{2,1,0:T(2,128)S(1)} async-done(((f32[16,2,128]{2,1,0:T(2,128)}), f32[16,2,128]{2,1,0:T(2,128)S(1)}, u32[]{:S(2)}, u32[]{:S(2)}) %all-to-all-start) | async-done | bytes 16416 | tf_op jit(solution)/shard_map/all_to_all | solution.py:54
  39.1 1.2 copy-done
  40.3 1.3 tables.1
  41.6 10.3 %all-to-all-start.1 = ((f32[16,2,128]{2,1,0:T(2,128)}), f32[16,2,128]{2,1,0:T(2,128)S(1)}, u32[]{:S(2)}, u32[]{:S(2)}) async-start(f32[16,2,128]{2,1,0:T(2,128)} %get-tuple-element.57), calls=%async_computation.1 | async-start | bytes 32768 | tf_op jit(solution)/shard_map/all_to_all | solution.py:54
  51.9 3.3 %collective-permute-start.2 = (f32[24,512]{1,0:T(8,128)}, f32[24,512]{1,0:T(8,128)S(1)}, u32[]{:S(2)}, u32[]{:S(2)}) collective-permute-start(f32[24,512]{1,0:T(8,128)} %copy-done.23), channel_id=1, source_target_pairs={{0,1},{1,2},{2,3},{3,4},{4,5},{5,6},{6,7},{7,8},{8,9},{9,10},{10,1... | collective-permute-start | bytes 147464 | tf_op jit(solution)/shard_map/ppermute | solution.py:50
  55.2 1.3 collective-permute-start.3
  56.5 3.7 %collective-permute-done.3.xl_ref = f32[16,512]{1,0:T(8,128)S(1)} collective-permute-done((f32[16,512]{1,0:T(8,128)S(1)}, f32[16,512]{1,0:T(8,128)S(1)}, u32[]{:S(2)}, u32[]{:S(2)}) %collective-permute-start.3) | collective-permute-done | bytes 32800 | tf_op jit(solution)/shard_map/ppermute | solution.py:50
  60.2 3.1 %all-to-all-done.1.got_ref = f32[16,2,128]{2,1,0:T(2,128)S(1)} async-done(((f32[16,2,128]{2,1,0:T(2,128)}), f32[16,2,128]{2,1,0:T(2,128)S(1)}, u32[]{:S(2)}, u32[]{:S(2)}) %all-to-all-start.1) | async-done | bytes 16416 | tf_op jit(solution)/shard_map/all_to_all | solution.py:54
  63.3 0.8 currents.4
  64.1 4.9 %collective-permute-start.4 = (f32[64,512]{1,0:T(8,128)S(1)}, f32[64,512]{1,0:T(8,128)S(1)}, u32[]{:S(2)}, u32[]{:S(2)}) collective-permute-start(f32[64,512]{1,0:T(8,128)S(1)} %get-tuple-element.62), channel_id=1, source_target_pairs={{0,16},{16,32},{32,48},{48,64},{64,80},{80,96},{96,112},{112,128},... | collective-permute-start | bytes 393224 | tf_op jit(solution)/shard_map/ppermute | solution.py:50
  69.0 1.9 %collective-permute-start.5 = (f32[48,512]{1,0:T(8,128)S(1)}, f32[48,512]{1,0:T(8,128)S(1)}, u32[]{:S(2)}, u32[]{:S(2)}) collective-permute-start(f32[48,512]{1,0:T(8,128)S(1)} %get-tuple-element.63), channel_id=1, source_target_pairs={{16,0},{32,16},{48,32},{64,48},{80,64},{96,80},{112,96},{128,112},... | collective-permute-start | bytes 294920 | tf_op jit(solution)/shard_map/ppermute | solution.py:50
  70.9 0.3 inner_h.3.h_in
  71.2 5.8 %collective-permute-done.5.down_ref = f32[48,512]{1,0:T(8,128)S(1)} collective-permute-done((f32[48,512]{1,0:T(8,128)S(1)}, f32[48,512]{1,0:T(8,128)S(1)}, u32[]{:S(2)}, u32[]{:S(2)}) %collective-permute-start.5) | collective-permute-done | bytes 98336 | tf_op jit(solution)/shard_map/ppermute | solution.py:50
  77.0 1.4 volts.3
  78.5 0.6 copy-done.24
  79.1 8.6 %all-to-all-start.2 = ((f32[16,2,128]{2,1,0:T(2,128)}), f32[16,2,128]{2,1,0:T(2,128)S(1)}, u32[]{:S(2)}, u32[]{:S(2)}) async-start(f32[16,2,128]{2,1,0:T(2,128)} %get-tuple-element.67), calls=%async_computation.2 | async-start | bytes 32768 | tf_op jit(solution)/shard_map/all_to_all | solution.py:54
  87.7 3.3 %collective-permute-start.6 = (f32[24,512]{1,0:T(8,128)S(1)}, f32[24,512]{1,0:T(8,128)S(1)}, u32[]{:S(2)}, u32[]{:S(2)}) collective-permute-start(f32[24,512]{1,0:T(8,128)S(1)} %get-tuple-element.68), channel_id=1, source_target_pairs={{0,1},{1,2},{2,3},{3,4},{4,5},{5,6},{6,7},{7,8},{8,9},{9,10},{10,1... | collective-permute-start | bytes 147464 | tf_op jit(solution)/shard_map/ppermute | solution.py:50
  91.0 1.3 collective-permute-start.7
  92.3 3.9 %collective-permute-done.7.xl_ref = f32[16,512]{1,0:T(8,128)S(1)} collective-permute-done((f32[16,512]{1,0:T(8,128)}, f32[16,512]{1,0:T(8,128)S(1)}, u32[]{:S(2)}, u32[]{:S(2)}) %collective-permute-start.7) | collective-permute-done | bytes 32800 | tf_op jit(solution)/shard_map/ppermute | solution.py:50
  96.2 2.9 %all-to-all-done.2.got_ref = f32[16,2,128]{2,1,0:T(2,128)S(1)} async-done(((f32[16,2,128]{2,1,0:T(2,128)}), f32[16,2,128]{2,1,0:T(2,128)S(1)}, u32[]{:S(2)}, u32[]{:S(2)}) %all-to-all-start.2) | async-done | bytes 16416 | tf_op jit(solution)/shard_map/all_to_all | solution.py:54
  99.0 0.7 currents.5
  99.8 3.3 %collective-permute-start.8 = (f32[64,512]{1,0:T(8,128)S(1)}, f32[64,512]{1,0:T(8,128)S(1)}, u32[]{:S(2)}, u32[]{:S(2)}) collective-permute-start(f32[64,512]{1,0:T(8,128)S(1)} %get-tuple-element.72), channel_id=1, source_target_pairs={{0,16},{16,32},{32,48},{48,64},{64,80},{80,96},{96,112},{112,128},... | collective-permute-start | bytes 393224 | tf_op jit(solution)/shard_map/ppermute | solution.py:50
  103.1 1.9 %collective-permute-start.9 = (f32[48,512]{1,0:T(8,128)S(1)}, f32[48,512]{1,0:T(8,128)S(1)}, u32[]{:S(2)}, u32[]{:S(2)}) collective-permute-start(f32[48,512]{1,0:T(8,128)S(1)} %get-tuple-element.73), channel_id=1, source_target_pairs={{16,0},{32,16},{48,32},{64,48},{80,64},{96,80},{112,96},{128,112},... | collective-permute-start | bytes 294920 | tf_op jit(solution)/shard_map/ppermute | solution.py:50
  105.3 5.8 %collective-permute-done.9.down_ref = f32[48,512]{1,0:T(8,128)S(1)} collective-permute-done((f32[48,512]{1,0:T(8,128)S(1)}, f32[48,512]{1,0:T(8,128)S(1)}, u32[]{:S(2)}, u32[]{:S(2)}) %collective-permute-start.9) | collective-permute-done | bytes 98336 | tf_op jit(solution)/shard_map/ppermute | solution.py:50
  111.2 1.4 volts.4
  112.6 0.6 copy-done.25
  113.2 8.9 %all-to-all-start.3 = ((f32[16,2,128]{2,1,0:T(2,128)}), f32[16,2,128]{2,1,0:T(2,128)S(1)}, u32[]{:S(2)}, u32[]{:S(2)}) async-start(f32[16,2,128]{2,1,0:T(2,128)} %get-tuple-element.77), calls=%async_computation.3 | async-start | bytes 32768 | tf_op jit(solution)/shard_map/all_to_all | solution.py:54
  122.1 3.3 %collective-permute-start.10 = (f32[24,512]{1,0:T(8,128)S(1)}, f32[24,512]{1,0:T(8,128)S(1)}, u32[]{:S(2)}, u32[]{:S(2)}) collective-permute-start(f32[24,512]{1,0:T(8,128)S(1)} %get-tuple-element.78), channel_id=1, source_target_pairs={{0,1},{1,2},{2,3},{3,4},{4,5},{5,6},{6,7},{7,8},{8,9},{9,10},{10,1... | collective-permute-start | bytes 147464 | tf_op jit(solution)/shard_map/ppermute | solution.py:50
  125.4 1.3 collective-permute-start.11
  126.7 3.6 %collective-permute-done.11.xl_ref = f32[16,512]{1,0:T(8,128)S(1)} collective-permute-done((f32[16,512]{1,0:T(8,128)}, f32[16,512]{1,0:T(8,128)S(1)}, u32[]{:S(2)}, u32[]{:S(2)}) %collective-permute-start.11) | collective-permute-done | bytes 32800 | tf_op jit(solution)/shard_map/ppermute | solution.py:50
  130.3 3.3 %all-to-all-done.3.got_ref = f32[16,2,128]{2,1,0:T(2,128)S(1)} async-done(((f32[16,2,128]{2,1,0:T(2,128)}), f32[16,2,128]{2,1,0:T(2,128)S(1)}, u32[]{:S(2)}, u32[]{:S(2)}) %all-to-all-start.3) | async-done | bytes 16416 | tf_op jit(solution)/shard_map/all_to_all | solution.py:54
  133.5 0.7 currents.6
  134.3 3.3 %collective-permute-start.12 = (f32[64,512]{1,0:T(8,128)S(1)}, f32[64,512]{1,0:T(8,128)S(1)}, u32[]{:S(2)}, u32[]{:S(2)}) collective-permute-start(f32[64,512]{1,0:T(8,128)S(1)} %get-tuple-element.82), channel_id=1, source_target_pairs={{0,16},{16,32},{32,48},{48,64},{64,80},{80,96},{96,112},{112,128},... | collective-permute-start | bytes 393224 | tf_op jit(solution)/shard_map/ppermute | solution.py:50
  137.6 1.9 %collective-permute-start.13 = (f32[48,512]{1,0:T(8,128)S(1)}, f32[48,512]{1,0:T(8,128)S(1)}, u32[]{:S(2)}, u32[]{:S(2)}) collective-permute-start(f32[48,512]{1,0:T(8,128)S(1)} %get-tuple-element.83), channel_id=1, source_target_pairs={{16,0},{32,16},{48,32},{64,48},{80,64},{96,80},{112,96},{128,112},... | collective-permute-start | bytes 294920 | tf_op jit(solution)/shard_map/ppermute | solution.py:50
  139.8 5.8 %collective-permute-done.13.down_ref = f32[48,512]{1,0:T(8,128)S(1)} collective-permute-done((f32[48,512]{1,0:T(8,128)S(1)}, f32[48,512]{1,0:T(8,128)S(1)}, u32[]{:S(2)}, u32[]{:S(2)}) %collective-permute-start.13) | collective-permute-done | bytes 98336 | tf_op jit(solution)/shard_map/ppermute | solution.py:50
  145.6 1.5 volts.5
  147.1 8.9 %all-to-all-start.4 = ((f32[16,2,128]{2,1,0:T(2,128)}), f32[16,2,128]{2,1,0:T(2,128)S(1)}, u32[]{:S(2)}, u32[]{:S(2)}) async-start(f32[16,2,128]{2,1,0:T(2,128)} %get-tuple-element.87), calls=%async_computation.4 | async-start | bytes 32768 | tf_op jit(solution)/shard_map/all_to_all | solution.py:54
  156.0 3.3 %collective-permute-start.14 = (f32[24,512]{1,0:T(8,128)S(1)}, f32[24,512]{1,0:T(8,128)S(1)}, u32[]{:S(2)}, u32[]{:S(2)}) collective-permute-start(f32[24,512]{1,0:T(8,128)S(1)} %get-tuple-element.88), channel_id=1, source_target_pairs={{0,1},{1,2},{2,3},{3,4},{4,5},{5,6},{6,7},{7,8},{8,9},{9,10},{10,1... | collective-permute-start | bytes 147464 | tf_op jit(solution)/shard_map/ppermute | solution.py:50
  159.2 1.3 collective-permute-start.15
  160.5 3.4 %collective-permute-done.15.xl_ref = f32[16,512]{1,0:T(8,128)S(1)} collective-permute-done((f32[16,512]{1,0:T(8,128)S(1)}, f32[16,512]{1,0:T(8,128)S(1)}, u32[]{:S(2)}, u32[]{:S(2)}) %collective-permute-start.15) | collective-permute-done | bytes 32800 | tf_op jit(solution)/shard_map/ppermute | solution.py:50
  163.9 3.5 %all-to-all-done.4.got_ref = f32[16,2,128]{2,1,0:T(2,128)S(1)} async-done(((f32[16,2,128]{2,1,0:T(2,128)}), f32[16,2,128]{2,1,0:T(2,128)S(1)}, u32[]{:S(2)}, u32[]{:S(2)}) %all-to-all-start.4) | async-done | bytes 16416 | tf_op jit(solution)/shard_map/all_to_all | solution.py:54
  167.3 0.7 currents.7
  168.1 1.9 %collective-permute-start.16 = (f32[48,512]{1,0:T(8,128)S(1)}, f32[48,512]{1,0:T(8,128)S(1)}, u32[]{:S(2)}, u32[]{:S(2)}) collective-permute-start(f32[48,512]{1,0:T(8,128)S(1)} %get-tuple-element.95), channel_id=1, source_target_pairs={{16,0},{32,16},{48,32},{64,48},{80,64},{96,80},{112,96},{128,112},... | collective-permute-start | bytes 294920 | tf_op jit(solution)/shard_map/ppermute | solution.py:50
  170.0 1.2 inner_last.1
  171.2 5.0 %collective-permute-done.16.down_ref = f32[48,512]{1,0:T(8,128)S(1)} collective-permute-done((f32[48,512]{1,0:T(8,128)S(1)}, f32[48,512]{1,0:T(8,128)S(1)}, u32[]{:S(2)}, u32[]{:S(2)}) %collective-permute-start.16) | collective-permute-done | bytes 98336 | tf_op jit(solution)/shard_map/ppermute | solution.py:50
  176.1 1.3 last.1
  (47 shorter events, 0.7 us)
Async XLA Ops:
  0.6 31.6 %copy-start.5 = (f32[8,16,512]{2,1,0:T(8,128)S(1)}, f32[8,16,512]{2,1,0:T(8,128)}, u32[]{:S(2)}) copy-start(f32[8,16,512]{2,1,0:T(8,128)} %g_ref.5) | copy-start | bytes 786436
  0.6 31.6 %copy-start.4 = (f32[8,16,512]{2,1,0:T(8,128)S(1)}, f32[8,16,512]{2,1,0:T(8,128)}, u32[]{:S(2)}) copy-start(f32[8,16,512]{2,1,0:T(8,128)} %d_ref.5) | copy-start | bytes 786436
  0.7 1.2 copy-start.6
  1.8 1.1 copy-start.8
  3.0 0.7 copy-start.10
  3.6 0.7 copy-start.12
  4.3 0.7 copy-start.15
  5.0 0.7 copy-start.17
  5.6 0.7 copy-start.20
  6.3 0.7 copy-start.21
  6.9 0.7 copy-start.22
  7.6 24.6 %copy-start.11 = (s32[1,64]{1,0:T(1,128)S(1)}, s32[1,64]{1,0:T(1,128)}, u32[]{:S(2)}) copy-start(s32[1,64]{1,0:T(1,128)} %cell_ref.7) | copy-start | bytes 772
  8.9 30.2 %copy-start.13 = (f32[1,6,128]{2,0,1:T(1,128)S(1)}, f32[1,6,128]{2,0,1:T(1,128)}, u32[]{:S(2)}) copy-start(f32[1,6,128]{2,0,1:T(1,128)} %param.26) | copy-start | bytes 9220
  8.9 30.1 %copy-start.14 = (f32[1,6,128]{2,0,1:T(1,128)S(1)}, f32[1,6,128]{2,0,1:T(1,128)}, u32[]{:S(2)}) copy-start(f32[1,6,128]{2,0,1:T(1,128)} %param.27) | copy-start | bytes 9220
  8.9 30.1 %copy-start.16 = (s32[1,128]{1,0:T(1,128)S(1)}, s32[1,128]{1,0:T(1,128)}, u32[]{:S(2)}) copy-start(s32[1,128]{1,0:T(1,128)} %delay_in.1) | copy-start | bytes 1540
  8.9 30.1 %copy-start.18 = (f32[1,128]{1,0:T(1,128)S(1)}, f32[1,128]{1,0:T(1,128)}, u32[]{:S(2)}) copy-start(f32[1,128]{1,0:T(1,128)} %imped_in.1) | copy-start | bytes 1540
  8.9 30.1 %copy-start.19 = (s32[1,128]{1,0:T(1,128)S(1)}, s32[1,128]{1,0:T(1,128)}, u32[]{:S(2)}) copy-start(s32[1,128]{1,0:T(1,128)} %near_in.1) | copy-start | bytes 1540
  8.9 23.2 %collective-permute-start = (f32[40,512]{1,0:T(8,128)S(1)}, f32[40,512]{1,0:T(8,128)S(1)}, u32[]{:S(2)}, u32[]{:S(2)}) collective-permute-start(f32[40,512]{1,0:T(8,128)S(1)} %get-tuple-element.54), channel_id=1, source_target_pairs={{0,16},{16,32},{32,48},{48,64},{64,80},{80,96},{96,112},{112,128},... | collective-permute-start | bytes 245768 | tf_op jit(solution)/shard_map/ppermute | solution.py:50
  12.8 26.3 %all-to-all-start = ((f32[16,2,128]{2,1,0:T(2,128)}), f32[16,2,128]{2,1,0:T(2,128)S(1)}, u32[]{:S(2)}, u32[]{:S(2)}) async-start(f32[16,2,128]{2,1,0:T(2,128)} %get-tuple-element.53), calls=%async_computation | async-start | bytes 32768 | tf_op jit(solution)/shard_map/all_to_all | solution.py:54
  27.7 4.5 %collective-permute-start.1 = (f32[16,512]{1,0:T(8,128)S(1)}, f32[16,512]{1,0:T(8,128)S(1)}, u32[]{:S(2)}, u32[]{:S(2)}) collective-permute-start(f32[16,512]{1,0:T(8,128)S(1)} %get-tuple-element.55), channel_id=1, source_target_pairs={{0,1},{1,2},{2,3},{3,4},{4,5},{5,6},{6,7},{7,8},{8,9},{9,10},{10,1... | collective-permute-start | bytes 98312 | tf_op jit(solution)/shard_map/ppermute | solution.py:50
  32.2 1.1 copy-start.7
  33.3 1.1 copy-start.9
  35.3 0.6 copy-start.23
  39.1 1.2 copy-start
  41.6 21.7 %all-to-all-start.1 = ((f32[16,2,128]{2,1,0:T(2,128)}), f32[16,2,128]{2,1,0:T(2,128)S(1)}, u32[]{:S(2)}, u32[]{:S(2)}) async-start(f32[16,2,128]{2,1,0:T(2,128)} %get-tuple-element.57), calls=%async_computation.1 | async-start | bytes 32768 | tf_op jit(solution)/shard_map/all_to_all | solution.py:54
  51.9 8.3 %collective-permute-start.2 = (f32[24,512]{1,0:T(8,128)}, f32[24,512]{1,0:T(8,128)S(1)}, u32[]{:S(2)}, u32[]{:S(2)}) collective-permute-start(f32[24,512]{1,0:T(8,128)} %copy-done.23), channel_id=1, source_target_pairs={{0,1},{1,2},{2,3},{3,4},{4,5},{5,6},{6,7},{7,8},{8,9},{9,10},{10,1... | collective-permute-start | bytes 147464 | tf_op jit(solution)/shard_map/ppermute | solution.py:50
  55.2 5.0 %collective-permute-start.3 = (f32[16,512]{1,0:T(8,128)S(1)}, f32[16,512]{1,0:T(8,128)S(1)}, u32[]{:S(2)}, u32[]{:S(2)}) collective-permute-start(f32[16,512]{1,0:T(8,128)S(1)} %get-tuple-element.59), channel_id=1, source_target_pairs={{1,0},{2,1},{3,2},{4,3},{5,4},{6,5},{7,6},{8,7},{9,8},{10,9},{11,1... | collective-permute-start | bytes 98312 | tf_op jit(solution)/shard_map/ppermute | solution.py:50
  64.1 12.9 %collective-permute-start.4 = (f32[64,512]{1,0:T(8,128)S(1)}, f32[64,512]{1,0:T(8,128)S(1)}, u32[]{:S(2)}, u32[]{:S(2)}) collective-permute-start(f32[64,512]{1,0:T(8,128)S(1)} %get-tuple-element.62), channel_id=1, source_target_pairs={{0,16},{16,32},{32,48},{48,64},{64,80},{80,96},{96,112},{112,128},... | collective-permute-start | bytes 393224 | tf_op jit(solution)/shard_map/ppermute | solution.py:50
  69.0 8.0 %collective-permute-start.5 = (f32[48,512]{1,0:T(8,128)S(1)}, f32[48,512]{1,0:T(8,128)S(1)}, u32[]{:S(2)}, u32[]{:S(2)}) collective-permute-start(f32[48,512]{1,0:T(8,128)S(1)} %get-tuple-element.63), channel_id=1, source_target_pairs={{16,0},{32,16},{48,32},{64,48},{80,64},{96,80},{112,96},{128,112},... | collective-permute-start | bytes 294920 | tf_op jit(solution)/shard_map/ppermute | solution.py:50
  70.9 6.1 %copy-start.1 = (f32[1,128,2048]{2,1,0:T(8,128)S(1)}, f32[1,128,2048]{2,1,0:T(8,128)}, u32[]{:S(2)}) copy-start(f32[1,128,2048]{2,1,0:T(8,128)} %inverse_ref.5) | copy-start | bytes 3145732
  78.5 0.6 copy-start.24
  79.1 20.0 %all-to-all-start.2 = ((f32[16,2,128]{2,1,0:T(2,128)}), f32[16,2,128]{2,1,0:T(2,128)S(1)}, u32[]{:S(2)}, u32[]{:S(2)}) async-start(f32[16,2,128]{2,1,0:T(2,128)} %get-tuple-element.67), calls=%async_computation.2 | async-start | bytes 32768 | tf_op jit(solution)/shard_map/all_to_all | solution.py:54
  87.7 8.4 %collective-permute-start.6 = (f32[24,512]{1,0:T(8,128)S(1)}, f32[24,512]{1,0:T(8,128)S(1)}, u32[]{:S(2)}, u32[]{:S(2)}) collective-permute-start(f32[24,512]{1,0:T(8,128)S(1)} %get-tuple-element.68), channel_id=1, source_target_pairs={{0,1},{1,2},{2,3},{3,4},{4,5},{5,6},{6,7},{7,8},{8,9},{9,10},{10,1... | collective-permute-start | bytes 147464 | tf_op jit(solution)/shard_map/ppermute | solution.py:50
  91.0 5.2 %collective-permute-start.7 = (f32[16,512]{1,0:T(8,128)}, f32[16,512]{1,0:T(8,128)S(1)}, u32[]{:S(2)}, u32[]{:S(2)}) collective-permute-start(f32[16,512]{1,0:T(8,128)} %copy-done.24), channel_id=1, source_target_pairs={{1,0},{2,1},{3,2},{4,3},{5,4},{6,5},{7,6},{8,7},{9,8},{10,9},{11,1... | collective-permute-start | bytes 98312 | tf_op jit(solution)/shard_map/ppermute | solution.py:50
  99.8 11.4 %collective-permute-start.8 = (f32[64,512]{1,0:T(8,128)S(1)}, f32[64,512]{1,0:T(8,128)S(1)}, u32[]{:S(2)}, u32[]{:S(2)}) collective-permute-start(f32[64,512]{1,0:T(8,128)S(1)} %get-tuple-element.72), channel_id=1, source_target_pairs={{0,16},{16,32},{32,48},{48,64},{64,80},{80,96},{96,112},{112,128},... | collective-permute-start | bytes 393224 | tf_op jit(solution)/shard_map/ppermute | solution.py:50
  103.1 8.0 %collective-permute-start.9 = (f32[48,512]{1,0:T(8,128)S(1)}, f32[48,512]{1,0:T(8,128)S(1)}, u32[]{:S(2)}, u32[]{:S(2)}) collective-permute-start(f32[48,512]{1,0:T(8,128)S(1)} %get-tuple-element.73), channel_id=1, source_target_pairs={{16,0},{32,16},{48,32},{64,48},{80,64},{96,80},{112,96},{128,112},... | collective-permute-start | bytes 294920 | tf_op jit(solution)/shard_map/ppermute | solution.py:50
  105.0 6.1 %copy-start.2 = (f32[1,128,2048]{2,1,0:T(8,128)S(1)}, f32[1,128,2048]{2,1,0:T(8,128)}, u32[]{:S(2)}) copy-start(f32[1,128,2048]{2,1,0:T(8,128)} %inverse_ref.5) | copy-start | bytes 3145732
  112.6 0.6 copy-start.25
  113.2 20.3 %all-to-all-start.3 = ((f32[16,2,128]{2,1,0:T(2,128)}), f32[16,2,128]{2,1,0:T(2,128)S(1)}, u32[]{:S(2)}, u32[]{:S(2)}) async-start(f32[16,2,128]{2,1,0:T(2,128)} %get-tuple-element.77), calls=%async_computation.3 | async-start | bytes 32768 | tf_op jit(solution)/shard_map/all_to_all | solution.py:54
  122.1 8.1 %collective-permute-start.10 = (f32[24,512]{1,0:T(8,128)S(1)}, f32[24,512]{1,0:T(8,128)S(1)}, u32[]{:S(2)}, u32[]{:S(2)}) collective-permute-start(f32[24,512]{1,0:T(8,128)S(1)} %get-tuple-element.78), channel_id=1, source_target_pairs={{0,1},{1,2},{2,3},{3,4},{4,5},{5,6},{6,7},{7,8},{8,9},{9,10},{10,1... | collective-permute-start | bytes 147464 | tf_op jit(solution)/shard_map/ppermute | solution.py:50
  125.4 4.9 %collective-permute-start.11 = (f32[16,512]{1,0:T(8,128)}, f32[16,512]{1,0:T(8,128)S(1)}, u32[]{:S(2)}, u32[]{:S(2)}) collective-permute-start(f32[16,512]{1,0:T(8,128)} %copy-done.25), channel_id=1, source_target_pairs={{1,0},{2,1},{3,2},{4,3},{5,4},{6,5},{7,6},{8,7},{9,8},{10,9},{11,1... | collective-permute-start | bytes 98312 | tf_op jit(solution)/shard_map/ppermute | solution.py:50
  134.3 11.3 %collective-permute-start.12 = (f32[64,512]{1,0:T(8,128)S(1)}, f32[64,512]{1,0:T(8,128)S(1)}, u32[]{:S(2)}, u32[]{:S(2)}) collective-permute-start(f32[64,512]{1,0:T(8,128)S(1)} %get-tuple-element.82), channel_id=1, source_target_pairs={{0,16},{16,32},{32,48},{48,64},{64,80},{80,96},{96,112},{112,128},... | collective-permute-start | bytes 393224 | tf_op jit(solution)/shard_map/ppermute | solution.py:50
  137.6 8.0 %collective-permute-start.13 = (f32[48,512]{1,0:T(8,128)S(1)}, f32[48,512]{1,0:T(8,128)S(1)}, u32[]{:S(2)}, u32[]{:S(2)}) collective-permute-start(f32[48,512]{1,0:T(8,128)S(1)} %get-tuple-element.83), channel_id=1, source_target_pairs={{16,0},{32,16},{48,32},{64,48},{80,64},{96,80},{112,96},{128,112},... | collective-permute-start | bytes 294920 | tf_op jit(solution)/shard_map/ppermute | solution.py:50
  139.5 6.1 %copy-start.3 = (f32[1,128,2048]{2,1,0:T(8,128)S(1)}, f32[1,128,2048]{2,1,0:T(8,128)}, u32[]{:S(2)}) copy-start(f32[1,128,2048]{2,1,0:T(8,128)} %inverse_ref.5) | copy-start | bytes 3145732
  147.1 20.3 %all-to-all-start.4 = ((f32[16,2,128]{2,1,0:T(2,128)}), f32[16,2,128]{2,1,0:T(2,128)S(1)}, u32[]{:S(2)}, u32[]{:S(2)}) async-start(f32[16,2,128]{2,1,0:T(2,128)} %get-tuple-element.87), calls=%async_computation.4 | async-start | bytes 32768 | tf_op jit(solution)/shard_map/all_to_all | solution.py:54
  156.0 7.9 %collective-permute-start.14 = (f32[24,512]{1,0:T(8,128)S(1)}, f32[24,512]{1,0:T(8,128)S(1)}, u32[]{:S(2)}, u32[]{:S(2)}) collective-permute-start(f32[24,512]{1,0:T(8,128)S(1)} %get-tuple-element.88), channel_id=1, source_target_pairs={{0,1},{1,2},{2,3},{3,4},{4,5},{5,6},{6,7},{7,8},{8,9},{9,10},{10,1... | collective-permute-start | bytes 147464 | tf_op jit(solution)/shard_map/ppermute | solution.py:50
  159.2 4.7 %collective-permute-start.15 = (f32[16,512]{1,0:T(8,128)S(1)}, f32[16,512]{1,0:T(8,128)S(1)}, u32[]{:S(2)}, u32[]{:S(2)}) collective-permute-start(f32[16,512]{1,0:T(8,128)S(1)} %get-tuple-element.89), channel_id=1, source_target_pairs={{1,0},{2,1},{3,2},{4,3},{5,4},{6,5},{7,6},{8,7},{9,8},{10,9},{11,1... | collective-permute-start | bytes 98312 | tf_op jit(solution)/shard_map/ppermute | solution.py:50
  168.1 8.0 %collective-permute-start.16 = (f32[48,512]{1,0:T(8,128)S(1)}, f32[48,512]{1,0:T(8,128)S(1)}, u32[]{:S(2)}, u32[]{:S(2)}) collective-permute-start(f32[48,512]{1,0:T(8,128)S(1)} %get-tuple-element.95), channel_id=1, source_target_pairs={{16,0},{32,16},{48,32},{64,48},{80,64},{96,80},{112,96},{128,112},... | collective-permute-start | bytes 294920 | tf_op jit(solution)/shard_map/ppermute | solution.py:50

commit v3 on v2

--- a/solution.py
+++ b/solution.py
@@ -14,24 +14,27 @@
 NX = 16
 NY = 512
 GX = 24
+DEEP = 4
 NF = 32
 NB = 16
 HALF = 64
 LANES = 128
 DEPTH = 6
 VMEM = pl.BlockSpec(memory_space=pltpu.VMEM)
-ANY = pl.BlockSpec(memory_space=pl.ANY)
+ANY = pl.BlockSpec(memory_space=pltpu.HBM)
 NT = (((1,), (1,)), ((), ()))
 NODE, WHERE, COND, GAIN, EZ, STATIC, OWN, FROM_ABOVE, FROM_BELOW, WAVE, ROWS = 0, 16, 24, 32, 40, 48, 56, 72, 88, 104, 112
 E_SHAPE = (3, NZ + 2, GX, NY)
 H_SHAPE = (3, NZ + 1, GX, NY)
 PAY_SHAPE = (NB, 2, LANES)
-XR_SHAPE, XL_SHAPE = (3 * NZ, NY), (2 * NZ, NY)
-UP_SHAPE, DOWN_SHAPE = (2 * NX + GX + 8, NY), (NX + GX + 8, NY)
+LAYERS = 8 * NZ + 2
+SIDE_SHAPE = (LAYERS * DEEP, NY)
+WIDE = (NZ, GX, NY)
+UP_SHAPE, DOWN_SHAPE = (3 * GX + 8, NY), (2 * GX + 8, NY)
 FIELD = (3, NZ, NX, NY)
 
 
-def call(kernel, outs, *args, alias=None, name=None, far=(), far_out=(), scratch=()):
+def call(kernel, outs, *args, alias=None, name=None, far=(), far_out=(), scratch=(), room=40 << 20):
     return pl.pallas_call(
         kernel,
         out_shape=[jax.ShapeDtypeStruct(s, F32) for s in outs],
@@ -40,7 +43,7 @@
         scratch_shapes=list(scratch),
         input_output_aliases=alias or {},
         name=name,
-        compiler_params=pltpu.CompilerParams(vmem_limit_bytes=40 << 20),
+        compiler_params=pltpu.CompilerParams(vmem_limit_bytes=room),
     )(*args)
 
 
@@ -147,8 +150,8 @@
 
 def k_first(
     e_ref, h_ref, cell_ref, node_ref, cond_ref, far_ref, delay_ref, imped_ref, near_hist_ref,
-    pay_ref, up_ref, right_ref,
-    ez, side, cell, node, cond, far, delay, imped, hist, sems,
+    pay_out, up_ref, right_ref,
+    ez, side, cell, node, cond, far, delay, imped, hist, pay_ref, sems,
 ):
     pairs = [
         (cell_ref, cell), (node_ref, node), (cond_ref, cond), (e_ref.at[2], ez),
@@ -162,7 +165,7 @@
     here = at_ports(ez[...].reshape(NZ * NX, NY), own_ports(cell[...]))
     first = jnp.concatenate([node[...], cell[...]], 1).astype(F32)
     second = jnp.concatenate([cond[...], here[:, :HALF]], 1)
-    pay_ref[...] = jnp.broadcast_to(jnp.concatenate([first, second], 0)[None], PAY_SHAPE)
+    sending = payload(pay_out, pay_ref, sems.at[11], first, second)
     wait(started[4:])
     up_ref[2 * NX : 2 * NX + 1, 0:LANES] = far[...].astype(F32)
     up_ref[2 * NX + 1 : 2 * NX + 2, 0:LANES] = delay[...].astype(F32)
@@ -172,26 +175,23 @@
     for c in range(2):
         for z in range(NZ):
             right_ref[c * NZ + z : c * NZ + z + 1] = side[c, z, 7:8]
-
-
-def update_e(e_ref, h_ref, d_ref, g_ref):
+    sending.wait()
+
+
+def update_e(e_ref, h_ref, d_ref, g_ref, components, width):
     for z in range(NZ):
         hx, hy, hz = h_ref[0, z + 1], h_ref[1, z + 1], h_ref[2, z + 1]
-        own = hz[:NX]
-        curl_x = (own - last_y(own)) - (hy[:NX] - h_ref[1, z, :NX])
-        curl_y = (hx[:NX] - h_ref[0, z, :NX]) - (hz - last_x(hz))[:NX]
-        curl_z = (hy - last_x(hy))[:NX] - (hx[:NX] - last_y(hx[:NX]))
         d, g = d_ref[z], g_ref[z]
-        for c, curl in enumerate((curl_x, curl_y, curl_z)):
-            e_ref[c, z + 1, :NX] = d * e_ref[c, z + 1, :NX] + g * curl
-
-
-def send_x(e_ref, right_ref, left_ref):
-    for z in range(NZ):
-        for c in range(3):
-            right_ref[c * NZ + z : c * NZ + z + 1] = e_ref[c, z + 1, NX - 1 : NX]
-        for c in range(2):
-            left_ref[c * NZ + z : c * NZ + z + 1] = e_ref[1 + c, z + 1, 0:1]
+        for c in components:
+            if c == 0:
+                own = hz[:width]
+                curl = (own - last_y(own)) - (hy[:width] - h_ref[1, z, :width])
+            elif c == 1:
+                curl = (hx[:width] - h_ref[0, z, :width]) - (hz - last_x(hz))[:width]
+            else:
+                own = hx[:width]
+                curl = (hy - last_x(hy))[:width] - (own - last_y(own))
+            e_ref[c, z + 1, :width] = d * e_ref[c, z + 1, :width] + g * curl
 
 
 def own_rows(ref):
@@ -199,7 +199,8 @@
 
 
 def k_start(
-    e_in, h_in, d_in, g_in, cell_in, up_ref, right_ref, e_ref, h_ref, pre_ref, xr_ref, xl_ref, d_ref, g_ref, cell_ref, sems
+    e_in, h_in, d_in, g_in, cell_in, up_ref, right_ref, e_ref, h_ref, pre_ref, right_out, left_out,
+    d_ref, g_ref, cell_ref, send_right, send_left, sems,
 ):
     pairs = [(e_in, own_rows(e_ref)), (h_in, own_rows(h_ref)), (d_in, d_ref), (g_in, g_ref), (cell_in, cell_ref)]
     started = copies(pairs, sems)
@@ -216,12 +217,44 @@
     h_ref[0, 0, :NX] = up_ref[0:NX]
     h_ref[1, 0, :NX] = up_ref[NX : 2 * NX]
     wait(started)
-    update_e(e_ref, h_ref, d_ref, g_ref)
+    update_e(e_ref, h_ref, d_ref, g_ref, (0, 1, 2), NX)
+    layers = [(e_ref, (c, z + 1)) for c in range(3) for z in range(NZ)]
+    layers += [(h_ref, (c, z + 1)) for c in range(3) for z in range(NZ)] + [(h_ref, (c, 0)) for c in range(2)]
+    layers += [(d_ref, (z,)) for z in range(NZ)] + [(g_ref, (z,)) for z in range(NZ)]
+    for k, (ref, at) in enumerate(layers):
+        send_right[k * DEEP : (k + 1) * DEEP] = ref[(*at, slice(NX - DEEP, NX))]
+        send_left[k * DEEP : (k + 1) * DEEP] = ref[(*at, slice(0, DEEP))]
+    started = copies([(send_right, right_out), (send_left, left_out)], sems)
     ports = own_ports(cell_ref[...])
     pre = at_ports(e_ref[2, 1 : NZ + 1, :NX].reshape(NZ * NX, NY), ports)
     gain = at_ports(g_ref[...].reshape(NZ * NX, NY), ports)
     pre_ref[...] = jnp.broadcast_to(pre + pltpu.roll(gain, HALF, 1), (8, LANES))
-    send_x(e_ref, xr_ref, xl_ref)
+    wait(started)
+
+
+def k_widen(right_in, left_in, d_in, g_in, e_in, h_in, e_ref, h_ref, d_out, g_out, right_ref, left_ref, d_tile, g_tile, sems):
+    pairs = [(right_in, right_ref), (left_in, left_ref), (d_in, d_out.at[:, 0:NX]), (g_in, g_out.at[:, 0:NX])]
+    started = copies(pairs, sems)
+    wait(started[:2])
+
+    def tile(k):
+        rows = slice(k * DEEP, (k + 1) * DEEP)
+        return jnp.concatenate([left_ref[rows], right_ref[rows]], 0)
+
+    for z in range(NZ):
+        d_tile[z] = tile(6 * NZ + 2 + z)
+        g_tile[z] = tile(7 * NZ + 2 + z)
+    more = [pltpu.make_async_copy(d_tile, d_out.at[:, NX:], sems.at[4]), pltpu.make_async_copy(g_tile, g_out.at[:, NX:], sems.at[5])]
+    for copy in more:
+        copy.start()
+    for c in range(3):
+        for z in range(NZ):
+            e_ref[c, z + 1, NX:] = tile(c * NZ + z)
+            h_ref[c, z + 1, NX:] = tile(3 * NZ + c * NZ + z)
+    for c in range(2):
+        h_ref[c, 0, NX:] = tile(6 * NZ + c)
+    wait(started[2:])
+    wait(more)
 
 
 def low_onehots(node):
@@ -269,14 +302,17 @@
     return own_volts(w, lines, state_ref[NODE : NODE + 16].astype(jnp.int32), inverse_ref)
 
 
-def payload(pay_ref, volts, pre):
+def payload(pay_out, pay_ref, sem, volts, pre):
     pay_ref[...] = jnp.broadcast_to(jnp.concatenate([volts, pre], 0)[None], PAY_SHAPE)
+    copy = pltpu.make_async_copy(pay_ref, pay_out, sem)
+    copy.start()
+    return copy
 
 
 def k_tables(
     got_ref, up_ref, pre_ref, near_in, delay_in, imped_in, near_hist_in, far_hist_in, inverse_in,
-    pay_ref, state_ref,
-    near_ref, delay_ref, imped_ref, near_hist_ref, far_hist_ref, inverse_ref, sems,
+    pay_out, state_ref,
+    near_ref, delay_ref, imped_ref, near_hist_ref, far_hist_ref, inverse_ref, pay_ref, sems,
 ):
     pairs = [
         (near_in, near_ref), (delay_in, delay_ref), (imped_in, imped_ref),
@@ -302,7 +338,7 @@
         state_ref[FROM_ABOVE + k : FROM_ABOVE + k + 1] = far_hist_ref[back]
         state_ref[FROM_BELOW + k : FROM_BELOW + k + 1] = up_ref[2 * NX + back : 2 * NX + back + 1, LANES : 2 * LANES]
     wait(started[5:])
-    payload(pay_ref, next_volts(state_ref, inverse_ref, 0), pre_ref[0:1])
+    payload(pay_out, pay_ref, sems.at[6], next_volts(state_ref, inverse_ref, 0), pre_ref[0:1]).wait()
 
 
 def block_row(k):
@@ -318,7 +354,7 @@
         cell = jnp.sum(jnp.where(pick, where, 0.0), 0, keepdims=True).astype(jnp.int32) % (NZ * NX * NY)
         values = jnp.sum(jnp.where(pick, drop, 0.0), 0, keepdims=True)
         x = (cell // NY) % NX + k * NX
-        position = jnp.where((x >= 0) & (x <= NX), x, jnp.where(x == -1, GX - 1, -1))
+        position = jnp.where((x >= 0) & (x < NX + DEEP), x, jnp.where((x < 0) & (x >= -DEEP), x + GX, -1))
         inside = (iota((1, LANES), 1) // HALF == half) & exists & (position >= 0)
         target = jnp.where(inside, (cell // (NX * NY)) * GX + position, -1)
         at_row = ones_where(iota((NZ * GX, LANES), 0) == target)
@@ -331,7 +367,7 @@
         e_ref[2, z + 1] = e_ref[2, z + 1] - spread[z * GX : (z + 1) * GX]
 
 
-def k_currents(n, last, got_ref, xr_ref, xl_ref, e_in, state_in, e_ref, state_ref, *sends):
+def k_currents(n, last, got_ref, e_in, state_in, e_ref, state_ref, *sends):
     pre = lower(got_ref, 1)
     if n == 0:
         state_ref[GAIN : GAIN + 8] = upper(got_ref, 1)
@@ -351,31 +387,23 @@
     top = jnp.where(row() == NF - 1, -into_own, 0.0)
     state_ref[WAVE : WAVE + 2] = jnp.concatenate([out_near, top], 0)
 
-    first = iota((8, NY), 0)
-    for z in range(NZ):
-        for c in range(3):
-            ghost = jnp.where(first == 7, xr_ref[c * NZ + z : c * NZ + z + 1], 0.0)
-            if c:
-                ghost = jnp.where(first == 0, xl_ref[(c - 1) * NZ + z : (c - 1) * NZ + z + 1], ghost)
-            e_ref[c, z + 1, NX:] = ghost
     spread_currents(e_ref, where, gain * current)
 
     down_ref = sends[-1]
-    down_ref[0:GX] = e_ref[0, 1]
-    down_ref[GX : GX + NX] = e_ref[1, 1, :NX]
-    down_ref[GX + NX :] = jnp.zeros((8, NY), F32)
-    down_ref[GX + NX : GX + NX + 1, 0:LANES] = out_below
+    for c in range(2):
+        down_ref[c * GX : (c + 1) * GX] = e_ref[c, 1]
+    down_ref[2 * GX :] = jnp.zeros((8, NY), F32)
+    down_ref[2 * GX : 2 * GX + 1, 0:LANES] = out_below
     if not last:
         up_ref = sends[0]
-        up_ref[0:NX] = e_ref[0, NZ, :NX]
-        up_ref[NX : 2 * NX] = e_ref[1, NZ, :NX]
-        up_ref[2 * NX : 2 * NX + GX] = e_ref[2, NZ]
-        up_ref[2 * NX + GX :] = jnp.zeros((8, NY), F32)
-        up_ref[2 * NX + GX : 2 * NX + GX + 1, 0:LANES] = out_near
+        for c in range(3):
+            up_ref[c * GX : (c + 1) * GX] = e_ref[c, NZ]
+        up_ref[3 * GX :] = jnp.zeros((8, NY), F32)
+        up_ref[3 * GX : 3 * GX + 1, 0:LANES] = out_near
 
 
 def new_h(e_ref, h_ref, layer, ex_above, ey_above):
-    scale = jnp.where((iota((GX, 1), 0) >= NX) & (column() == 0), 0.0, 0.5)
+    scale = jnp.where((iota((GX, 1), 0) >= GX - DEEP) & (column() == 0), 0.0, 0.5)
     ex, ey, ez = e_ref[0, layer], e_ref[1, layer], e_ref[2, layer]
     if layer == 0:
         scale = jnp.where(row() == 0, 0.0, scale)
@@ -405,35 +433,39 @@
     second.wait()
 
 
-def k_volts(n, last, up_ref, down_ref, d_ref, g_ref, inverse_ref, cell_ref, e_in, h_in, state_in, e_ref, h_ref, state_ref, pay_ref, xr_ref, xl_ref, *volts_ref):
+def k_volts(
+    n, last, up_ref, down_ref, d_ref, g_ref, inverse_ref, cell_ref, e_in, h_in, state_in,
+    e_ref, h_ref, state_ref, pay_out, *rest,
+):
+    pay_ref, sem = rest[-2:]
     at = n - 1 + DEPTH
-    wave = down_ref[GX + NX : GX + NX + 1, 0:LANES] + state_ref[WAVE + 1 : WAVE + 2]
     state_ref[OWN + at : OWN + at + 1] = state_ref[WAVE : WAVE + 1]
-    state_ref[FROM_ABOVE + at : FROM_ABOVE + at + 1] = wave
-    state_ref[FROM_BELOW + at : FROM_BELOW + at + 1] = up_ref[2 * NX + GX : 2 * NX + GX + 1, 0:LANES]
+    state_ref[FROM_ABOVE + at : FROM_ABOVE + at + 1] = down_ref[2 * GX : 2 * GX + 1, 0:LANES] + state_ref[WAVE + 1 : WAVE + 2]
+    state_ref[FROM_BELOW + at : FROM_BELOW + at + 1] = up_ref[3 * GX : 3 * GX + 1, 0:LANES]
     volts = next_volts(state_ref, inverse_ref, n)
     if last:
-        volts_ref[0][...] = volts
-    e_ref[0, 0, :NX] = up_ref[0:NX]
-    e_ref[1, 0, :NX] = up_ref[NX : 2 * NX]
-    e_ref[2, 0] = up_ref[2 * NX : 2 * NX + GX]
-    e_ref[0, NZ + 1] = down_ref[0:GX]
-    e_ref[1, NZ + 1, :NX] = down_ref[GX : GX + NX]
+        rest[0][...] = volts
+    for c in range(3):
+        e_ref[c, 0] = up_ref[c * GX : (c + 1) * GX]
+    for c in range(2):
+        e_ref[c, NZ + 1] = down_ref[c * GX : (c + 1) * GX]
     update_h(e_ref, h_ref, 0)
     update_h(e_ref, h_ref, NZ)
-    update_e(e_ref, h_ref, d_ref, g_ref)
+    update_e(e_ref, h_ref, d_ref, g_ref, (2,), GX)
     pre = at_ports(e_ref[2, 1 : NZ + 1, :NX].reshape(NZ * NX, NY), own_ports(cell_ref[...]))
-    payload(pay_ref, volts, pre)
-    send_x(e_ref, xr_ref, xl_ref)
+    payload(pay_out, pay_ref, sem, volts, pre).wait()
+
+
+def k_exy(h_ref, d_ref, g_ref, e_in, e_ref):
+    update_e(e_ref, h_ref, d_ref, g_ref, (0, 1), GX)
 
 
 def k_last(down_ref, state_ref, e_ref, h_ref, h_in, h_out, wave_out, layer_ref, sem):
-    ey_above = jnp.concatenate([down_ref[GX : GX + NX], jnp.zeros((8, NY), F32)], 0)
-    for c, value in enumerate(new_h(e_ref, h_ref, NZ, down_ref[0:GX], ey_above)):
+    for c, value in enumerate(new_h(e_ref, h_ref, NZ, down_ref[0:GX], down_ref[GX : 2 * GX])):
         layer_ref[c] = value[:NX]
     copy = pltpu.make_async_copy(layer_ref, h_out.at[:, NZ - 1], sem)
     copy.start()
-    above = down_ref[GX + NX : GX + NX + 1, 0:LANES] + state_ref[WAVE + 1 : WAVE + 2]
+    above = down_ref[2 * GX : 2 * GX + 1, 0:LANES] + state_ref[WAVE + 1 : WAVE + 2]
     wave_out[...] = jnp.concatenate([state_ref[WAVE : WAVE + 1], above], 0)[None]
     copy.wait()
 
@@ -461,6 +493,9 @@
     line_int = pltpu.VMEM((1, LANES), jnp.int32)
     ports_int = pltpu.VMEM((1, HALF), jnp.int32)
     block = pltpu.VMEM((NZ, NX, NY), F32)
+    pay_scratch = pltpu.VMEM(PAY_SHAPE, F32)
+    side = pltpu.VMEM(SIDE_SHAPE, F32)
+    tiles = pltpu.VMEM((NZ, 8, NY), F32)
 
     pay, up, right = call(
         k_first,
@@ -469,19 +504,22 @@
         far=range(9),
         scratch=[
             block, pltpu.VMEM((2, NZ, 8, NY), F32), ports_int, ports_int, pltpu.VMEM((1, HALF), F32),
-            line_int, line_int, line, hist_shape, pltpu.SemaphoreType.DMA((11,)),
+            line_int, line_int, line, hist_shape, pay_scratch, pltpu.SemaphoreType.DMA((12,)),
         ],
+        far_out=(0,),
+        room=67000000,
         name="first",
     )
     got = exchanged(pay)
     up = shifted(up, "fz", 1)
     right = shifted(right, "fxy", 1)
-    e, h, pre, xr, xl = call(
+    e, h, pre, to_right, to_left = call(
         k_start,
-        [E_SHAPE, H_SHAPE, (8, LANES), XR_SHAPE, XL_SHAPE],
+        [E_SHAPE, H_SHAPE, (8, LANES), SIDE_SHAPE, SIDE_SHAPE],
         e_field, h_field, e_decay, e_gain, port_cell, up, right,
         far=range(5),
-        scratch=[block, block, ports_int, pltpu.SemaphoreType.DMA((5,))],
+        far_out=(3, 4),
+        scratch=[block, block, ports_int, side, side, pltpu.SemaphoreType.DMA((5,))],
         name="start",
     )
     pay, state = call(
@@ -491,20 +529,33 @@
         far=range(3, 9),
         scratch=[
             line_int, line_int, line, hist_shape, hist_shape,
-            pltpu.VMEM((1, LANES, NB * LANES), F32), pltpu.SemaphoreType.DMA((6,)),
+            pltpu.VMEM((1, LANES, NB * LANES), F32), pay_scratch, pltpu.SemaphoreType.DMA((7,)),
         ],
+        far_out=(0,),
         name="tables",
     )
+    to_right, to_left, pay = lax.optimization_barrier((to_right, to_left, pay))
     for n in range(STEPS):
         last = n == STEPS - 1
         got = exchanged(pay)
-        xr = shifted(xr, "fxy", 1)
-        xl = shifted(xl, "fxy", -1)
+        if n == 0:
+            e, h, d, g = call(
+                k_widen,
+                [E_SHAPE, H_SHAPE, WIDE, WIDE],
+                shifted(to_right, "fxy", 1), shifted(to_left, "fxy", -1), e_decay, e_gain, e, h,
+                far=range(4),
+                far_out=(2, 3),
+                alias={4: 0, 5: 1},
+                scratch=[side, side, tiles, tiles, pltpu.SemaphoreType.DMA((6,))],
+                name="widen",
+            )
+        else:
+            (e,) = call(k_exy, [E_SHAPE], h, d, g, e, alias={3: 0}, name="exy")
         e, state, *sends = call(
             functools.partial(k_currents, n, last),
             [E_SHAPE, (ROWS, LANES)] + ([] if last else [UP_SHAPE]) + [DOWN_SHAPE],
-            got, xr, xl, e, state,
-            alias={3: 0, 4: 1},
+            got, e, state,
+            alias={1: 0, 2: 1},
             name="currents",
         )
         down = shifted(sends[-1], "fz", -1)
@@ -512,11 +563,13 @@
             break
         up = shifted(sends[0], "fz", 1)
         (h,) = call(k_inner_h, [H_SHAPE], e, h, alias={1: 0}, name="inner_h")
-        e, h, state, pay, xr, xl, *node_volt = call(
+        e, h, state, pay, *node_volt = call(
             functools.partial(k_volts, n + 1, n + 1 == STEPS - 1),
-            [E_SHAPE, H_SHAPE, (ROWS, LANES), PAY_SHAPE, XR_SHAPE, XL_SHAPE] + ([(1, LANES)] if n + 1 == STEPS - 1 else []),
-            up, down, e_decay, e_gain, inverse, port_cell, e, h, state,
+            [E_SHAPE, H_SHAPE, (ROWS, LANES), PAY_SHAPE] + ([(1, LANES)] if n + 1 == STEPS - 1 else []),
+            up, down, d, g, inverse, port_cell, e, h, state,
             alias={6: 0, 7: 1, 8: 2},
+            far_out=(3,),
+            scratch=[pay_scratch, pltpu.SemaphoreType.DMA],
             name="volts",
         )
     h, e_out, h_out = call(

time: 179 us -> 167 us (0.933)
  starting transfers between devices: 96.1 us -> 71.5 us
  waiting for transfers between devices: 53.9 us -> 62.8 us
  Pallas kernels: 14 us -> 18.5 us
    all_to_all x5, waiting for transfers between devices: 15.8 us -> 37.7 us  [exchanged(): return lax.all_to_all(value, 'fxy', 0, 0, tiled=True)]
    ppermute x17 -> x11, waiting for transfers between devices: 38.1 us -> 25.1 us  [shifted(): return lax.ppermute(value, axis, pairs)]
    all_to_all x5, starting transfers between devices: 51.7 us -> 39.1 us  [exchanged(): return lax.all_to_all(value, 'fxy', 0, 0, tiled=True)]
    ppermute x17 -> x11, starting transfers between devices: 44.5 us -> 32.4 us  [shifted(): return lax.ppermute(value, axis, pairs)]
    pallas_call x15 -> x19, Pallas kernels: 14 us -> 18.5 us  [call(): pl.pallas_call(kernel, out_shape=[jax.ShapeDtypeStruct(s, F32) for s in o...]
    unnamed x52 -> x50, local copies, waits for them, and re-layouts: 12.3 us -> 11.7 us
  transfers between devices with their start and end apart: 22 -> 16, of which waited for: 14 -> 10; matrix products, arithmetic and copies ran while one was open for 0% -> 0% of each run, Pallas kernels for 2% -> 3%
where the time goes in v3:
time: 167 us; the launch traced here: 166 us
  starting transfers between devices  71.5 us (43%)
  waiting for transfers between devices  62.8 us (38%)
  Pallas kernels  18.5 us (11%)
  local copies, waits for them, and re-layouts  11.7 us (7%)
    all_to_all x5, starting transfers between devices, exchanged(): return lax.all_to_all(value, 'fxy', 0, 0, tiled=True)  39.1 us
    all_to_all x5, waiting for transfers between devices, exchanged(): return lax.all_to_all(value, 'fxy', 0, 0, tiled=True)  37.7 us
    ppermute x11, starting transfers between devices, shifted(): return lax.ppermute(value, axis, pairs)  32.4 us
    ppermute x11, waiting for transfers between devices, shifted(): return lax.ppermute(value, axis, pairs)  25.1 us
    pallas_call x19, Pallas kernels, call(): pl.pallas_call(kernel, out_shape=[jax.ShapeDtypeStruct(s, F32) for s in o...  18.5 us
    unnamed x50, local copies, waits for them, and re-layouts  11.7 us
  transfers between devices with their start and end apart: 16, of which 10 were waited for; matrix products, arithmetic and copies ran while one was open for 0% of the time, Pallas kernels for 3%

profile of v3, /device:TPU:7, one launch (start us, length us, event | category | flops | bytes accessed | tf_op | source)
XLA Modules:
  0.0 165.6 jit_solution(7851978385014050261)
XLA Ops:
  0.6 2.8 %first.1 = (f32[16,2,128]{2,1,0:T(2,128)}, f32[40,512]{1,0:T(8,128)}, f32[16,512]{1,0:T(8,128)}) custom-call(f32[3,8,16,512]{3,2,1,0:T(8,128)} %e_in.1, f32[3,8,16,512]{3,2,1,0:T(8,128)} %h_in.1, s32[1,64]{1,0:T(1,128)} %cell_ref.7, s32[1,64]{1,0:T(1,128)} %node_ref.1, f32[1,64]{1,0:T(1,128)} %cond_ref.1, s32[1,128]{1,0:T(1,128)} %far_ref.1, ...), custom_call_target="tpu_custom_call" | custom-call | tf_op jit(solution)/shard_map/first/pallas_call | solution.py:38
  3.4 0.0 copy-start.18
  3.4 0.0 copy-start.19
  3.5 0.0 copy-start.21
  3.5 0.0 copy-start.22
  3.5 3.8 %collective-permute-start = (f32[40,512]{1,0:T(8,128)}, f32[40,512]{1,0:T(8,128)S(1)}, u32[]{:S(2)}, u32[]{:S(2)}) collective-permute-start(f32[40,512]{1,0:T(8,128)} %get-tuple-element.54), channel_id=1, source_target_pairs={{0,16},{16,32},{32,48},{48,64},{64,80},{80,96},{96,112},{112,128},... | collective-permute-start | bytes 245768 | tf_op jit(solution)/shard_map/ppermute | solution.py:53
  7.3 14.9 %all-to-all-start = ((f32[16,2,128]{2,1,0:T(2,128)}), f32[16,2,128]{2,1,0:T(2,128)S(1)}, u32[]{:S(2)}, u32[]{:S(2)}) async-start(f32[16,2,128]{2,1,0:T(2,128)} %get-tuple-element.58), calls=%async_computation | async-start | bytes 32768 | tf_op jit(solution)/shard_map/all_to_all | solution.py:57
  22.2 3.3 %collective-permute-start.1 = (f32[16,512]{1,0:T(8,128)}, f32[16,512]{1,0:T(8,128)S(1)}, u32[]{:S(2)}, u32[]{:S(2)}) collective-permute-start(f32[16,512]{1,0:T(8,128)} %get-tuple-element.55), channel_id=1, source_target_pairs={{0,1},{1,2},{2,3},{3,4},{4,5},{5,6},{6,7},{7,8},{8,9},{9,10},{10,1... | collective-permute-start | bytes 98312 | tf_op jit(solution)/shard_map/ppermute | solution.py:53
  25.5 1.6 collective-permute-done.1.right_ref
  27.1 1.1 copy-done.11
  28.2 1.1 copy-done.12
  29.4 0.9 copy-done.13
  30.3 0.9 copy-done.15
  31.3 1.4 start.1
  32.7 0.0 copy-start.23
  32.7 0.8 copy-done.23
  33.5 0.8 copy-done.24
  34.4 1.2 copy-done
  35.6 1.3 tables.1
  36.9 4.8 %collective-permute-start.2 = (f32[264,512]{1,0:T(8,128)}, f32[264,512]{1,0:T(8,128)}, u32[]{:S(2)}, u32[]{:S(2)}) collective-permute-start(f32[264,512]{1,0:T(8,128)} %copy-done.24), channel_id=1, source_target_pairs={{0,1},{1,2},{2,3},{3,4},{4,5},{5,6},{6,7},{7,8},{8,9},{9,10},{10,1... | collective-permute-start | bytes 1622024 | tf_op jit(solution)/shard_map/ppermute | solution.py:53
  41.7 1.3 collective-permute-start.3
  43.0 13.6 %all-to-all-start.1 = ((f32[16,2,128]{2,1,0:T(2,128)}), f32[16,2,128]{2,1,0:T(2,128)S(1)}, u32[]{:S(2)}, u32[]{:S(2)}) async-start(f32[16,2,128]{2,1,0:T(2,128)} %get-tuple-element.61), calls=%async_computation.1 | async-start | bytes 32768 | tf_op jit(solution)/shard_map/all_to_all | solution.py:57
  56.6 0.5 collective-permute-done.3.left_in
  57.1 0.9 copy-done.16
  58.1 1.5 widen.1
  59.5 0.0 copy-start.4
  59.5 0.7 copy-done.4
  60.3 7.7 %all-to-all-done.1.got_ref = f32[16,2,128]{2,1,0:T(2,128)S(1)} async-done(((f32[16,2,128]{2,1,0:T(2,128)}), f32[16,2,128]{2,1,0:T(2,128)S(1)}, u32[]{:S(2)}, u32[]{:S(2)}) %all-to-all-start.1) | async-done | bytes 16416 | tf_op jit(solution)/shard_map/all_to_all | solution.py:57
  68.0 0.7 currents.4
  68.7 5.3 %collective-permute-start.4 = (f32[80,512]{1,0:T(8,128)S(1)}, f32[80,512]{1,0:T(8,128)S(1)}, u32[]{:S(2)}, u32[]{:S(2)}) collective-permute-start(f32[80,512]{1,0:T(8,128)S(1)} %get-tuple-element.68), channel_id=1, source_target_pairs={{0,16},{16,32},{32,48},{48,64},{64,80},{80,96},{96,112},{112,128},... | collective-permute-start | bytes 491528 | tf_op jit(solution)/shard_map/ppermute | solution.py:53
  74.1 1.9 %collective-permute-start.5 = (f32[56,512]{1,0:T(8,128)S(1)}, f32[56,512]{1,0:T(8,128)S(1)}, u32[]{:S(2)}, u32[]{:S(2)}) collective-permute-start(f32[56,512]{1,0:T(8,128)S(1)} %get-tuple-element.69), channel_id=1, source_target_pairs={{16,0},{32,16},{48,32},{64,48},{80,64},{96,80},{112,96},{128,112},... | collective-permute-start | bytes 344072 | tf_op jit(solution)/shard_map/ppermute | solution.py:53
  76.0 0.0 copy-start.5
  76.0 0.3 inner_h.3.h_in
  76.3 6.0 %collective-permute-done.5.down_ref = f32[56,512]{1,0:T(8,128)S(1)} collective-permute-done((f32[56,512]{1,0:T(8,128)S(1)}, f32[56,512]{1,0:T(8,128)S(1)}, u32[]{:S(2)}, u32[]{:S(2)}) %collective-permute-start.5) | collective-permute-done | bytes 114720 | tf_op jit(solution)/shard_map/ppermute | solution.py:53
  82.3 1.3 volts.3
  83.6 3.5 %all-to-all-start.2 = ((f32[16,2,128]{2,1,0:T(2,128)}), f32[16,2,128]{2,1,0:T(2,128)S(1)}, u32[]{:S(2)}, u32[]{:S(2)}) async-start(f32[16,2,128]{2,1,0:T(2,128)} %get-tuple-element.75), calls=%async_computation.2 | async-start | bytes 32768 | tf_op jit(solution)/shard_map/all_to_all | solution.py:57
  87.2 1.0 copy-done.6
  88.2 0.3 exy.3.e_in
  88.5 10.1 %all-to-all-done.2.got_ref = f32[16,2,128]{2,1,0:T(2,128)S(1)} async-done(((f32[16,2,128]{2,1,0:T(2,128)}), f32[16,2,128]{2,1,0:T(2,128)S(1)}, u32[]{:S(2)}, u32[]{:S(2)}) %all-to-all-start.2) | async-done | bytes 16416 | tf_op jit(solution)/shard_map/all_to_all | solution.py:57
  98.6 0.7 currents.5
  99.3 3.2 %collective-permute-start.6 = (f32[80,512]{1,0:T(8,128)S(1)}, f32[80,512]{1,0:T(8,128)S(1)}, u32[]{:S(2)}, u32[]{:S(2)}) collective-permute-start(f32[80,512]{1,0:T(8,128)S(1)} %get-tuple-element.79), channel_id=1, source_target_pairs={{0,16},{16,32},{32,48},{48,64},{64,80},{80,96},{96,112},{112,128},... | collective-permute-start | bytes 491528 | tf_op jit(solution)/shard_map/ppermute | solution.py:53
  102.5 1.9 %collective-permute-start.7 = (f32[56,512]{1,0:T(8,128)S(1)}, f32[56,512]{1,0:T(8,128)S(1)}, u32[]{:S(2)}, u32[]{:S(2)}) collective-permute-start(f32[56,512]{1,0:T(8,128)S(1)} %get-tuple-element.80), channel_id=1, source_target_pairs={{16,0},{32,16},{48,32},{64,48},{80,64},{96,80},{112,96},{128,112},... | collective-permute-start | bytes 344072 | tf_op jit(solution)/shard_map/ppermute | solution.py:53
  104.5 0.3 inner_h.4.h_in
  104.8 6.0 %collective-permute-done.7.down_ref = f32[56,512]{1,0:T(8,128)S(1)} collective-permute-done((f32[56,512]{1,0:T(8,128)S(1)}, f32[56,512]{1,0:T(8,128)S(1)}, u32[]{:S(2)}, u32[]{:S(2)}) %collective-permute-start.7) | collective-permute-done | bytes 114720 | tf_op jit(solution)/shard_map/ppermute | solution.py:53
  110.8 1.3 volts.4
  112.1 3.5 %all-to-all-start.3 = ((f32[16,2,128]{2,1,0:T(2,128)}), f32[16,2,128]{2,1,0:T(2,128)S(1)}, u32[]{:S(2)}, u32[]{:S(2)}) async-start(f32[16,2,128]{2,1,0:T(2,128)} %get-tuple-element.83), calls=%async_computation.3 | async-start | bytes 32768 | tf_op jit(solution)/shard_map/all_to_all | solution.py:57
  115.6 1.0 copy-done.8
  116.6 0.3 exy.4.e_in
  116.9 9.9 %all-to-all-done.3.got_ref = f32[16,2,128]{2,1,0:T(2,128)S(1)} async-done(((f32[16,2,128]{2,1,0:T(2,128)}), f32[16,2,128]{2,1,0:T(2,128)S(1)}, u32[]{:S(2)}, u32[]{:S(2)}) %all-to-all-start.3) | async-done | bytes 16416 | tf_op jit(solution)/shard_map/all_to_all | solution.py:57
  126.8 0.7 currents.6
  127.5 3.0 %collective-permute-start.8 = (f32[80,512]{1,0:T(8,128)S(1)}, f32[80,512]{1,0:T(8,128)S(1)}, u32[]{:S(2)}, u32[]{:S(2)}) collective-permute-start(f32[80,512]{1,0:T(8,128)S(1)} %get-tuple-element.87), channel_id=1, source_target_pairs={{0,16},{16,32},{32,48},{48,64},{64,80},{80,96},{96,112},{112,128},... | collective-permute-start | bytes 491528 | tf_op jit(solution)/shard_map/ppermute | solution.py:53
  130.6 1.9 %collective-permute-start.9 = (f32[56,512]{1,0:T(8,128)S(1)}, f32[56,512]{1,0:T(8,128)S(1)}, u32[]{:S(2)}, u32[]{:S(2)}) collective-permute-start(f32[56,512]{1,0:T(8,128)S(1)} %get-tuple-element.88), channel_id=1, source_target_pairs={{16,0},{32,16},{48,32},{64,48},{80,64},{96,80},{112,96},{128,112},... | collective-permute-start | bytes 344072 | tf_op jit(solution)/shard_map/ppermute | solution.py:53
  132.5 0.3 inner_h.5.h_in
  132.8 6.0 %collective-permute-done.9.down_ref = f32[56,512]{1,0:T(8,128)S(1)} collective-permute-done((f32[56,512]{1,0:T(8,128)S(1)}, f32[56,512]{1,0:T(8,128)S(1)}, u32[]{:S(2)}, u32[]{:S(2)}) %collective-permute-start.9) | collective-permute-done | bytes 114720 | tf_op jit(solution)/shard_map/ppermute | solution.py:53
  138.8 1.8 %volts.5 = (f32[3,10,24,512]{3,2,1,0:T(8,128)S(1)}, f32[3,9,24,512]{3,2,1,0:T(8,128)S(1)}, f32[112,128]{1,0:T(8,128)S(1)}, f32[16,2,128]{2,1,0:T(2,128)}, f32[1,128]{1,0:T(1,128)}) custom-call(f32[80,512]{1,0:T(8,128)S(1)} %collective-permute-done.8.up_ref, ...), custom_call_target="tpu_custom_call", output_to_operand_aliasing={{0}: (6, {}), {1}: (7, {}), {2}: (8, {})} | custom-call | tf_op jit(solution)/shard_map/volts/pallas_call | solution.py:38
  140.6 3.5 %all-to-all-start.4 = ((f32[16,2,128]{2,1,0:T(2,128)}), f32[16,2,128]{2,1,0:T(2,128)S(1)}, u32[]{:S(2)}, u32[]{:S(2)}) async-start(f32[16,2,128]{2,1,0:T(2,128)} %get-tuple-element.91), calls=%async_computation.4 | async-start | bytes 32768 | tf_op jit(solution)/shard_map/all_to_all | solution.py:57
  144.2 1.0 copy-done.10
  145.1 0.3 exy.5.e_in
  145.4 9.9 %all-to-all-done.4.got_ref = f32[16,2,128]{2,1,0:T(2,128)S(1)} async-done(((f32[16,2,128]{2,1,0:T(2,128)}), f32[16,2,128]{2,1,0:T(2,128)S(1)}, u32[]{:S(2)}, u32[]{:S(2)}) %all-to-all-start.4) | async-done | bytes 16416 | tf_op jit(solution)/shard_map/all_to_all | solution.py:57
  155.3 0.7 currents.7
  156.1 1.9 %collective-permute-start.10 = (f32[56,512]{1,0:T(8,128)S(1)}, f32[56,512]{1,0:T(8,128)S(1)}, u32[]{:S(2)}, u32[]{:S(2)}) collective-permute-start(f32[56,512]{1,0:T(8,128)S(1)} %get-tuple-element.97), channel_id=1, source_target_pairs={{16,0},{32,16},{48,32},{64,48},{80,64},{96,80},{112,96},{128,112},... | collective-permute-start | bytes 344072 | tf_op jit(solution)/shard_map/ppermute | solution.py:53
  158.0 1.2 inner_last.1
  159.2 5.1 %collective-permute-done.10.down_ref = f32[56,512]{1,0:T(8,128)S(1)} collective-permute-done((f32[56,512]{1,0:T(8,128)S(1)}, f32[56,512]{1,0:T(8,128)S(1)}, u32[]{:S(2)}, u32[]{:S(2)}) %collective-permute-start.10) | collective-permute-done | bytes 114720 | tf_op jit(solution)/shard_map/ppermute | solution.py:53
  164.3 1.3 last.1
  (37 shorter events, 0.1 us)
Async XLA Ops:
  0.6 26.5 %copy-start.17 = (s32[1,64]{1,0:T(1,128)S(1)}, s32[1,64]{1,0:T(1,128)}, u32[]{:S(2)}) copy-start(s32[1,64]{1,0:T(1,128)} %cell_ref.7) | copy-start | bytes 772
  3.4 30.9 %copy-start.18 = (f32[1,6,128]{2,0,1:T(1,128)S(1)}, f32[1,6,128]{2,0,1:T(1,128)}, u32[]{:S(2)}) copy-start(f32[1,6,128]{2,0,1:T(1,128)} %param.26) | copy-start | bytes 9220
  3.4 30.9 %copy-start.19 = (f32[1,6,128]{2,0,1:T(1,128)S(1)}, f32[1,6,128]{2,0,1:T(1,128)}, u32[]{:S(2)}) copy-start(f32[1,6,128]{2,0,1:T(1,128)} %param.27) | copy-start | bytes 9220
  3.4 30.9 %copy-start.20 = (s32[1,128]{1,0:T(1,128)S(1)}, s32[1,128]{1,0:T(1,128)}, u32[]{:S(2)}) copy-start(s32[1,128]{1,0:T(1,128)} %delay_in.1) | copy-start | bytes 1540
  3.5 30.9 %copy-start.21 = (f32[1,128]{1,0:T(1,128)S(1)}, f32[1,128]{1,0:T(1,128)}, u32[]{:S(2)}) copy-start(f32[1,128]{1,0:T(1,128)} %imped_in.1) | copy-start | bytes 1540
  3.5 30.9 %copy-start.22 = (s32[1,128]{1,0:T(1,128)S(1)}, s32[1,128]{1,0:T(1,128)}, u32[]{:S(2)}) copy-start(s32[1,128]{1,0:T(1,128)} %near_in.1) | copy-start | bytes 1540
  3.5 23.6 %collective-permute-start = (f32[40,512]{1,0:T(8,128)}, f32[40,512]{1,0:T(8,128)S(1)}, u32[]{:S(2)}, u32[]{:S(2)}) collective-permute-start(f32[40,512]{1,0:T(8,128)} %get-tuple-element.54), channel_id=1, source_target_pairs={{0,16},{16,32},{32,48},{48,64},{64,80},{80,96},{96,112},{112,128},... | collective-permute-start | bytes 245768 | tf_op jit(solution)/shard_map/ppermute | solution.py:53
  7.3 27.0 %all-to-all-start = ((f32[16,2,128]{2,1,0:T(2,128)}), f32[16,2,128]{2,1,0:T(2,128)S(1)}, u32[]{:S(2)}, u32[]{:S(2)}) async-start(f32[16,2,128]{2,1,0:T(2,128)} %get-tuple-element.58), calls=%async_computation | async-start | bytes 32768 | tf_op jit(solution)/shard_map/all_to_all | solution.py:57
  22.2 4.9 %collective-permute-start.1 = (f32[16,512]{1,0:T(8,128)}, f32[16,512]{1,0:T(8,128)S(1)}, u32[]{:S(2)}, u32[]{:S(2)}) collective-permute-start(f32[16,512]{1,0:T(8,128)} %get-tuple-element.55), channel_id=1, source_target_pairs={{0,1},{1,2},{2,3},{3,4},{4,5},{5,6},{6,7},{7,8},{8,9},{9,10},{10,1... | collective-permute-start | bytes 98312 | tf_op jit(solution)/shard_map/ppermute | solution.py:53
  27.1 1.1 copy-start.11
  28.2 1.1 copy-start.12
  29.4 0.9 copy-start.13
  30.3 0.9 copy-start.15
  31.3 25.8 %copy-start.14 = (f32[8,16,512]{2,1,0:T(8,128)S(1)}, f32[8,16,512]{2,1,0:T(8,128)}, u32[]{:S(2)}) copy-start(f32[8,16,512]{2,1,0:T(8,128)} %d_in.3) | copy-start | bytes 786436
  32.7 0.8 copy-start.23
  33.5 0.8 copy-start.24
  34.4 1.2 copy-start
  36.9 19.7 %collective-permute-start.2 = (f32[264,512]{1,0:T(8,128)}, f32[264,512]{1,0:T(8,128)}, u32[]{:S(2)}, u32[]{:S(2)}) collective-permute-start(f32[264,512]{1,0:T(8,128)} %copy-done.24), channel_id=1, source_target_pairs={{0,1},{1,2},{2,3},{3,4},{4,5},{5,6},{6,7},{7,8},{8,9},{9,10},{10,1... | collective-permute-start | bytes 1622024 | tf_op jit(solution)/shard_map/ppermute | solution.py:53
  41.7 15.4 %collective-permute-start.3 = (f32[264,512]{1,0:T(8,128)}, f32[264,512]{1,0:T(8,128)}, u32[]{:S(2)}, u32[]{:S(2)}) collective-permute-start(f32[264,512]{1,0:T(8,128)} %copy-done.23), channel_id=1, source_target_pairs={{1,0},{2,1},{3,2},{4,3},{5,4},{6,5},{7,6},{8,7},{9,8},{10,9},{11,1... | collective-permute-start | bytes 1622024 | tf_op jit(solution)/shard_map/ppermute | solution.py:53
  43.0 25.0 %all-to-all-start.1 = ((f32[16,2,128]{2,1,0:T(2,128)}), f32[16,2,128]{2,1,0:T(2,128)S(1)}, u32[]{:S(2)}, u32[]{:S(2)}) async-start(f32[16,2,128]{2,1,0:T(2,128)} %get-tuple-element.61), calls=%async_computation.1 | async-start | bytes 32768 | tf_op jit(solution)/shard_map/all_to_all | solution.py:57
  57.1 1.0 copy-start.16
  59.5 0.7 copy-start.4
  68.7 13.6 %collective-permute-start.4 = (f32[80,512]{1,0:T(8,128)S(1)}, f32[80,512]{1,0:T(8,128)S(1)}, u32[]{:S(2)}, u32[]{:S(2)}) collective-permute-start(f32[80,512]{1,0:T(8,128)S(1)} %get-tuple-element.68), channel_id=1, source_target_pairs={{0,16},{16,32},{32,48},{48,64},{64,80},{80,96},{96,112},{112,128},... | collective-permute-start | bytes 491528 | tf_op jit(solution)/shard_map/ppermute | solution.py:53
  74.1 8.2 %collective-permute-start.5 = (f32[56,512]{1,0:T(8,128)S(1)}, f32[56,512]{1,0:T(8,128)S(1)}, u32[]{:S(2)}, u32[]{:S(2)}) collective-permute-start(f32[56,512]{1,0:T(8,128)S(1)} %get-tuple-element.69), channel_id=1, source_target_pairs={{16,0},{32,16},{48,32},{64,48},{80,64},{96,80},{112,96},{128,112},... | collective-permute-start | bytes 344072 | tf_op jit(solution)/shard_map/ppermute | solution.py:53
  76.0 6.3 %copy-start.1 = (f32[1,128,2048]{2,1,0:T(8,128)S(1)}, f32[1,128,2048]{2,1,0:T(8,128)}, u32[]{:S(2)}) copy-start(f32[1,128,2048]{2,1,0:T(8,128)} %inverse_ref.5) | copy-start | bytes 3145732
  76.0 6.3 %copy-start.5 = (f32[8,24,512]{2,1,0:T(8,128)S(1)}, f32[8,24,512]{2,1,0:T(8,128)}, u32[]{:S(2)}) copy-start(f32[8,24,512]{2,1,0:T(8,128)} %copy-done.4) | copy-start | bytes 1179652
  83.6 14.9 %all-to-all-start.2 = ((f32[16,2,128]{2,1,0:T(2,128)}), f32[16,2,128]{2,1,0:T(2,128)S(1)}, u32[]{:S(2)}, u32[]{:S(2)}) async-start(f32[16,2,128]{2,1,0:T(2,128)} %get-tuple-element.75), calls=%async_computation.2 | async-start | bytes 32768 | tf_op jit(solution)/shard_map/all_to_all | solution.py:57
  87.2 1.0 copy-start.6
  99.3 11.4 %collective-permute-start.6 = (f32[80,512]{1,0:T(8,128)S(1)}, f32[80,512]{1,0:T(8,128)S(1)}, u32[]{:S(2)}, u32[]{:S(2)}) collective-permute-start(f32[80,512]{1,0:T(8,128)S(1)} %get-tuple-element.79), channel_id=1, source_target_pairs={{0,16},{16,32},{32,48},{48,64},{64,80},{80,96},{96,112},{112,128},... | collective-permute-start | bytes 491528 | tf_op jit(solution)/shard_map/ppermute | solution.py:53
  102.5 8.2 %collective-permute-start.7 = (f32[56,512]{1,0:T(8,128)S(1)}, f32[56,512]{1,0:T(8,128)S(1)}, u32[]{:S(2)}, u32[]{:S(2)}) collective-permute-start(f32[56,512]{1,0:T(8,128)S(1)} %get-tuple-element.80), channel_id=1, source_target_pairs={{16,0},{32,16},{48,32},{64,48},{80,64},{96,80},{112,96},{128,112},... | collective-permute-start | bytes 344072 | tf_op jit(solution)/shard_map/ppermute | solution.py:53
  104.5 6.3 %copy-start.2 = (f32[1,128,2048]{2,1,0:T(8,128)S(1)}, f32[1,128,2048]{2,1,0:T(8,128)}, u32[]{:S(2)}) copy-start(f32[1,128,2048]{2,1,0:T(8,128)} %inverse_ref.5) | copy-start | bytes 3145732
  104.5 6.3 %copy-start.7 = (f32[8,24,512]{2,1,0:T(8,128)S(1)}, f32[8,24,512]{2,1,0:T(8,128)}, u32[]{:S(2)}) copy-start(f32[8,24,512]{2,1,0:T(8,128)} %copy-done.4) | copy-start | bytes 1179652
  112.1 14.7 %all-to-all-start.3 = ((f32[16,2,128]{2,1,0:T(2,128)}), f32[16,2,128]{2,1,0:T(2,128)S(1)}, u32[]{:S(2)}, u32[]{:S(2)}) async-start(f32[16,2,128]{2,1,0:T(2,128)} %get-tuple-element.83), calls=%async_computation.3 | async-start | bytes 32768 | tf_op jit(solution)/shard_map/all_to_all | solution.py:57
  115.6 1.0 copy-start.8
  127.5 11.3 %collective-permute-start.8 = (f32[80,512]{1,0:T(8,128)S(1)}, f32[80,512]{1,0:T(8,128)S(1)}, u32[]{:S(2)}, u32[]{:S(2)}) collective-permute-start(f32[80,512]{1,0:T(8,128)S(1)} %get-tuple-element.87), channel_id=1, source_target_pairs={{0,16},{16,32},{32,48},{48,64},{64,80},{80,96},{96,112},{112,128},... | collective-permute-start | bytes 491528 | tf_op jit(solution)/shard_map/ppermute | solution.py:53
  130.6 8.2 %collective-permute-start.9 = (f32[56,512]{1,0:T(8,128)S(1)}, f32[56,512]{1,0:T(8,128)S(1)}, u32[]{:S(2)}, u32[]{:S(2)}) collective-permute-start(f32[56,512]{1,0:T(8,128)S(1)} %get-tuple-element.88), channel_id=1, source_target_pairs={{16,0},{32,16},{48,32},{64,48},{80,64},{96,80},{112,96},{128,112},... | collective-permute-start | bytes 344072 | tf_op jit(solution)/shard_map/ppermute | solution.py:53
  132.5 6.3 %copy-start.3 = (f32[1,128,2048]{2,1,0:T(8,128)S(1)}, f32[1,128,2048]{2,1,0:T(8,128)}, u32[]{:S(2)}) copy-start(f32[1,128,2048]{2,1,0:T(8,128)} %inverse_ref.5) | copy-start | bytes 3145732
  132.5 6.3 %copy-start.9 = (f32[8,24,512]{2,1,0:T(8,128)S(1)}, f32[8,24,512]{2,1,0:T(8,128)}, u32[]{:S(2)}) copy-start(f32[8,24,512]{2,1,0:T(8,128)} %copy-done.4) | copy-start | bytes 1179652
  140.6 14.7 %all-to-all-start.4 = ((f32[16,2,128]{2,1,0:T(2,128)}), f32[16,2,128]{2,1,0:T(2,128)S(1)}, u32[]{:S(2)}, u32[]{:S(2)}) async-start(f32[16,2,128]{2,1,0:T(2,128)} %get-tuple-element.91), calls=%async_computation.4 | async-start | bytes 32768 | tf_op jit(solution)/shard_map/all_to_all | solution.py:57
  144.1 1.0 copy-start.10
  156.1 8.2 %collective-permute-start.10 = (f32[56,512]{1,0:T(8,128)S(1)}, f32[56,512]{1,0:T(8,128)S(1)}, u32[]{:S(2)}, u32[]{:S(2)}) collective-permute-start(f32[56,512]{1,0:T(8,128)S(1)} %get-tuple-element.97), channel_id=1, source_target_pairs={{16,0},{32,16},{48,32},{64,48},{80,64},{96,80},{112,96},{128,112},... | collective-permute-start | bytes 344072 | tf_op jit(solution)/shard_map/ppermute | solution.py:53

commit v4 on v3

--- a/solution.py
+++ b/solution.py
@@ -27,17 +27,19 @@
 E_SHAPE = (3, NZ + 2, GX, NY)
 H_SHAPE = (3, NZ + 1, GX, NY)
 PAY_SHAPE = (NB, 2, LANES)
-LAYERS = 8 * NZ + 2
+LAYERS = 8 * NZ
 SIDE_SHAPE = (LAYERS * DEEP, NY)
 WIDE = (NZ, GX, NY)
-UP_SHAPE, DOWN_SHAPE = (3 * GX + 8, NY), (2 * GX + 8, NY)
+UP_SHAPE, DOWN_SHAPE, TOP_SHAPE = (3 * GX + 8, NY), (2 * GX + 8, NY), (2 * GX, NY)
+LINES_SHAPE = (8, 2 * LANES)
 FIELD = (3, NZ, NX, NY)
 
 
 def call(kernel, outs, *args, alias=None, name=None, far=(), far_out=(), scratch=(), room=40 << 20):
+    args = [pltpu.with_memory_space_constraint(x, pltpu.HBM) if k in far else x for k, x in enumerate(args)]
     return pl.pallas_call(
         kernel,
-        out_shape=[jax.ShapeDtypeStruct(s, F32) for s in outs],
+        out_shape=[pltpu.HBM(s, F32) if k in far_out else jax.ShapeDtypeStruct(s, F32) for k, s in enumerate(outs)],
         in_specs=[ANY if k in far else VMEM for k in range(len(args))],
         out_specs=[ANY if k in far_out else VMEM for k in range(len(outs))],
         scratch_shapes=list(scratch),
@@ -149,33 +151,40 @@
 
 
 def k_first(
-    e_ref, h_ref, cell_ref, node_ref, cond_ref, far_ref, delay_ref, imped_ref, near_hist_ref,
-    pay_out, up_ref, right_ref,
-    ez, side, cell, node, cond, far, delay, imped, hist, pay_ref, sems,
+    e_in, h_in, d_in, g_in, cell_ref, node_ref, cond_ref, far_ref, delay_ref, imped_ref, near_hist_ref,
+    pay_out, lines_ref, right_out, left_out,
+    e_ref, h_ref, d_ref, g_ref, cell, node, cond, far, delay, imped, hist, pay_ref, right_ref, left_ref, sems,
 ):
     pairs = [
-        (cell_ref, cell), (node_ref, node), (cond_ref, cond), (e_ref.at[2], ez),
+        (cell_ref, cell), (node_ref, node), (cond_ref, cond), (e_in.at[2], e_ref.at[2]),
+        (e_in.at[0:2], e_ref.at[0:2]), (h_in, h_ref), (d_in, d_ref), (g_in, g_ref),
         (far_ref, far), (delay_ref, delay), (imped_ref, imped), (near_hist_ref, hist),
-        (h_ref.at[0, NZ - 1], up_ref.at[0:NX]), (h_ref.at[1, NZ - 1], up_ref.at[NX : 2 * NX]),
-        (h_ref.at[1:3, :, NX - 8 : NX], side),
     ]
     started = copies(pairs, sems)
-    up_ref[2 * NX :] = jnp.zeros((8, NY), F32)
+    lines_ref[...] = jnp.zeros(LINES_SHAPE, F32)
     wait(started[:4])
-    here = at_ports(ez[...].reshape(NZ * NX, NY), own_ports(cell[...]))
+    here = at_ports(e_ref[2].reshape(NZ * NX, NY), own_ports(cell[...]))
     first = jnp.concatenate([node[...], cell[...]], 1).astype(F32)
     second = jnp.concatenate([cond[...], here[:, :HALF]], 1)
-    sending = payload(pay_out, pay_ref, sems.at[11], first, second)
-    wait(started[4:])
-    up_ref[2 * NX : 2 * NX + 1, 0:LANES] = far[...].astype(F32)
-    up_ref[2 * NX + 1 : 2 * NX + 2, 0:LANES] = delay[...].astype(F32)
-    up_ref[2 * NX + 2 : 2 * NX + 3, 0:LANES] = imped[...]
+    sending = [payload(pay_out, pay_ref, sems.at[12], first, second)]
+    wait(started[4:8])
+    layers = [(ref, (c, z)) for ref in (e_ref, h_ref) for c in range(3) for z in range(NZ)]
+    layers += [(ref, (z,)) for ref in (d_ref, g_ref) for z in range(NZ)]
+    for k in range(0, LAYERS, 2):
+        tiles = [ref[(*at, slice(NX - 8, NX))] for ref, at in layers[k : k + 2]]
+        right_ref[k * DEEP : (k + 2) * DEEP] = jnp.concatenate([t[DEEP:] for t in tiles], 0)
+        tiles = [ref[(*at, slice(0, 8))] for ref, at in layers[k : k + 2]]
+        left_ref[k * DEEP : (k + 2) * DEEP] = jnp.concatenate([t[:DEEP] for t in tiles], 0)
+    for k, (a, b) in enumerate(((right_ref, right_out), (left_ref, left_out))):
+        sending.append(pltpu.make_async_copy(a, b, sems.at[13 + k]))
+        sending[-1].start()
+    wait(started[8:])
+    lines_ref[0:1, 0:LANES] = far[...].astype(F32)
+    lines_ref[1:2, 0:LANES] = delay[...].astype(F32)
+    lines_ref[2:3, 0:LANES] = imped[...]
     for k in range(DEPTH):
-        up_ref[2 * NX + k : 2 * NX + k + 1, LANES : 2 * LANES] = hist[k]
-    for c in range(2):
-        for z in range(NZ):
-            right_ref[c * NZ + z : c * NZ + z + 1] = side[c, z, 7:8]
-    sending.wait()
+        lines_ref[k : k + 1, LANES:] = hist[k]
+    wait(sending)
 
 
 def update_e(e_ref, h_ref, d_ref, g_ref, components, width):
@@ -199,76 +208,53 @@
 
 
 def k_start(
-    e_in, h_in, d_in, g_in, cell_in, up_ref, right_ref, e_ref, h_ref, pre_ref, right_out, left_out,
-    d_ref, g_ref, cell_ref, send_right, send_left, sems,
+    e_in, h_in, d_in, g_in, right_ref, left_ref, cell_in, lines_ref, e_ref, h_ref, d_out, g_out, pre_ref, top_ref,
+    d_ref, g_ref, cell_ref, sems,
 ):
-    pairs = [(e_in, own_rows(e_ref)), (h_in, own_rows(h_ref)), (d_in, d_ref), (g_in, g_ref), (cell_in, cell_ref)]
+    pairs = [
+        (d_in, d_ref.at[:, 0:NX]), (g_in, g_ref.at[:, 0:NX]), (e_in, own_rows(e_ref)), (h_in, own_rows(h_ref)), (cell_in, cell_ref),
+    ]
     started = copies(pairs, sems)
-    first = iota((8, NY), 0)
-    for z in range(NZ):
-        h_ref[0, z + 1, NX:] = jnp.zeros((8, NY), F32)
-        for c in range(2):
-            ghost = right_ref[c * NZ + z : c * NZ + z + 1]
-            h_ref[1 + c, z + 1, NX:] = jnp.where(first == 7, ghost, 0.0)
     for c in range(3):
         h_ref[c, 0] = jnp.zeros((GX, NY), F32)
         e_ref[c, 0] = jnp.zeros((GX, NY), F32)
         e_ref[c, NZ + 1] = jnp.zeros((GX, NY), F32)
-    h_ref[0, 0, :NX] = up_ref[0:NX]
-    h_ref[1, 0, :NX] = up_ref[NX : 2 * NX]
-    wait(started)
-    update_e(e_ref, h_ref, d_ref, g_ref, (0, 1, 2), NX)
-    layers = [(e_ref, (c, z + 1)) for c in range(3) for z in range(NZ)]
-    layers += [(h_ref, (c, z + 1)) for c in range(3) for z in range(NZ)] + [(h_ref, (c, 0)) for c in range(2)]
-    layers += [(d_ref, (z,)) for z in range(NZ)] + [(g_ref, (z,)) for z in range(NZ)]
-    for k, (ref, at) in enumerate(layers):
-        send_right[k * DEEP : (k + 1) * DEEP] = ref[(*at, slice(NX - DEEP, NX))]
-        send_left[k * DEEP : (k + 1) * DEEP] = ref[(*at, slice(0, DEEP))]
-    started = copies([(send_right, right_out), (send_left, left_out)], sems)
-    ports = own_ports(cell_ref[...])
-    pre = at_ports(e_ref[2, 1 : NZ + 1, :NX].reshape(NZ * NX, NY), ports)
-    gain = at_ports(g_ref[...].reshape(NZ * NX, NY), ports)
-    pre_ref[...] = jnp.broadcast_to(pre + pltpu.roll(gain, HALF, 1), (8, LANES))
-    wait(started)
-
-
-def k_widen(right_in, left_in, d_in, g_in, e_in, h_in, e_ref, h_ref, d_out, g_out, right_ref, left_ref, d_tile, g_tile, sems):
-    pairs = [(right_in, right_ref), (left_in, left_ref), (d_in, d_out.at[:, 0:NX]), (g_in, g_out.at[:, 0:NX])]
-    started = copies(pairs, sems)
-    wait(started[:2])
 
     def tile(k):
         rows = slice(k * DEEP, (k + 1) * DEEP)
         return jnp.concatenate([left_ref[rows], right_ref[rows]], 0)
 
     for z in range(NZ):
-        d_tile[z] = tile(6 * NZ + 2 + z)
-        g_tile[z] = tile(7 * NZ + 2 + z)
-    more = [pltpu.make_async_copy(d_tile, d_out.at[:, NX:], sems.at[4]), pltpu.make_async_copy(g_tile, g_out.at[:, NX:], sems.at[5])]
+        d_ref[z, NX:] = tile(6 * NZ + z)
+        g_ref[z, NX:] = tile(7 * NZ + z)
+    wait(started[:2])
+    more = [pltpu.make_async_copy(d_ref, d_out, sems.at[5]), pltpu.make_async_copy(g_ref, g_out, sems.at[6])]
     for copy in more:
         copy.start()
     for c in range(3):
         for z in range(NZ):
             e_ref[c, z + 1, NX:] = tile(c * NZ + z)
             h_ref[c, z + 1, NX:] = tile(3 * NZ + c * NZ + z)
+    wait(started[2:])
+    update_e(e_ref, h_ref, d_ref, g_ref, (2,), GX)
     for c in range(2):
-        h_ref[c, 0, NX:] = tile(6 * NZ + c)
-    wait(started[2:])
+        top_ref[c * GX : (c + 1) * GX] = h_ref[c, NZ]
+    ports = own_ports(cell_ref[...])
+    pre = at_ports(e_ref[2, 1 : NZ + 1, :NX].reshape(NZ * NX, NY), ports)
+    gain = at_ports(g_ref[:, :NX].reshape(NZ * NX, NY), ports)
+    pre_ref[...] = jnp.broadcast_to(pre + pltpu.roll(gain, HALF, 1), (8, LANES))
     wait(more)
 
 
 def low_onehots(node):
-    return [ones_where(iota((LANES, LANES), 0) == node[t : t + 1] % LANES) for t in range(10)]
+    return jnp.concatenate([ones_where(iota((LANES, LANES), 0) == node[t : t + 1] % LANES) for t in range(10)], 1)
 
 
 def own_volts(w, lines, node, inverse_ref):
     high = node // LANES
-    sources = jnp.zeros((NB, LANES), F32)
     values = jnp.concatenate([w, lines], 0)
-    onehots = low_onehots(node)
-    for t in range(10):
-        spread = jnp.where(iota((NB, LANES), 0) == high[t : t + 1], values[t : t + 1], 0.0)
-        sources = sources + dot3(spread, onehots[t], NT)
+    spread = [jnp.where(iota((NB, LANES), 0) == high[t : t + 1], values[t : t + 1], 0.0) for t in range(10)]
+    sources = dot3(jnp.concatenate(spread, 1), low_onehots(node), NT)
     total = jnp.zeros((LANES, LANES), F32)
     for t in range(NB):
         total = total + inverse_ref[0, :, t * LANES : (t + 1) * LANES] * sources[t : t + 1]
@@ -277,11 +263,11 @@
 
 def node_values(volts, node):
     high = node // LANES
+    picked = dot3(volts, low_onehots(node))
     rows = []
-    onehots = low_onehots(node)
     for t in range(10):
-        picked = dot3(volts, onehots[t])
-        rows.append(jnp.sum(jnp.where(iota((NB, LANES), 0) == high[t : t + 1], picked, 0.0), 0, keepdims=True))
+        mine = jnp.where(iota((NB, LANES), 0) == high[t : t + 1], picked[:, t * LANES : (t + 1) * LANES], 0.0)
+        rows.append(jnp.sum(mine, 0, keepdims=True))
     return jnp.concatenate(rows, 0)
 
 
@@ -310,7 +296,7 @@
 
 
 def k_tables(
-    got_ref, up_ref, pre_ref, near_in, delay_in, imped_in, near_hist_in, far_hist_in, inverse_in,
+    got_ref, lines_ref, pre_ref, near_in, delay_in, imped_in, near_hist_in, far_hist_in, inverse_in,
     pay_out, state_ref,
     near_ref, delay_ref, imped_ref, near_hist_ref, far_hist_ref, inverse_ref, pay_ref, sems,
 ):
@@ -325,18 +311,18 @@
     state_ref[WHERE : WHERE + 8] = upper(got_ref, 0) + (device * (NZ * NX * NY)).astype(F32)
     state_ref[COND : COND + 8] = lower(got_ref, 1)
     state_ref[EZ : EZ + 8] = upper(got_ref, 1)
-    far_below = up_ref[2 * NX : 2 * NX + 1, 0:LANES]
-    imped_below = jnp.where(row() == 0, 1.0, up_ref[2 * NX + 2 : 2 * NX + 3, 0:LANES])
+    far_below = lines_ref[0:1, 0:LANES]
+    imped_below = jnp.where(row() == 0, 1.0, lines_ref[2:3, 0:LANES])
     wait(started[:5])
     near = near_ref[...].astype(F32)
-    static = [near, far_below, imped_ref[...], imped_below, delay_ref[...].astype(F32), up_ref[2 * NX + 1 : 2 * NX + 2, 0:LANES]]
+    static = [near, far_below, imped_ref[...], imped_below, delay_ref[...].astype(F32), lines_ref[1:2, 0:LANES]]
     state_ref[NODE + 8 : NODE + 10] = jnp.concatenate(static[:2], 0)
     state_ref[STATIC : STATIC + 6] = jnp.concatenate(static, 0)
     for k in range(DEPTH):
         back = DEPTH - 1 - k
         state_ref[OWN + k : OWN + k + 1] = near_hist_ref[back]
         state_ref[FROM_ABOVE + k : FROM_ABOVE + k + 1] = far_hist_ref[back]
-        state_ref[FROM_BELOW + k : FROM_BELOW + k + 1] = up_ref[2 * NX + back : 2 * NX + back + 1, LANES : 2 * LANES]
+        state_ref[FROM_BELOW + k : FROM_BELOW + k + 1] = lines_ref[back : back + 1, LANES:]
     wait(started[5:])
     payload(pay_out, pay_ref, sems.at[6], next_volts(state_ref, inverse_ref, 0), pre_ref[0:1]).wait()
 
@@ -454,6 +440,12 @@
     update_e(e_ref, h_ref, d_ref, g_ref, (2,), GX)
     pre = at_ports(e_ref[2, 1 : NZ + 1, :NX].reshape(NZ * NX, NY), own_ports(cell_ref[...]))
     payload(pay_out, pay_ref, sem, volts, pre).wait()
+
+
+def k_exy_first(top_ref, d_ref, g_ref, e_in, h_in, e_ref, h_ref):
+    for c in range(2):
+        h_ref[c, 0] = top_ref[c * GX : (c + 1) * GX]
+    update_e(e_ref, h_ref, d_ref, g_ref, (0, 1), GX)
 
 
 def k_exy(h_ref, d_ref, g_ref, e_in, e_ref):
@@ -495,37 +487,35 @@
     block = pltpu.VMEM((NZ, NX, NY), F32)
     pay_scratch = pltpu.VMEM(PAY_SHAPE, F32)
     side = pltpu.VMEM(SIDE_SHAPE, F32)
-    tiles = pltpu.VMEM((NZ, 8, NY), F32)
-
-    pay, up, right = call(
+    wide = pltpu.VMEM(WIDE, F32)
+
+    pay, lines, to_right, to_left = call(
         k_first,
-        [PAY_SHAPE, (2 * NX + 8, NY), (2 * NZ, NY)],
-        e_field, h_field, port_cell, port_node, port_conductance, line_far, line_delay, line_imped, hist_near,
-        far=range(9),
+        [PAY_SHAPE, LINES_SHAPE, SIDE_SHAPE, SIDE_SHAPE],
+        e_field, h_field, e_decay, e_gain, port_cell, port_node, port_conductance, line_far, line_delay, line_imped, hist_near,
+        far=range(11),
+        far_out=(0, 2, 3),
         scratch=[
-            block, pltpu.VMEM((2, NZ, 8, NY), F32), ports_int, ports_int, pltpu.VMEM((1, HALF), F32),
-            line_int, line_int, line, hist_shape, pay_scratch, pltpu.SemaphoreType.DMA((12,)),
+            pltpu.VMEM(FIELD, F32), pltpu.VMEM(FIELD, F32), block, block, ports_int, ports_int, pltpu.VMEM((1, HALF), F32),
+            line_int, line_int, line, hist_shape, pay_scratch, side, side, pltpu.SemaphoreType.DMA((15,)),
         ],
-        far_out=(0,),
-        room=67000000,
         name="first",
     )
     got = exchanged(pay)
-    up = shifted(up, "fz", 1)
-    right = shifted(right, "fxy", 1)
-    e, h, pre, to_right, to_left = call(
+    lines = shifted(lines, "fz", 1)
+    e, h, d, g, pre, top = call(
         k_start,
-        [E_SHAPE, H_SHAPE, (8, LANES), SIDE_SHAPE, SIDE_SHAPE],
-        e_field, h_field, e_decay, e_gain, port_cell, up, right,
-        far=range(5),
-        far_out=(3, 4),
-        scratch=[block, block, ports_int, side, side, pltpu.SemaphoreType.DMA((5,))],
+        [E_SHAPE, H_SHAPE, WIDE, WIDE, (8, LANES), TOP_SHAPE],
+        e_field, h_field, e_decay, e_gain, shifted(to_right, "fxy", 1), shifted(to_left, "fxy", -1), port_cell, lines,
+        far=(0, 1, 2, 3, 6),
+        far_out=(2, 3),
+        scratch=[wide, wide, ports_int, pltpu.SemaphoreType.DMA((7,))],
         name="start",
     )
     pay, state = call(
         k_tables,
         [PAY_SHAPE, (ROWS, LANES)],
-        got, up, pre, line_near, line_delay, line_imped, hist_near, hist_far, inverse,
+        got, lines, pre, line_near, line_delay, line_imped, hist_near, hist_far, inverse,
         far=range(3, 9),
         scratch=[
             line_int, line_int, line, hist_shape, hist_shape,
@@ -534,20 +524,16 @@
         far_out=(0,),
         name="tables",
     )
-    to_right, to_left, pay = lax.optimization_barrier((to_right, to_left, pay))
     for n in range(STEPS):
         last = n == STEPS - 1
         got = exchanged(pay)
         if n == 0:
-            e, h, d, g = call(
-                k_widen,
-                [E_SHAPE, H_SHAPE, WIDE, WIDE],
-                shifted(to_right, "fxy", 1), shifted(to_left, "fxy", -1), e_decay, e_gain, e, h,
-                far=range(4),
-                far_out=(2, 3),
-                alias={4: 0, 5: 1},
-                scratch=[side, side, tiles, tiles, pltpu.SemaphoreType.DMA((6,))],
-                name="widen",
+            e, h = call(
+                k_exy_first,
+                [E_SHAPE, H_SHAPE],
+                shifted(top, "fz", 1), d, g, e, h,
+                alias={3: 0, 4: 1},
+                name="exy_first",
             )
         else:
             (e,) = call(k_exy, [E_SHAPE], h, d, g, e, alias={3: 0}, name="exy")

time: 167 us -> 162 us (0.970)
  local copies, waits for them, and re-layouts: 11.7 us -> 6.85 us
    unnamed x50 -> x30, local copies, waits for them, and re-layouts: 11.7 us -> 6.85 us
  transfers between devices with their start and end apart: 16 -> 16, of which waited for: 10 -> 9; matrix products, arithmetic and copies ran while one was open for 0% -> 0% of each run, Pallas kernels for 3% -> 5%
where the time goes in v4:
time: 162 us; the launch traced here: 161 us
  starting transfers between devices  71.5 us (44%)
  waiting for transfers between devices  62.6 us (39%)
  Pallas kernels  19.1 us (12%)
  local copies, waits for them, and re-layouts  6.85 us (4%)
    all_to_all x5, waiting for transfers between devices, exchanged(): return lax.all_to_all(value, 'fxy', 0, 0, tiled=True)  38.8 us
    all_to_all x5, starting transfers between devices, exchanged(): return lax.all_to_all(value, 'fxy', 0, 0, tiled=True)  38.8 us
    ppermute x11, starting transfers between devices, shifted(): return lax.ppermute(value, axis, pairs)  32.7 us
    ppermute x11, waiting for transfers between devices, shifted(): return lax.ppermute(value, axis, pairs)  23.8 us
    pallas_call x19, Pallas kernels, call(): pl.pallas_call(kernel, out_shape=[pltpu.HBM(s, F32) if k in far_out else...  19.1 us
    unnamed x30, local copies, waits for them, and re-layouts  6.85 us
  transfers between devices with their start and end apart: 16, of which 9 were waited for; matrix products, arithmetic and copies ran while one was open for 0% of the time, Pallas kernels for 5%

profile of v4, /device:TPU:7, one launch (start us, length us, event | category | flops | bytes accessed | tf_op | source)
XLA Modules:
  0.0 161.1 jit_solution(17878563010732929455)
XLA Ops:
  0.6 2.7 %first.1 = (f32[16,2,128]{2,1,0:T(2,128)}, f32[8,256]{1,0:T(8,128)S(1)}, f32[256,512]{1,0:T(8,128)}, f32[256,512]{1,0:T(8,128)}) custom-call(f32[3,8,16,512]{3,2,1,0:T(8,128)} %e_in.3, f32[3,8,16,512]{3,2,1,0:T(8,128)} %h_in.3, f32[8,16,512]{2,1,0:T(8,128)} %d_in.3, f32[8,16,512]{2,1,0:T(8,128)} %g_in.3, s32[1,64]{1,0:T(1,128)} %cell_ref.7, ...), custom_call_target="tpu_custom_call" | custom-call | tf_op jit(solution)/shard_map/first/pallas_call | solution.py:40
  3.3 3.6 %collective-permute-start.1 = (f32[256,512]{1,0:T(8,128)}, f32[256,512]{1,0:T(8,128)S(1)}, u32[]{:S(2)}, u32[]{:S(2)}) collective-permute-start(f32[256,512]{1,0:T(8,128)} %get-tuple-element.53), channel_id=1, source_target_pairs={{0,1},{1,2},{2,3},{3,4},{4,5},{5,6},{6,7},{7,8},{8,9},{9,10},{10,1... | collective-permute-start | bytes 1572872 | tf_op jit(solution)/shard_map/ppermute | solution.py:55
  6.9 1.3 collective-permute-start.2
  8.2 16.6 %all-to-all-start = ((f32[16,2,128]{2,1,0:T(2,128)}), f32[16,2,128]{2,1,0:T(2,128)S(1)}, u32[]{:S(2)}, u32[]{:S(2)}) async-start(f32[16,2,128]{2,1,0:T(2,128)} %get-tuple-element.51), calls=%async_computation | async-start | bytes 32768 | tf_op jit(solution)/shard_map/all_to_all | solution.py:59
  24.8 4.5 %collective-permute-start = (f32[8,256]{1,0:T(8,128)S(1)}, f32[8,256]{1,0:T(8,128)S(1)}, u32[]{:S(2)}, u32[]{:S(2)}) collective-permute-start(f32[8,256]{1,0:T(8,128)S(1)} %get-tuple-element.52), channel_id=1, source_target_pairs={{0,16},{16,32},{32,48},{48,64},{64,80},{80,96},{96,112},{112,128},... | collective-permute-start | bytes 24584 | tf_op jit(solution)/shard_map/ppermute | solution.py:55
  29.3 0.8 collective-permute-done.lines_ref
  30.1 0.0 collective-permute-done.2.left_ref
  30.1 0.8 copy-done.12
  30.9 1.0 copy-done.13
  31.9 2.2 %start.1 = (f32[3,10,24,512]{3,2,1,0:T(8,128)S(1)}, f32[3,9,24,512]{3,2,1,0:T(8,128)S(1)}, f32[8,24,512]{2,1,0:T(8,128)}, f32[8,24,512]{2,1,0:T(8,128)}, f32[8,128]{1,0:T(8,128)S(1)}, /*index=5*/f32[48,512]{1,0:T(8,128)S(1)}) custom-call(f32[3,8,16,512]{3,2,1,0:T(8,128)} %e_in.3, f32[3,8,16,512]{3,2,1,0:T(8,128)} %h_in.3, f32[8,16,512]{2,1,0:T(8,128)} %d_in.3, ...), custom_call_target="tpu_custom_call" | custom-call | tf_op jit(solution)/shard_map/start/pallas_call | solution.py:40
  34.1 6.3 %collective-permute-start.3 = (f32[48,512]{1,0:T(8,128)S(1)}, f32[48,512]{1,0:T(8,128)S(1)}, u32[]{:S(2)}, u32[]{:S(2)}) collective-permute-start(f32[48,512]{1,0:T(8,128)S(1)} %get-tuple-element.57), channel_id=1, source_target_pairs={{0,16},{16,32},{32,48},{48,64},{64,80},{80,96},{96,112},{112,128},... | collective-permute-start | bytes 294920 | tf_op jit(solution)/shard_map/ppermute | solution.py:55
  40.4 2.4 %tables.1 = (f32[16,2,128]{2,1,0:T(2,128)}, f32[112,128]{1,0:T(8,128)S(1)}) custom-call(f32[16,2,128]{2,1,0:T(2,128)S(1)} %all-to-all-done.got_ref, f32[8,256]{1,0:T(8,128)S(1)} %collective-permute-done.lines_ref, f32[8,128]{1,0:T(8,128)S(1)} %get-tuple-element.55.pre_ref, s32[1,128]{1,0:T(1,128)} %near_in.1, s32[1,128]{1,0:T(1,128)} %delay_in.1, ...), custom_call_target="tpu_custom_call" | custom-call | tf_op jit(solution)/shard_map/tables/pallas_call | solution.py:40
  42.8 11.7 %all-to-all-start.1 = ((f32[16,2,128]{2,1,0:T(2,128)}), f32[16,2,128]{2,1,0:T(2,128)S(1)}, u32[]{:S(2)}, u32[]{:S(2)}) async-start(f32[16,2,128]{2,1,0:T(2,128)} %get-tuple-element.56), calls=%async_computation.1 | async-start | bytes 32768 | tf_op jit(solution)/shard_map/all_to_all | solution.py:59
  54.6 0.0 copy-start
  54.6 1.0 copy-done
  55.6 1.0 copy-done.2
  56.6 0.3 exy_first.1
  56.9 9.0 %all-to-all-done.1.got_ref = f32[16,2,128]{2,1,0:T(2,128)S(1)} async-done(((f32[16,2,128]{2,1,0:T(2,128)}), f32[16,2,128]{2,1,0:T(2,128)S(1)}, u32[]{:S(2)}, u32[]{:S(2)}) %all-to-all-start.1) | async-done | bytes 16416 | tf_op jit(solution)/shard_map/all_to_all | solution.py:59
  65.9 0.7 currents.4
  66.7 3.4 %collective-permute-start.4 = (f32[80,512]{1,0:T(8,128)S(1)}, f32[80,512]{1,0:T(8,128)S(1)}, u32[]{:S(2)}, u32[]{:S(2)}) collective-permute-start(f32[80,512]{1,0:T(8,128)S(1)} %get-tuple-element.64), channel_id=1, source_target_pairs={{0,16},{16,32},{32,48},{48,64},{64,80},{80,96},{96,112},{112,128},... | collective-permute-start | bytes 491528 | tf_op jit(solution)/shard_map/ppermute | solution.py:55
  70.0 1.9 %collective-permute-start.5 = (f32[56,512]{1,0:T(8,128)S(1)}, f32[56,512]{1,0:T(8,128)S(1)}, u32[]{:S(2)}, u32[]{:S(2)}) collective-permute-start(f32[56,512]{1,0:T(8,128)S(1)} %get-tuple-element.65), channel_id=1, source_target_pairs={{16,0},{32,16},{48,32},{64,48},{80,64},{96,80},{112,96},{128,112},... | collective-permute-start | bytes 344072 | tf_op jit(solution)/shard_map/ppermute | solution.py:55
  72.0 0.0 copy-start.1
  72.0 0.0 copy-start.3
  72.0 0.0 copy-start.9
  72.0 0.0 copy-start.14
  72.0 0.3 inner_h.3.h_in
  72.3 5.9 %collective-permute-done.5.down_ref = f32[56,512]{1,0:T(8,128)S(1)} collective-permute-done((f32[56,512]{1,0:T(8,128)S(1)}, f32[56,512]{1,0:T(8,128)S(1)}, u32[]{:S(2)}, u32[]{:S(2)}) %collective-permute-start.5) | collective-permute-done | bytes 114720 | tf_op jit(solution)/shard_map/ppermute | solution.py:55
  78.3 1.3 volts.3
  79.6 3.5 %all-to-all-start.2 = ((f32[16,2,128]{2,1,0:T(2,128)}), f32[16,2,128]{2,1,0:T(2,128)S(1)}, u32[]{:S(2)}, u32[]{:S(2)}) async-start(f32[16,2,128]{2,1,0:T(2,128)} %get-tuple-element.69), calls=%async_computation.2 | async-start | bytes 32768 | tf_op jit(solution)/shard_map/all_to_all | solution.py:59
  83.1 0.0 copy-start.4
  83.1 1.0 copy-done.4
  84.1 0.3 exy.3.e_in
  84.4 9.9 %all-to-all-done.2.got_ref = f32[16,2,128]{2,1,0:T(2,128)S(1)} async-done(((f32[16,2,128]{2,1,0:T(2,128)}), f32[16,2,128]{2,1,0:T(2,128)S(1)}, u32[]{:S(2)}, u32[]{:S(2)}) %all-to-all-start.2) | async-done | bytes 16416 | tf_op jit(solution)/shard_map/all_to_all | solution.py:59
  94.3 0.7 currents.5
  95.0 3.0 %collective-permute-start.6 = (f32[80,512]{1,0:T(8,128)S(1)}, f32[80,512]{1,0:T(8,128)S(1)}, u32[]{:S(2)}, u32[]{:S(2)}) collective-permute-start(f32[80,512]{1,0:T(8,128)S(1)} %get-tuple-element.73), channel_id=1, source_target_pairs={{0,16},{16,32},{32,48},{48,64},{64,80},{80,96},{96,112},{112,128},... | collective-permute-start | bytes 491528 | tf_op jit(solution)/shard_map/ppermute | solution.py:55
  98.0 1.9 %collective-permute-start.7 = (f32[56,512]{1,0:T(8,128)S(1)}, f32[56,512]{1,0:T(8,128)S(1)}, u32[]{:S(2)}, u32[]{:S(2)}) collective-permute-start(f32[56,512]{1,0:T(8,128)S(1)} %get-tuple-element.74), channel_id=1, source_target_pairs={{16,0},{32,16},{48,32},{64,48},{80,64},{96,80},{112,96},{128,112},... | collective-permute-start | bytes 344072 | tf_op jit(solution)/shard_map/ppermute | solution.py:55
  100.0 0.0 copy-start.5
  100.0 0.0 copy-start.10
  100.0 0.3 inner_h.4.h_in
  100.3 6.0 %collective-permute-done.7.down_ref = f32[56,512]{1,0:T(8,128)S(1)} collective-permute-done((f32[56,512]{1,0:T(8,128)S(1)}, f32[56,512]{1,0:T(8,128)S(1)}, u32[]{:S(2)}, u32[]{:S(2)}) %collective-permute-start.7) | collective-permute-done | bytes 114720 | tf_op jit(solution)/shard_map/ppermute | solution.py:55
  106.3 1.3 volts.4
  107.5 3.5 %all-to-all-start.3 = ((f32[16,2,128]{2,1,0:T(2,128)}), f32[16,2,128]{2,1,0:T(2,128)S(1)}, u32[]{:S(2)}, u32[]{:S(2)}) async-start(f32[16,2,128]{2,1,0:T(2,128)} %get-tuple-element.77), calls=%async_computation.3 | async-start | bytes 32768 | tf_op jit(solution)/shard_map/all_to_all | solution.py:59
  111.1 0.0 copy-start.6
  111.1 1.0 copy-done.6
  112.1 0.3 exy.4.e_in
  112.4 9.9 %all-to-all-done.3.got_ref = f32[16,2,128]{2,1,0:T(2,128)S(1)} async-done(((f32[16,2,128]{2,1,0:T(2,128)}), f32[16,2,128]{2,1,0:T(2,128)S(1)}, u32[]{:S(2)}, u32[]{:S(2)}) %all-to-all-start.3) | async-done | bytes 16416 | tf_op jit(solution)/shard_map/all_to_all | solution.py:59
  122.3 0.7 currents.6
  123.0 3.0 %collective-permute-start.8 = (f32[80,512]{1,0:T(8,128)S(1)}, f32[80,512]{1,0:T(8,128)S(1)}, u32[]{:S(2)}, u32[]{:S(2)}) collective-permute-start(f32[80,512]{1,0:T(8,128)S(1)} %get-tuple-element.81), channel_id=1, source_target_pairs={{0,16},{16,32},{32,48},{48,64},{64,80},{80,96},{96,112},{112,128},... | collective-permute-start | bytes 491528 | tf_op jit(solution)/shard_map/ppermute | solution.py:55
  125.9 1.9 %collective-permute-start.9 = (f32[56,512]{1,0:T(8,128)S(1)}, f32[56,512]{1,0:T(8,128)S(1)}, u32[]{:S(2)}, u32[]{:S(2)}) collective-permute-start(f32[56,512]{1,0:T(8,128)S(1)} %get-tuple-element.82), channel_id=1, source_target_pairs={{16,0},{32,16},{48,32},{64,48},{80,64},{96,80},{112,96},{128,112},... | collective-permute-start | bytes 344072 | tf_op jit(solution)/shard_map/ppermute | solution.py:55
  127.9 0.0 copy-start.7
  127.9 0.0 copy-start.11
  127.9 0.3 inner_h.5.h_in
  128.2 6.0 %collective-permute-done.9.down_ref = f32[56,512]{1,0:T(8,128)S(1)} collective-permute-done((f32[56,512]{1,0:T(8,128)S(1)}, f32[56,512]{1,0:T(8,128)S(1)}, u32[]{:S(2)}, u32[]{:S(2)}) %collective-permute-start.9) | collective-permute-done | bytes 114720 | tf_op jit(solution)/shard_map/ppermute | solution.py:55
  134.2 1.8 %volts.5 = (f32[3,10,24,512]{3,2,1,0:T(8,128)S(1)}, f32[3,9,24,512]{3,2,1,0:T(8,128)S(1)}, f32[112,128]{1,0:T(8,128)S(1)}, f32[16,2,128]{2,1,0:T(2,128)}, f32[1,128]{1,0:T(1,128)}) custom-call(f32[80,512]{1,0:T(8,128)S(1)} %collective-permute-done.8.up_ref, ...), custom_call_target="tpu_custom_call", output_to_operand_aliasing={{0}: (6, {}), {1}: (7, {}), {2}: (8, {})} | custom-call | tf_op jit(solution)/shard_map/volts/pallas_call | solution.py:40
  136.0 3.5 %all-to-all-start.4 = ((f32[16,2,128]{2,1,0:T(2,128)}), f32[16,2,128]{2,1,0:T(2,128)S(1)}, u32[]{:S(2)}, u32[]{:S(2)}) async-start(f32[16,2,128]{2,1,0:T(2,128)} %get-tuple-element.85), calls=%async_computation.4 | async-start | bytes 32768 | tf_op jit(solution)/shard_map/all_to_all | solution.py:59
  139.5 0.0 copy-start.8
  139.5 1.0 copy-done.8
  140.5 0.3 exy.5.e_in
  140.8 10.0 %all-to-all-done.4.got_ref = f32[16,2,128]{2,1,0:T(2,128)S(1)} async-done(((f32[16,2,128]{2,1,0:T(2,128)}), f32[16,2,128]{2,1,0:T(2,128)S(1)}, u32[]{:S(2)}, u32[]{:S(2)}) %all-to-all-start.4) | async-done | bytes 16416 | tf_op jit(solution)/shard_map/all_to_all | solution.py:59
  150.8 0.7 currents.7
  151.5 1.9 %collective-permute-start.10 = (f32[56,512]{1,0:T(8,128)S(1)}, f32[56,512]{1,0:T(8,128)S(1)}, u32[]{:S(2)}, u32[]{:S(2)}) collective-permute-start(f32[56,512]{1,0:T(8,128)S(1)} %get-tuple-element.91), channel_id=1, source_target_pairs={{16,0},{32,16},{48,32},{64,48},{80,64},{96,80},{112,96},{128,112},... | collective-permute-start | bytes 344072 | tf_op jit(solution)/shard_map/ppermute | solution.py:55
  153.5 1.2 inner_last.1
  154.6 5.1 %collective-permute-done.10.down_ref = f32[56,512]{1,0:T(8,128)S(1)} collective-permute-done((f32[56,512]{1,0:T(8,128)S(1)}, f32[56,512]{1,0:T(8,128)S(1)}, u32[]{:S(2)}, u32[]{:S(2)}) %collective-permute-start.10) | collective-permute-done | bytes 114720 | tf_op jit(solution)/shard_map/ppermute | solution.py:55
  159.8 1.3 last.1
  (17 shorter events, 0.0 us)
Async XLA Ops:
  3.3 26.7 %collective-permute-start.1 = (f32[256,512]{1,0:T(8,128)}, f32[256,512]{1,0:T(8,128)S(1)}, u32[]{:S(2)}, u32[]{:S(2)}) collective-permute-start(f32[256,512]{1,0:T(8,128)} %get-tuple-element.53), channel_id=1, source_target_pairs={{0,1},{1,2},{2,3},{3,4},{4,5},{5,6},{6,7},{7,8},{8,9},{9,10},{10,1... | collective-permute-start | bytes 1572872 | tf_op jit(solution)/shard_map/ppermute | solution.py:55
  6.9 23.2 %collective-permute-start.2 = (f32[256,512]{1,0:T(8,128)}, f32[256,512]{1,0:T(8,128)S(1)}, u32[]{:S(2)}, u32[]{:S(2)}) collective-permute-start(f32[256,512]{1,0:T(8,128)} %get-tuple-element.54), channel_id=1, source_target_pairs={{1,0},{2,1},{3,2},{4,3},{5,4},{6,5},{7,6},{8,7},{9,8},{10,9},{11,1... | collective-permute-start | bytes 1572872 | tf_op jit(solution)/shard_map/ppermute | solution.py:55
  8.2 32.2 %all-to-all-start = ((f32[16,2,128]{2,1,0:T(2,128)}), f32[16,2,128]{2,1,0:T(2,128)S(1)}, u32[]{:S(2)}, u32[]{:S(2)}) async-start(f32[16,2,128]{2,1,0:T(2,128)} %get-tuple-element.51), calls=%async_computation | async-start | bytes 32768 | tf_op jit(solution)/shard_map/all_to_all | solution.py:59
  24.8 5.3 %collective-permute-start = (f32[8,256]{1,0:T(8,128)S(1)}, f32[8,256]{1,0:T(8,128)S(1)}, u32[]{:S(2)}, u32[]{:S(2)}) collective-permute-start(f32[8,256]{1,0:T(8,128)S(1)} %get-tuple-element.52), channel_id=1, source_target_pairs={{0,16},{16,32},{32,48},{48,64},{64,80},{80,96},{96,112},{112,128},... | collective-permute-start | bytes 24584 | tf_op jit(solution)/shard_map/ppermute | solution.py:55
  30.1 0.8 copy-start.12
  30.9 1.0 copy-start.13
  34.1 20.5 %collective-permute-start.3 = (f32[48,512]{1,0:T(8,128)S(1)}, f32[48,512]{1,0:T(8,128)S(1)}, u32[]{:S(2)}, u32[]{:S(2)}) collective-permute-start(f32[48,512]{1,0:T(8,128)S(1)} %get-tuple-element.57), channel_id=1, source_target_pairs={{0,16},{16,32},{32,48},{48,64},{64,80},{80,96},{96,112},{112,128},... | collective-permute-start | bytes 294920 | tf_op jit(solution)/shard_map/ppermute | solution.py:55
  42.8 23.1 %all-to-all-start.1 = ((f32[16,2,128]{2,1,0:T(2,128)}), f32[16,2,128]{2,1,0:T(2,128)S(1)}, u32[]{:S(2)}, u32[]{:S(2)}) async-start(f32[16,2,128]{2,1,0:T(2,128)} %get-tuple-element.56), calls=%async_computation.1 | async-start | bytes 32768 | tf_op jit(solution)/shard_map/all_to_all | solution.py:59
  54.6 1.0 copy-start
  55.6 1.0 copy-start.2
  66.7 11.6 %collective-permute-start.4 = (f32[80,512]{1,0:T(8,128)S(1)}, f32[80,512]{1,0:T(8,128)S(1)}, u32[]{:S(2)}, u32[]{:S(2)}) collective-permute-start(f32[80,512]{1,0:T(8,128)S(1)} %get-tuple-element.64), channel_id=1, source_target_pairs={{0,16},{16,32},{32,48},{48,64},{64,80},{80,96},{96,112},{112,128},... | collective-permute-start | bytes 491528 | tf_op jit(solution)/shard_map/ppermute | solution.py:55
  70.0 8.2 %collective-permute-start.5 = (f32[56,512]{1,0:T(8,128)S(1)}, f32[56,512]{1,0:T(8,128)S(1)}, u32[]{:S(2)}, u32[]{:S(2)}) collective-permute-start(f32[56,512]{1,0:T(8,128)S(1)} %get-tuple-element.65), channel_id=1, source_target_pairs={{16,0},{32,16},{48,32},{64,48},{80,64},{96,80},{112,96},{128,112},... | collective-permute-start | bytes 344072 | tf_op jit(solution)/shard_map/ppermute | solution.py:55
  72.0 6.3 %copy-start.1 = (f32[8,24,512]{2,1,0:T(8,128)S(1)}, f32[8,24,512]{2,1,0:T(8,128)}, u32[]{:S(2)}) copy-start(f32[8,24,512]{2,1,0:T(8,128)} %get-tuple-element.58.d_ref) | copy-start | bytes 1179652
  72.0 6.3 %copy-start.3 = (f32[8,24,512]{2,1,0:T(8,128)S(1)}, f32[8,24,512]{2,1,0:T(8,128)}, u32[]{:S(2)}) copy-start(f32[8,24,512]{2,1,0:T(8,128)} %get-tuple-element.59.g_ref) | copy-start | bytes 1179652
  72.0 6.3 %copy-start.9 = (f32[1,128,2048]{2,1,0:T(8,128)S(1)}, f32[1,128,2048]{2,1,0:T(8,128)}, u32[]{:S(2)}) copy-start(f32[1,128,2048]{2,1,0:T(8,128)} %inverse_ref.5) | copy-start | bytes 3145732
  72.0 6.3 %copy-start.14 = (s32[1,64]{1,0:T(1,128)S(1)}, s32[1,64]{1,0:T(1,128)}, u32[]{:S(2)}) copy-start(s32[1,64]{1,0:T(1,128)} %cell_ref.7) | copy-start | bytes 772
  79.6 14.7 %all-to-all-start.2 = ((f32[16,2,128]{2,1,0:T(2,128)}), f32[16,2,128]{2,1,0:T(2,128)S(1)}, u32[]{:S(2)}, u32[]{:S(2)}) async-start(f32[16,2,128]{2,1,0:T(2,128)} %get-tuple-element.69), calls=%async_computation.2 | async-start | bytes 32768 | tf_op jit(solution)/shard_map/all_to_all | solution.py:59
  83.1 1.0 copy-start.4
  95.0 11.2 %collective-permute-start.6 = (f32[80,512]{1,0:T(8,128)S(1)}, f32[80,512]{1,0:T(8,128)S(1)}, u32[]{:S(2)}, u32[]{:S(2)}) collective-permute-start(f32[80,512]{1,0:T(8,128)S(1)} %get-tuple-element.73), channel_id=1, source_target_pairs={{0,16},{16,32},{32,48},{48,64},{64,80},{80,96},{96,112},{112,128},... | collective-permute-start | bytes 491528 | tf_op jit(solution)/shard_map/ppermute | solution.py:55
  98.0 8.2 %collective-permute-start.7 = (f32[56,512]{1,0:T(8,128)S(1)}, f32[56,512]{1,0:T(8,128)S(1)}, u32[]{:S(2)}, u32[]{:S(2)}) collective-permute-start(f32[56,512]{1,0:T(8,128)S(1)} %get-tuple-element.74), channel_id=1, source_target_pairs={{16,0},{32,16},{48,32},{64,48},{80,64},{96,80},{112,96},{128,112},... | collective-permute-start | bytes 344072 | tf_op jit(solution)/shard_map/ppermute | solution.py:55
  100.0 6.3 %copy-start.5 = (f32[8,24,512]{2,1,0:T(8,128)S(1)}, f32[8,24,512]{2,1,0:T(8,128)}, u32[]{:S(2)}) copy-start(f32[8,24,512]{2,1,0:T(8,128)} %get-tuple-element.59.g_ref) | copy-start | bytes 1179652
  100.0 6.3 %copy-start.10 = (f32[1,128,2048]{2,1,0:T(8,128)S(1)}, f32[1,128,2048]{2,1,0:T(8,128)}, u32[]{:S(2)}) copy-start(f32[1,128,2048]{2,1,0:T(8,128)} %inverse_ref.5) | copy-start | bytes 3145732
  107.5 14.7 %all-to-all-start.3 = ((f32[16,2,128]{2,1,0:T(2,128)}), f32[16,2,128]{2,1,0:T(2,128)S(1)}, u32[]{:S(2)}, u32[]{:S(2)}) async-start(f32[16,2,128]{2,1,0:T(2,128)} %get-tuple-element.77), calls=%async_computation.3 | async-start | bytes 32768 | tf_op jit(solution)/shard_map/all_to_all | solution.py:59
  111.1 1.0 copy-start.6
  123.0 11.2 %collective-permute-start.8 = (f32[80,512]{1,0:T(8,128)S(1)}, f32[80,512]{1,0:T(8,128)S(1)}, u32[]{:S(2)}, u32[]{:S(2)}) collective-permute-start(f32[80,512]{1,0:T(8,128)S(1)} %get-tuple-element.81), channel_id=1, source_target_pairs={{0,16},{16,32},{32,48},{48,64},{64,80},{80,96},{96,112},{112,128},... | collective-permute-start | bytes 491528 | tf_op jit(solution)/shard_map/ppermute | solution.py:55
  125.9 8.2 %collective-permute-start.9 = (f32[56,512]{1,0:T(8,128)S(1)}, f32[56,512]{1,0:T(8,128)S(1)}, u32[]{:S(2)}, u32[]{:S(2)}) collective-permute-start(f32[56,512]{1,0:T(8,128)S(1)} %get-tuple-element.82), channel_id=1, source_target_pairs={{16,0},{32,16},{48,32},{64,48},{80,64},{96,80},{112,96},{128,112},... | collective-permute-start | bytes 344072 | tf_op jit(solution)/shard_map/ppermute | solution.py:55
  127.9 6.3 %copy-start.7 = (f32[8,24,512]{2,1,0:T(8,128)S(1)}, f32[8,24,512]{2,1,0:T(8,128)}, u32[]{:S(2)}) copy-start(f32[8,24,512]{2,1,0:T(8,128)} %get-tuple-element.59.g_ref) | copy-start | bytes 1179652
  127.9 6.3 %copy-start.11 = (f32[1,128,2048]{2,1,0:T(8,128)S(1)}, f32[1,128,2048]{2,1,0:T(8,128)}, u32[]{:S(2)}) copy-start(f32[1,128,2048]{2,1,0:T(8,128)} %inverse_ref.5) | copy-start | bytes 3145732
  136.0 14.8 %all-to-all-start.4 = ((f32[16,2,128]{2,1,0:T(2,128)}), f32[16,2,128]{2,1,0:T(2,128)S(1)}, u32[]{:S(2)}, u32[]{:S(2)}) async-start(f32[16,2,128]{2,1,0:T(2,128)} %get-tuple-element.85), calls=%async_computation.4 | async-start | bytes 32768 | tf_op jit(solution)/shard_map/all_to_all | solution.py:59
  139.5 1.0 copy-start.8
  151.5 8.2 %collective-permute-start.10 = (f32[56,512]{1,0:T(8,128)S(1)}, f32[56,512]{1,0:T(8,128)S(1)}, u32[]{:S(2)}, u32[]{:S(2)}) collective-permute-start(f32[56,512]{1,0:T(8,128)S(1)} %get-tuple-element.91), channel_id=1, source_target_pairs={{16,0},{32,16},{48,32},{64,48},{80,64},{96,80},{112,96},{128,112},... | collective-permute-start | bytes 344072 | tf_op jit(solution)/shard_map/ppermute | solution.py:55

commit v5 on v4

--- a/solution.py
+++ b/solution.py
@@ -30,8 +30,8 @@
 LAYERS = 8 * NZ
 SIDE_SHAPE = (LAYERS * DEEP, NY)
 WIDE = (NZ, GX, NY)
-UP_SHAPE, DOWN_SHAPE, TOP_SHAPE = (3 * GX + 8, NY), (2 * GX + 8, NY), (2 * GX, NY)
-LINES_SHAPE = (8, 2 * LANES)
+UP_SHAPE, DOWN_SHAPE = (3 * GX + 8, NY), (2 * GX + 8, NY)
+BELOW_SHAPE, CORNER_SHAPE = (2 * NX + 8, NY), (2 * DEEP, NY)
 FIELD = (3, NZ, NX, NY)
 
 
@@ -55,6 +55,11 @@
     return lax.ppermute(value, axis, pairs)
 
 
+def shifted_up(value, by):
+    pairs = [(s * NB + j, (s + 1) * NB + j + by) for s in range(NF - 1) for j in range(NB) if 0 <= j + by < NB]
+    return lax.ppermute(value, ("fz", "fxy"), pairs)
+
+
 def exchanged(value):
     return lax.all_to_all(value, "fxy", 0, 0, tiled=True)
 
@@ -152,7 +157,7 @@
 
 def k_first(
     e_in, h_in, d_in, g_in, cell_ref, node_ref, cond_ref, far_ref, delay_ref, imped_ref, near_hist_ref,
-    pay_out, lines_ref, right_out, left_out,
+    pay_out, below_ref, corner_right, corner_left, right_out, left_out,
     e_ref, h_ref, d_ref, g_ref, cell, node, cond, far, delay, imped, hist, pay_ref, right_ref, left_ref, sems,
 ):
     pairs = [
@@ -161,7 +166,7 @@
         (far_ref, far), (delay_ref, delay), (imped_ref, imped), (near_hist_ref, hist),
     ]
     started = copies(pairs, sems)
-    lines_ref[...] = jnp.zeros(LINES_SHAPE, F32)
+    below_ref[2 * NX :] = jnp.zeros((8, NY), F32)
     wait(started[:4])
     here = at_ports(e_ref[2].reshape(NZ * NX, NY), own_ports(cell[...]))
     first = jnp.concatenate([node[...], cell[...]], 1).astype(F32)
@@ -178,12 +183,16 @@
     for k, (a, b) in enumerate(((right_ref, right_out), (left_ref, left_out))):
         sending.append(pltpu.make_async_copy(a, b, sems.at[13 + k]))
         sending[-1].start()
+    for c in range(2):
+        below_ref[c * NX : (c + 1) * NX] = h_ref[c, NZ - 1]
+        corner_right[c * DEEP : (c + 1) * DEEP] = h_ref[c, NZ - 1, NX - DEEP :]
+        corner_left[c * DEEP : (c + 1) * DEEP] = h_ref[c, NZ - 1, :DEEP]
     wait(started[8:])
-    lines_ref[0:1, 0:LANES] = far[...].astype(F32)
-    lines_ref[1:2, 0:LANES] = delay[...].astype(F32)
-    lines_ref[2:3, 0:LANES] = imped[...]
+    below_ref[2 * NX : 2 * NX + 1, 0:LANES] = far[...].astype(F32)
+    below_ref[2 * NX + 1 : 2 * NX + 2, 0:LANES] = delay[...].astype(F32)
+    below_ref[2 * NX + 2 : 2 * NX + 3, 0:LANES] = imped[...]
     for k in range(DEPTH):
-        lines_ref[k : k + 1, LANES:] = hist[k]
+        below_ref[2 * NX + k : 2 * NX + k + 1, LANES : 2 * LANES] = hist[k]
     wait(sending)
 
 
@@ -208,17 +217,22 @@
 
 
 def k_start(
-    e_in, h_in, d_in, g_in, right_ref, left_ref, cell_in, lines_ref, e_ref, h_ref, d_out, g_out, pre_ref, top_ref,
-    d_ref, g_ref, cell_ref, sems,
+    e_in, h_in, d_in, g_in, cell_in, near_in, delay_in, imped_in, near_hist_in, far_hist_in,
+    right_in, left_in, below_ref, corner_right, corner_left,
+    e_ref, h_ref, d_out, g_out, pre_ref, state_ref,
+    right_ref, left_ref, d_ref, g_ref, cell_ref, near_ref, delay_ref, imped_ref, near_hist_ref, far_hist_ref, sems,
 ):
     pairs = [
         (d_in, d_ref.at[:, 0:NX]), (g_in, g_ref.at[:, 0:NX]), (e_in, own_rows(e_ref)), (h_in, own_rows(h_ref)), (cell_in, cell_ref),
+        (near_in, near_ref), (delay_in, delay_ref), (imped_in, imped_ref), (near_hist_in, near_hist_ref), (far_hist_in, far_hist_ref),
     ]
+    sides = copies([(right_in, right_ref), (left_in, left_ref)], sems.at[12:14])
     started = copies(pairs, sems)
     for c in range(3):
         h_ref[c, 0] = jnp.zeros((GX, NY), F32)
         e_ref[c, 0] = jnp.zeros((GX, NY), F32)
         e_ref[c, NZ + 1] = jnp.zeros((GX, NY), F32)
+    wait(sides)
 
     def tile(k):
         rows = slice(k * DEEP, (k + 1) * DEEP)
@@ -228,7 +242,7 @@
         d_ref[z, NX:] = tile(6 * NZ + z)
         g_ref[z, NX:] = tile(7 * NZ + z)
     wait(started[:2])
-    more = [pltpu.make_async_copy(d_ref, d_out, sems.at[5]), pltpu.make_async_copy(g_ref, g_out, sems.at[6])]
+    more = [pltpu.make_async_copy(d_ref, d_out, sems.at[10]), pltpu.make_async_copy(g_ref, g_out, sems.at[11])]
     for copy in more:
         copy.start()
     for c in range(3):
@@ -238,11 +252,27 @@
     wait(started[2:])
     update_e(e_ref, h_ref, d_ref, g_ref, (2,), GX)
     for c in range(2):
-        top_ref[c * GX : (c + 1) * GX] = h_ref[c, NZ]
+        rows = slice(c * DEEP, (c + 1) * DEEP)
+        h_ref[c, 0, :NX] = below_ref[c * NX : (c + 1) * NX]
+        h_ref[c, 0, NX:] = jnp.concatenate([corner_left[rows], corner_right[rows]], 0)
     ports = own_ports(cell_ref[...])
     pre = at_ports(e_ref[2, 1 : NZ + 1, :NX].reshape(NZ * NX, NY), ports)
     gain = at_ports(g_ref[:, :NX].reshape(NZ * NX, NY), ports)
     pre_ref[...] = jnp.broadcast_to(pre + pltpu.roll(gain, HALF, 1), (8, LANES))
+
+    state_ref[...] = jnp.zeros((ROWS, LANES), F32)
+    far_below = below_ref[2 * NX : 2 * NX + 1, 0:LANES]
+    imped_below = jnp.where(row() == 0, 1.0, below_ref[2 * NX + 2 : 2 * NX + 3, 0:LANES])
+    delay_below = below_ref[2 * NX + 1 : 2 * NX + 2, 0:LANES]
+    near = near_ref[...].astype(F32)
+    static = [near, far_below, imped_ref[...], imped_below, delay_ref[...].astype(F32), delay_below]
+    state_ref[NODE + 8 : NODE + 10] = jnp.concatenate(static[:2], 0)
+    state_ref[STATIC : STATIC + 6] = jnp.concatenate(static, 0)
+    for k in range(DEPTH):
+        back = DEPTH - 1 - k
+        state_ref[OWN + k : OWN + k + 1] = near_hist_ref[back]
+        state_ref[FROM_ABOVE + k : FROM_ABOVE + k + 1] = far_hist_ref[back]
+        state_ref[FROM_BELOW + k : FROM_BELOW + k + 1] = below_ref[2 * NX + back : 2 * NX + back + 1, LANES : 2 * LANES]
     wait(more)
 
 
@@ -250,11 +280,12 @@
     return jnp.concatenate([ones_where(iota((LANES, LANES), 0) == node[t : t + 1] % LANES) for t in range(10)], 1)
 
 
-def own_volts(w, lines, node, inverse_ref):
+def own_volts(w, lines, node, inverse_ref, ready):
     high = node // LANES
     values = jnp.concatenate([w, lines], 0)
     spread = [jnp.where(iota((NB, LANES), 0) == high[t : t + 1], values[t : t + 1], 0.0) for t in range(10)]
     sources = dot3(jnp.concatenate(spread, 1), low_onehots(node), NT)
+    ready()
     total = jnp.zeros((LANES, LANES), F32)
     for t in range(NB):
         total = total + inverse_ref[0, :, t * LANES : (t + 1) * LANES] * sources[t : t + 1]
@@ -281,11 +312,11 @@
     )
 
 
-def next_volts(state_ref, inverse_ref, n):
+def next_volts(state_ref, inverse_ref, n, ready=lambda: None):
     into_near, into_below, _ = line_inputs(state_ref, n)
     lines = -jnp.concatenate([into_near, into_below], 0)
     w = state_ref[COND : COND + 8] * state_ref[EZ : EZ + 8]
-    return own_volts(w, lines, state_ref[NODE : NODE + 16].astype(jnp.int32), inverse_ref)
+    return own_volts(w, lines, state_ref[NODE : NODE + 16].astype(jnp.int32), inverse_ref, ready)
 
 
 def payload(pay_out, pay_ref, sem, volts, pre):
@@ -295,36 +326,15 @@
     return copy
 
 
-def k_tables(
-    got_ref, lines_ref, pre_ref, near_in, delay_in, imped_in, near_hist_in, far_hist_in, inverse_in,
-    pay_out, state_ref,
-    near_ref, delay_ref, imped_ref, near_hist_ref, far_hist_ref, inverse_ref, pay_ref, sems,
-):
-    pairs = [
-        (near_in, near_ref), (delay_in, delay_ref), (imped_in, imped_ref),
-        (near_hist_in, near_hist_ref), (far_hist_in, far_hist_ref), (inverse_in, inverse_ref),
-    ]
-    started = copies(pairs, sems)
-    state_ref[...] = jnp.zeros((ROWS, LANES), F32)
+def k_tables(got_ref, pre_ref, inverse_in, state_in, pay_out, state_ref, inverse_ref, pay_ref, sems):
+    started = copies([(inverse_in, inverse_ref)], sems)
     state_ref[NODE : NODE + 8] = lower(got_ref, 0)
     device = iota((8, LANES), 0) + 8 * (iota((8, LANES), 1) // HALF)
     state_ref[WHERE : WHERE + 8] = upper(got_ref, 0) + (device * (NZ * NX * NY)).astype(F32)
     state_ref[COND : COND + 8] = lower(got_ref, 1)
     state_ref[EZ : EZ + 8] = upper(got_ref, 1)
-    far_below = lines_ref[0:1, 0:LANES]
-    imped_below = jnp.where(row() == 0, 1.0, lines_ref[2:3, 0:LANES])
-    wait(started[:5])
-    near = near_ref[...].astype(F32)
-    static = [near, far_below, imped_ref[...], imped_below, delay_ref[...].astype(F32), lines_ref[1:2, 0:LANES]]
-    state_ref[NODE + 8 : NODE + 10] = jnp.concatenate(static[:2], 0)
-    state_ref[STATIC : STATIC + 6] = jnp.concatenate(static, 0)
-    for k in range(DEPTH):
-        back = DEPTH - 1 - k
-        state_ref[OWN + k : OWN + k + 1] = near_hist_ref[back]
-        state_ref[FROM_ABOVE + k : FROM_ABOVE + k + 1] = far_hist_ref[back]
-        state_ref[FROM_BELOW + k : FROM_BELOW + k + 1] = lines_ref[back : back + 1, LANES:]
-    wait(started[5:])
-    payload(pay_out, pay_ref, sems.at[6], next_volts(state_ref, inverse_ref, 0), pre_ref[0:1]).wait()
+    volts = next_volts(state_ref, inverse_ref, 0, lambda: wait(started))
+    payload(pay_out, pay_ref, sems.at[1], volts, pre_ref[0:1]).wait()
 
 
 def block_row(k):
@@ -430,7 +440,9 @@
     state_ref[FROM_BELOW + at : FROM_BELOW + at + 1] = up_ref[3 * GX : 3 * GX + 1, 0:LANES]
     volts = next_volts(state_ref, inverse_ref, n)
     if last:
-        rest[0][...] = volts
+        rest[1][...] = volts
+        sending = pltpu.make_async_copy(rest[1], rest[0], rest[2])
+        sending.start()
     for c in range(3):
         e_ref[c, 0] = up_ref[c * GX : (c + 1) * GX]
     for c in range(2):
@@ -440,26 +452,23 @@
     update_e(e_ref, h_ref, d_ref, g_ref, (2,), GX)
     pre = at_ports(e_ref[2, 1 : NZ + 1, :NX].reshape(NZ * NX, NY), own_ports(cell_ref[...]))
     payload(pay_out, pay_ref, sem, volts, pre).wait()
-
-
-def k_exy_first(top_ref, d_ref, g_ref, e_in, h_in, e_ref, h_ref):
-    for c in range(2):
-        h_ref[c, 0] = top_ref[c * GX : (c + 1) * GX]
-    update_e(e_ref, h_ref, d_ref, g_ref, (0, 1), GX)
+    if last:
+        sending.wait()
 
 
 def k_exy(h_ref, d_ref, g_ref, e_in, e_ref):
     update_e(e_ref, h_ref, d_ref, g_ref, (0, 1), GX)
 
 
-def k_last(down_ref, state_ref, e_ref, h_ref, h_in, h_out, wave_out, layer_ref, sem):
+def k_last(down_ref, state_ref, e_ref, h_ref, h_in, h_out, wave_out, layer_ref, wave_ref, sems):
+    above = down_ref[2 * GX : 2 * GX + 1, 0:LANES] + state_ref[WAVE + 1 : WAVE + 2]
+    wave_ref[...] = jnp.concatenate([state_ref[WAVE : WAVE + 1], above], 0)[None]
+    sending = copies([(wave_ref, wave_out)], sems)
     for c, value in enumerate(new_h(e_ref, h_ref, NZ, down_ref[0:GX], down_ref[GX : 2 * GX])):
         layer_ref[c] = value[:NX]
-    copy = pltpu.make_async_copy(layer_ref, h_out.at[:, NZ - 1], sem)
-    copy.start()
-    above = down_ref[2 * GX : 2 * GX + 1, 0:LANES] + state_ref[WAVE + 1 : WAVE + 2]
-    wave_out[...] = jnp.concatenate([state_ref[WAVE : WAVE + 1], above], 0)[None]
-    copy.wait()
+    sending.append(pltpu.make_async_copy(layer_ref, h_out.at[:, NZ - 1], sems.at[1]))
+    sending[1].start()
+    wait(sending)
 
 
 def local(
@@ -489,12 +498,12 @@
     side = pltpu.VMEM(SIDE_SHAPE, F32)
     wide = pltpu.VMEM(WIDE, F32)
 
-    pay, lines, to_right, to_left = call(
+    pay, below, corner_right, corner_left, to_right, to_left = call(
         k_first,
-        [PAY_SHAPE, LINES_SHAPE, SIDE_SHAPE, SIDE_SHAPE],
+        [PAY_SHAPE, BELOW_SHAPE, CORNER_SHAPE, CORNER_SHAPE, SIDE_SHAPE, SIDE_SHAPE],
         e_field, h_field, e_decay, e_gain, port_cell, port_node, port_conductance, line_far, line_delay, line_imped, hist_near,
         far=range(11),
-        far_out=(0, 2, 3),
+        far_out=(0, 4, 5),
         scratch=[
             pltpu.VMEM(FIELD, F32), pltpu.VMEM(FIELD, F32), block, block, ports_int, ports_int, pltpu.VMEM((1, HALF), F32),
             line_int, line_int, line, hist_shape, pay_scratch, side, side, pltpu.SemaphoreType.DMA((15,)),
@@ -502,41 +511,31 @@
         name="first",
     )
     got = exchanged(pay)
-    lines = shifted(lines, "fz", 1)
-    e, h, d, g, pre, top = call(
+    e, h, d, g, pre, state = call(
         k_start,
-        [E_SHAPE, H_SHAPE, WIDE, WIDE, (8, LANES), TOP_SHAPE],
-        e_field, h_field, e_decay, e_gain, shifted(to_right, "fxy", 1), shifted(to_left, "fxy", -1), port_cell, lines,
-        far=(0, 1, 2, 3, 6),
+        [E_SHAPE, H_SHAPE, WIDE, WIDE, (8, LANES), (ROWS, LANES)],
+        e_field, h_field, e_decay, e_gain, port_cell, line_near, line_delay, line_imped, hist_near, hist_far,
+        shifted(to_right, "fxy", 1), shifted(to_left, "fxy", -1),
+        shifted(below, "fz", 1), shifted_up(corner_right, 1), shifted_up(corner_left, -1),
+        far=range(12),
         far_out=(2, 3),
-        scratch=[wide, wide, ports_int, pltpu.SemaphoreType.DMA((7,))],
+        scratch=[side, side, wide, wide, ports_int, line_int, line_int, line, hist_shape, hist_shape, pltpu.SemaphoreType.DMA((14,))],
         name="start",
     )
     pay, state = call(
         k_tables,
         [PAY_SHAPE, (ROWS, LANES)],
-        got, lines, pre, line_near, line_delay, line_imped, hist_near, hist_far, inverse,
-        far=range(3, 9),
-        scratch=[
-            line_int, line_int, line, hist_shape, hist_shape,
-            pltpu.VMEM((1, LANES, NB * LANES), F32), pay_scratch, pltpu.SemaphoreType.DMA((7,)),
-        ],
+        got, pre, inverse, state,
+        alias={3: 1},
+        far=(2,),
         far_out=(0,),
+        scratch=[pltpu.VMEM((1, LANES, NB * LANES), F32), pay_scratch, pltpu.SemaphoreType.DMA((2,))],
         name="tables",
     )
     for n in range(STEPS):
         last = n == STEPS - 1
         got = exchanged(pay)
-        if n == 0:
-            e, h = call(
-                k_exy_first,
-                [E_SHAPE, H_SHAPE],
-                shifted(top, "fz", 1), d, g, e, h,
-                alias={3: 0, 4: 1},
-                name="exy_first",
-            )
-        else:
-            (e,) = call(k_exy, [E_SHAPE], h, d, g, e, alias={3: 0}, name="exy")
+        (e,) = call(k_exy, [E_SHAPE], h, d, g, e, alias={3: 0}, name="exy")
         e, state, *sends = call(
             functools.partial(k_currents, n, last),
             [E_SHAPE, (ROWS, LANES)] + ([] if last else [UP_SHAPE]) + [DOWN_SHAPE],
@@ -554,8 +553,8 @@
             [E_SHAPE, H_SHAPE, (ROWS, LANES), PAY_SHAPE] + ([(1, LANES)] if n + 1 == STEPS - 1 else []),
             up, down, d, g, inverse, port_cell, e, h, state,
             alias={6: 0, 7: 1, 8: 2},
-            far_out=(3,),
-            scratch=[pay_scratch, pltpu.SemaphoreType.DMA],
+            far_out=(3, 4) if n + 1 == STEPS - 1 else (3,),
+            scratch=([line, pltpu.SemaphoreType.DMA] if n + 1 == STEPS - 1 else []) + [pay_scratch, pltpu.SemaphoreType.DMA],
             name="volts",
         )
     h, e_out, h_out = call(
@@ -573,8 +572,8 @@
         down, state, e, h, h_out,
         alias={4: 0},
         far=(4,),
-        far_out=(0,),
-        scratch=[pltpu.VMEM((3, NX, NY), F32), pltpu.SemaphoreType.DMA],
+        far_out=(0, 1),
+        scratch=[pltpu.VMEM((3, NX, NY), F32), pltpu.VMEM((1, 2, LANES), F32), pltpu.SemaphoreType.DMA((2,))],
         name="last",
     )
     return e_out, h_out, node_volt[0], line_wave

time: 162 us -> 166 us (1.025)
  waiting for transfers between devices: 62.6 us -> 66 us
  starting transfers between devices: 71.5 us -> 73.5 us
    ppermute x0 -> x2, starting transfers between devices: none -> 4.84 us  [shifted_up(): return lax.ppermute(value, ('fz', 'fxy'), pairs)]
    ppermute x0 -> x2, waiting for transfers between devices: none -> 4.04 us  [shifted_up(): return lax.ppermute(value, ('fz', 'fxy'), pairs)]
    ppermute x11 -> x10, starting transfers between devices: 32.7 us -> 29.7 us  [shifted(): return lax.ppermute(value, axis, pairs)]
    ppermute x11 -> x10, waiting for transfers between devices: 23.8 us -> 23 us  [shifted(): return lax.ppermute(value, axis, pairs)]
  transfers between devices with their start and end apart: 16 -> 17, of which waited for: 9 -> 9; matrix products, arithmetic and copies ran while one was open for 0% -> 0% of each run, Pallas kernels for 5% -> 3%
where the time goes in v5:
time: 166 us; the launch traced here: 165 us
  starting transfers between devices  73.5 us (44%)
  waiting for transfers between devices  66 us (40%)
  Pallas kernels  18 us (11%)
  local copies, waits for them, and re-layouts  6.57 us (4%)
    all_to_all x5, starting transfers between devices, exchanged(): return lax.all_to_all(value, 'fxy', 0, 0, tiled=True)  39 us
    all_to_all x5, waiting for transfers between devices, exchanged(): return lax.all_to_all(value, 'fxy', 0, 0, tiled=True)  38.9 us
    ppermute x10, starting transfers between devices, shifted(): return lax.ppermute(value, axis, pairs)  29.7 us
    ppermute x10, waiting for transfers between devices, shifted(): return lax.ppermute(value, axis, pairs)  23 us
    pallas_call x19, Pallas kernels, call(): pl.pallas_call(kernel, out_shape=[pltpu.HBM(s, F32) if k in far_out else...  18 us
    unnamed x30, local copies, waits for them, and re-layouts  6.57 us
    ppermute x2, starting transfers between devices, shifted_up(): return lax.ppermute(value, ('fz', 'fxy'), pairs)  4.84 us
    ppermute x2, waiting for transfers between devices, shifted_up(): return lax.ppermute(value, ('fz', 'fxy'), pairs)  4.04 us
  transfers between devices with their start and end apart: 17, of which 9 were waited for; matrix products, arithmetic and copies ran while one was open for 0% of the time, Pallas kernels for 3%

profile of v5, /device:TPU:7, one launch (start us, length us, event | category | flops | bytes accessed | tf_op | source)
XLA Modules:
  0.0 165.1 jit_solution(16640779680494520595)
XLA Ops:
  0.6 2.7 %first.1 = (f32[16,2,128]{2,1,0:T(2,128)}, f32[40,512]{1,0:T(8,128)S(1)}, f32[8,512]{1,0:T(8,128)S(1)}, f32[8,512]{1,0:T(8,128)S(1)}, f32[256,512]{1,0:T(8,128)}, /*index=5*/f32[256,512]{1,0:T(8,128)}) custom-call(f32[3,8,16,512]{3,2,1,0:T(8,128)} %e_in.3, f32[3,8,16,512]{3,2,1,0:T(8,128)} %h_in.3, f32[8,16,512]{2,1,0:T(8,128)} %d_in.3, f32[8,16,512]{2,1,0:T(8,128)} %g_in.3, ...), custom_call_target="tpu_custom_call" | custom-call | tf_op jit(solution)/shard_map/first/pallas_call | solution.py:40
  3.3 3.6 %collective-permute-start = (f32[256,512]{1,0:T(8,128)}, f32[256,512]{1,0:T(8,128)S(1)}, u32[]{:S(2)}, u32[]{:S(2)}) collective-permute-start(f32[256,512]{1,0:T(8,128)} %get-tuple-element.52), channel_id=1, source_target_pairs={{0,1},{1,2},{2,3},{3,4},{4,5},{5,6},{6,7},{7,8},{8,9},{9,10},{10,1... | collective-permute-start | bytes 1572872 | tf_op jit(solution)/shard_map/ppermute | solution.py:55
  6.9 1.3 collective-permute-start.1
  8.2 4.0 %collective-permute-start.2 = (f32[40,512]{1,0:T(8,128)S(1)}, f32[40,512]{1,0:T(8,128)S(1)}, u32[]{:S(2)}, u32[]{:S(2)}) collective-permute-start(f32[40,512]{1,0:T(8,128)S(1)} %get-tuple-element.54), channel_id=1, source_target_pairs={{0,16},{16,32},{32,48},{48,64},{64,80},{80,96},{96,112},{112,128},... | collective-permute-start | bytes 245768 | tf_op jit(solution)/shard_map/ppermute | solution.py:55
  12.2 16.8 %all-to-all-start = ((f32[16,2,128]{2,1,0:T(2,128)}), f32[16,2,128]{2,1,0:T(2,128)S(1)}, u32[]{:S(2)}, u32[]{:S(2)}) async-start(f32[16,2,128]{2,1,0:T(2,128)} %get-tuple-element.51), calls=%async_computation | async-start | bytes 32768 | tf_op jit(solution)/shard_map/all_to_all | solution.py:64
  29.0 3.5 %collective-permute-start.3 = (f32[8,512]{1,0:T(8,128)S(1)}, f32[8,512]{1,0:T(8,128)S(1)}, u32[]{:S(2)}, u32[]{:S(2)}) collective-permute-start(f32[8,512]{1,0:T(8,128)S(1)} %get-tuple-element.55), channel_id=1, source_target_pairs={{0,17},{1,18},{2,19},{3,20},{4,21},{5,22},{6,23},{7,24},{8,25},{9,... | collective-permute-start | bytes 49160 | tf_op jit(solution)/shard_map/ppermute | solution.py:60
  32.6 1.3 collective-permute-start.4
  33.9 0.0 collective-permute-done.3.corner_right
  33.9 4.0 %collective-permute-done.4.corner_left = f32[8,512]{1,0:T(8,128)S(1)} collective-permute-done((f32[8,512]{1,0:T(8,128)S(1)}, f32[8,512]{1,0:T(8,128)S(1)}, u32[]{:S(2)}, u32[]{:S(2)}) %collective-permute-start.4) | collective-permute-done | bytes 16416 | tf_op jit(solution)/shard_map/ppermute | solution.py:60
  37.9 0.0 collective-permute-done.2.below_ref
  38.0 0.0 collective-permute-done.right_in
  38.0 0.0 collective-permute-done.1.left_in
  38.0 0.8 copy-done.13
  38.8 0.8 copy-done.14
  39.5 2.6 %start.1 = (f32[3,10,24,512]{3,2,1,0:T(8,128)S(1)}, f32[3,9,24,512]{3,2,1,0:T(8,128)S(1)}, f32[8,24,512]{2,1,0:T(8,128)}, f32[8,24,512]{2,1,0:T(8,128)}, f32[8,128]{1,0:T(8,128)S(1)}, /*index=5*/f32[112,128]{1,0:T(8,128)S(1)}) custom-call(f32[3,8,16,512]{3,2,1,0:T(8,128)} %e_in.3, f32[3,8,16,512]{3,2,1,0:T(8,128)} %h_in.3, f32[8,16,512]{2,1,0:T(8,128)} %d_in.3, ...), custom_call_target="tpu_custom_call" | custom-call | tf_op jit(solution)/shard_map/start/pallas_call | solution.py:40
  42.1 0.0 all-to-all-done.got_ref
  42.1 2.2 %tables.1 = (f32[16,2,128]{2,1,0:T(2,128)}, f32[112,128]{1,0:T(8,128)S(1)}) custom-call(f32[16,2,128]{2,1,0:T(2,128)S(1)} %all-to-all-done.got_ref, f32[8,128]{1,0:T(8,128)S(1)} %get-tuple-element.57.pre_ref, f32[1,128,2048]{2,1,0:T(8,128)} %inverse_ref.5, f32[112,128]{1,0:T(8,128)S(1)} %get-tuple-element.58.state_in), custom_call_target="tpu_custom_call", output_to_operand_aliasing={{1}: (3, {})} | custom-call | tf_op jit(solution)/shard_map/tables/pallas_call | solution.py:40
  44.3 11.6 %all-to-all-start.1 = ((f32[16,2,128]{2,1,0:T(2,128)}), f32[16,2,128]{2,1,0:T(2,128)S(1)}, u32[]{:S(2)}, u32[]{:S(2)}) async-start(f32[16,2,128]{2,1,0:T(2,128)} %get-tuple-element.59), calls=%async_computation.1 | async-start | bytes 32768 | tf_op jit(solution)/shard_map/all_to_all | solution.py:64
  56.0 1.0 copy-done
  57.0 1.0 copy-done.2
  57.9 0.3 exy.4.e_in
  58.2 9.1 %all-to-all-done.1.got_ref = f32[16,2,128]{2,1,0:T(2,128)S(1)} async-done(((f32[16,2,128]{2,1,0:T(2,128)}), f32[16,2,128]{2,1,0:T(2,128)S(1)}, u32[]{:S(2)}, u32[]{:S(2)}) %all-to-all-start.1) | async-done | bytes 16416 | tf_op jit(solution)/shard_map/all_to_all | solution.py:64
  67.3 0.7 currents.4
  68.1 7.3 %collective-permute-start.5 = (f32[80,512]{1,0:T(8,128)S(1)}, f32[80,512]{1,0:T(8,128)S(1)}, u32[]{:S(2)}, u32[]{:S(2)}) collective-permute-start(f32[80,512]{1,0:T(8,128)S(1)} %get-tuple-element.65), channel_id=1, source_target_pairs={{0,16},{16,32},{32,48},{48,64},{64,80},{80,96},{96,112},{112,128},... | collective-permute-start | bytes 491528 | tf_op jit(solution)/shard_map/ppermute | solution.py:55
  75.4 1.9 %collective-permute-start.6 = (f32[56,512]{1,0:T(8,128)S(1)}, f32[56,512]{1,0:T(8,128)S(1)}, u32[]{:S(2)}, u32[]{:S(2)}) collective-permute-start(f32[56,512]{1,0:T(8,128)S(1)} %get-tuple-element.66), channel_id=1, source_target_pairs={{16,0},{32,16},{48,32},{64,48},{80,64},{96,80},{112,96},{128,112},... | collective-permute-start | bytes 344072 | tf_op jit(solution)/shard_map/ppermute | solution.py:55
  77.3 0.0 copy-start.9
  77.3 0.0 copy-start.12
  77.3 0.3 inner_h.3.h_in
  77.6 6.0 %collective-permute-done.6.down_ref = f32[56,512]{1,0:T(8,128)S(1)} collective-permute-done((f32[56,512]{1,0:T(8,128)S(1)}, f32[56,512]{1,0:T(8,128)S(1)}, u32[]{:S(2)}, u32[]{:S(2)}) %collective-permute-start.6) | collective-permute-done | bytes 114720 | tf_op jit(solution)/shard_map/ppermute | solution.py:55
  83.6 0.0 collective-permute-done.5.up_ref
  83.6 1.2 volts.3
  84.9 3.5 %all-to-all-start.2 = ((f32[16,2,128]{2,1,0:T(2,128)}), f32[16,2,128]{2,1,0:T(2,128)S(1)}, u32[]{:S(2)}, u32[]{:S(2)}) async-start(f32[16,2,128]{2,1,0:T(2,128)} %get-tuple-element.69), calls=%async_computation.2 | async-start | bytes 32768 | tf_op jit(solution)/shard_map/all_to_all | solution.py:64
  88.4 1.0 copy-done.4
  89.4 0.3 exy.5.e_in
  89.7 9.9 %all-to-all-done.2.got_ref = f32[16,2,128]{2,1,0:T(2,128)S(1)} async-done(((f32[16,2,128]{2,1,0:T(2,128)}), f32[16,2,128]{2,1,0:T(2,128)S(1)}, u32[]{:S(2)}, u32[]{:S(2)}) %all-to-all-start.2) | async-done | bytes 16416 | tf_op jit(solution)/shard_map/all_to_all | solution.py:64
  99.6 0.7 currents.5
  100.3 2.9 %collective-permute-start.7 = (f32[80,512]{1,0:T(8,128)S(1)}, f32[80,512]{1,0:T(8,128)S(1)}, u32[]{:S(2)}, u32[]{:S(2)}) collective-permute-start(f32[80,512]{1,0:T(8,128)S(1)} %get-tuple-element.73), channel_id=1, source_target_pairs={{0,16},{16,32},{32,48},{48,64},{64,80},{80,96},{96,112},{112,128},... | collective-permute-start | bytes 491528 | tf_op jit(solution)/shard_map/ppermute | solution.py:55
  103.3 1.9 %collective-permute-start.8 = (f32[56,512]{1,0:T(8,128)S(1)}, f32[56,512]{1,0:T(8,128)S(1)}, u32[]{:S(2)}, u32[]{:S(2)}) collective-permute-start(f32[56,512]{1,0:T(8,128)S(1)} %get-tuple-element.74), channel_id=1, source_target_pairs={{16,0},{32,16},{48,32},{64,48},{80,64},{96,80},{112,96},{128,112},... | collective-permute-start | bytes 344072 | tf_op jit(solution)/shard_map/ppermute | solution.py:55
  105.2 0.0 copy-start.10
  105.2 0.3 inner_h.4.h_in
  105.5 6.0 %collective-permute-done.8.down_ref = f32[56,512]{1,0:T(8,128)S(1)} collective-permute-done((f32[56,512]{1,0:T(8,128)S(1)}, f32[56,512]{1,0:T(8,128)S(1)}, u32[]{:S(2)}, u32[]{:S(2)}) %collective-permute-start.8) | collective-permute-done | bytes 114720 | tf_op jit(solution)/shard_map/ppermute | solution.py:55
  111.5 0.0 collective-permute-done.7.up_ref
  111.5 1.2 volts.4
  112.7 3.5 %all-to-all-start.3 = ((f32[16,2,128]{2,1,0:T(2,128)}), f32[16,2,128]{2,1,0:T(2,128)S(1)}, u32[]{:S(2)}, u32[]{:S(2)}) async-start(f32[16,2,128]{2,1,0:T(2,128)} %get-tuple-element.77), calls=%async_computation.3 | async-start | bytes 32768 | tf_op jit(solution)/shard_map/all_to_all | solution.py:64
  116.3 1.0 copy-done.6
  117.2 0.3 exy.6.e_in
  117.5 9.9 %all-to-all-done.3.got_ref = f32[16,2,128]{2,1,0:T(2,128)S(1)} async-done(((f32[16,2,128]{2,1,0:T(2,128)}), f32[16,2,128]{2,1,0:T(2,128)S(1)}, u32[]{:S(2)}, u32[]{:S(2)}) %all-to-all-start.3) | async-done | bytes 16416 | tf_op jit(solution)/shard_map/all_to_all | solution.py:64
  127.4 0.7 currents.6
  128.2 3.0 %collective-permute-start.9 = (f32[80,512]{1,0:T(8,128)S(1)}, f32[80,512]{1,0:T(8,128)S(1)}, u32[]{:S(2)}, u32[]{:S(2)}) collective-permute-start(f32[80,512]{1,0:T(8,128)S(1)} %get-tuple-element.81), channel_id=1, source_target_pairs={{0,16},{16,32},{32,48},{48,64},{64,80},{80,96},{96,112},{112,128},... | collective-permute-start | bytes 491528 | tf_op jit(solution)/shard_map/ppermute | solution.py:55
  131.1 1.9 %collective-permute-start.10 = (f32[56,512]{1,0:T(8,128)S(1)}, f32[56,512]{1,0:T(8,128)S(1)}, u32[]{:S(2)}, u32[]{:S(2)}) collective-permute-start(f32[56,512]{1,0:T(8,128)S(1)} %get-tuple-element.82), channel_id=1, source_target_pairs={{16,0},{32,16},{48,32},{64,48},{80,64},{96,80},{112,96},{128,112},... | collective-permute-start | bytes 344072 | tf_op jit(solution)/shard_map/ppermute | solution.py:55
  133.1 0.0 copy-start.11
  133.1 0.3 inner_h.5.h_in
  133.4 6.0 %collective-permute-done.10.down_ref = f32[56,512]{1,0:T(8,128)S(1)} collective-permute-done((f32[56,512]{1,0:T(8,128)S(1)}, f32[56,512]{1,0:T(8,128)S(1)}, u32[]{:S(2)}, u32[]{:S(2)}) %collective-permute-start.10) | collective-permute-done | bytes 114720 | tf_op jit(solution)/shard_map/ppermute | solution.py:55
  139.4 0.0 collective-permute-done.9.up_ref
  139.4 1.3 volts.5
  140.6 3.5 %all-to-all-start.4 = ((f32[16,2,128]{2,1,0:T(2,128)}), f32[16,2,128]{2,1,0:T(2,128)S(1)}, u32[]{:S(2)}, u32[]{:S(2)}) async-start(f32[16,2,128]{2,1,0:T(2,128)} %get-tuple-element.85), calls=%async_computation.4 | async-start | bytes 32768 | tf_op jit(solution)/shard_map/all_to_all | solution.py:64
  144.2 1.0 copy-done.8
  145.2 0.3 exy.7.e_in
  145.4 9.9 %all-to-all-done.4.got_ref = f32[16,2,128]{2,1,0:T(2,128)S(1)} async-done(((f32[16,2,128]{2,1,0:T(2,128)}), f32[16,2,128]{2,1,0:T(2,128)S(1)}, u32[]{:S(2)}, u32[]{:S(2)}) %all-to-all-start.4) | async-done | bytes 16416 | tf_op jit(solution)/shard_map/all_to_all | solution.py:64
  155.4 0.7 currents.7
  156.1 1.9 %collective-permute-start.11 = (f32[56,512]{1,0:T(8,128)S(1)}, f32[56,512]{1,0:T(8,128)S(1)}, u32[]{:S(2)}, u32[]{:S(2)}) collective-permute-start(f32[56,512]{1,0:T(8,128)S(1)} %get-tuple-element.91), channel_id=1, source_target_pairs={{16,0},{32,16},{48,32},{64,48},{80,64},{96,80},{112,96},{128,112},... | collective-permute-start | bytes 344072 | tf_op jit(solution)/shard_map/ppermute | solution.py:55
  158.0 1.2 inner_last.1
  159.2 5.1 %collective-permute-done.11.down_ref = f32[56,512]{1,0:T(8,128)S(1)} collective-permute-done((f32[56,512]{1,0:T(8,128)S(1)}, f32[56,512]{1,0:T(8,128)S(1)}, u32[]{:S(2)}, u32[]{:S(2)}) %collective-permute-start.11) | collective-permute-done | bytes 114720 | tf_op jit(solution)/shard_map/ppermute | solution.py:55
  164.3 0.7 last.1
  (19 shorter events, 0.0 us)
Async XLA Ops:
  3.3 34.6 %collective-permute-start = (f32[256,512]{1,0:T(8,128)}, f32[256,512]{1,0:T(8,128)S(1)}, u32[]{:S(2)}, u32[]{:S(2)}) collective-permute-start(f32[256,512]{1,0:T(8,128)} %get-tuple-element.52), channel_id=1, source_target_pairs={{0,1},{1,2},{2,3},{3,4},{4,5},{5,6},{6,7},{7,8},{8,9},{9,10},{10,1... | collective-permute-start | bytes 1572872 | tf_op jit(solution)/shard_map/ppermute | solution.py:55
  6.9 31.0 %collective-permute-start.1 = (f32[256,512]{1,0:T(8,128)}, f32[256,512]{1,0:T(8,128)S(1)}, u32[]{:S(2)}, u32[]{:S(2)}) collective-permute-start(f32[256,512]{1,0:T(8,128)} %get-tuple-element.53), channel_id=1, source_target_pairs={{1,0},{2,1},{3,2},{4,3},{5,4},{6,5},{7,6},{8,7},{9,8},{10,9},{11,1... | collective-permute-start | bytes 1572872 | tf_op jit(solution)/shard_map/ppermute | solution.py:55
  8.2 29.7 %collective-permute-start.2 = (f32[40,512]{1,0:T(8,128)S(1)}, f32[40,512]{1,0:T(8,128)S(1)}, u32[]{:S(2)}, u32[]{:S(2)}) collective-permute-start(f32[40,512]{1,0:T(8,128)S(1)} %get-tuple-element.54), channel_id=1, source_target_pairs={{0,16},{16,32},{32,48},{48,64},{64,80},{80,96},{96,112},{112,128},... | collective-permute-start | bytes 245768 | tf_op jit(solution)/shard_map/ppermute | solution.py:55
  12.2 29.9 %all-to-all-start = ((f32[16,2,128]{2,1,0:T(2,128)}), f32[16,2,128]{2,1,0:T(2,128)S(1)}, u32[]{:S(2)}, u32[]{:S(2)}) async-start(f32[16,2,128]{2,1,0:T(2,128)} %get-tuple-element.51), calls=%async_computation | async-start | bytes 32768 | tf_op jit(solution)/shard_map/all_to_all | solution.py:64
  29.0 4.9 %collective-permute-start.3 = (f32[8,512]{1,0:T(8,128)S(1)}, f32[8,512]{1,0:T(8,128)S(1)}, u32[]{:S(2)}, u32[]{:S(2)}) collective-permute-start(f32[8,512]{1,0:T(8,128)S(1)} %get-tuple-element.55), channel_id=1, source_target_pairs={{0,17},{1,18},{2,19},{3,20},{4,21},{5,22},{6,23},{7,24},{8,25},{9,... | collective-permute-start | bytes 49160 | tf_op jit(solution)/shard_map/ppermute | solution.py:60
  32.6 5.4 %collective-permute-start.4 = (f32[8,512]{1,0:T(8,128)S(1)}, f32[8,512]{1,0:T(8,128)S(1)}, u32[]{:S(2)}, u32[]{:S(2)}) collective-permute-start(f32[8,512]{1,0:T(8,128)S(1)} %get-tuple-element.56), channel_id=1, source_target_pairs={{1,16},{2,17},{3,18},{4,19},{5,20},{6,21},{7,22},{8,23},{9,24},{10... | collective-permute-start | bytes 49160 | tf_op jit(solution)/shard_map/ppermute | solution.py:60
  38.0 0.8 copy-start.13
  38.7 0.8 copy-start.14
  44.3 23.0 %all-to-all-start.1 = ((f32[16,2,128]{2,1,0:T(2,128)}), f32[16,2,128]{2,1,0:T(2,128)S(1)}, u32[]{:S(2)}, u32[]{:S(2)}) async-start(f32[16,2,128]{2,1,0:T(2,128)} %get-tuple-element.59), calls=%async_computation.1 | async-start | bytes 32768 | tf_op jit(solution)/shard_map/all_to_all | solution.py:64
  56.0 1.0 copy-start
  57.0 1.0 copy-start.2
  68.1 15.5 %collective-permute-start.5 = (f32[80,512]{1,0:T(8,128)S(1)}, f32[80,512]{1,0:T(8,128)S(1)}, u32[]{:S(2)}, u32[]{:S(2)}) collective-permute-start(f32[80,512]{1,0:T(8,128)S(1)} %get-tuple-element.65), channel_id=1, source_target_pairs={{0,16},{16,32},{32,48},{48,64},{64,80},{80,96},{96,112},{112,128},... | collective-permute-start | bytes 491528 | tf_op jit(solution)/shard_map/ppermute | solution.py:55
  75.4 8.2 %collective-permute-start.6 = (f32[56,512]{1,0:T(8,128)S(1)}, f32[56,512]{1,0:T(8,128)S(1)}, u32[]{:S(2)}, u32[]{:S(2)}) collective-permute-start(f32[56,512]{1,0:T(8,128)S(1)} %get-tuple-element.66), channel_id=1, source_target_pairs={{16,0},{32,16},{48,32},{64,48},{80,64},{96,80},{112,96},{128,112},... | collective-permute-start | bytes 344072 | tf_op jit(solution)/shard_map/ppermute | solution.py:55
  77.3 6.3 %copy-start.1 = (f32[8,24,512]{2,1,0:T(8,128)S(1)}, f32[8,24,512]{2,1,0:T(8,128)}, u32[]{:S(2)}) copy-start(f32[8,24,512]{2,1,0:T(8,128)} %get-tuple-element.61.d_ref) | copy-start | bytes 1179652
  77.3 6.3 %copy-start.3 = (f32[8,24,512]{2,1,0:T(8,128)S(1)}, f32[8,24,512]{2,1,0:T(8,128)}, u32[]{:S(2)}) copy-start(f32[8,24,512]{2,1,0:T(8,128)} %get-tuple-element.62.g_ref) | copy-start | bytes 1179652
  77.3 6.3 %copy-start.9 = (f32[1,128,2048]{2,1,0:T(8,128)S(1)}, f32[1,128,2048]{2,1,0:T(8,128)}, u32[]{:S(2)}) copy-start(f32[1,128,2048]{2,1,0:T(8,128)} %inverse_ref.5) | copy-start | bytes 3145732
  77.3 6.3 %copy-start.12 = (s32[1,64]{1,0:T(1,128)S(1)}, s32[1,64]{1,0:T(1,128)}, u32[]{:S(2)}) copy-start(s32[1,64]{1,0:T(1,128)} %cell_ref.7) | copy-start | bytes 772
  84.9 14.7 %all-to-all-start.2 = ((f32[16,2,128]{2,1,0:T(2,128)}), f32[16,2,128]{2,1,0:T(2,128)S(1)}, u32[]{:S(2)}, u32[]{:S(2)}) async-start(f32[16,2,128]{2,1,0:T(2,128)} %get-tuple-element.69), calls=%async_computation.2 | async-start | bytes 32768 | tf_op jit(solution)/shard_map/all_to_all | solution.py:64
  88.4 1.0 copy-start.4
  100.3 11.2 %collective-permute-start.7 = (f32[80,512]{1,0:T(8,128)S(1)}, f32[80,512]{1,0:T(8,128)S(1)}, u32[]{:S(2)}, u32[]{:S(2)}) collective-permute-start(f32[80,512]{1,0:T(8,128)S(1)} %get-tuple-element.73), channel_id=1, source_target_pairs={{0,16},{16,32},{32,48},{48,64},{64,80},{80,96},{96,112},{112,128},... | collective-permute-start | bytes 491528 | tf_op jit(solution)/shard_map/ppermute | solution.py:55
  103.3 8.2 %collective-permute-start.8 = (f32[56,512]{1,0:T(8,128)S(1)}, f32[56,512]{1,0:T(8,128)S(1)}, u32[]{:S(2)}, u32[]{:S(2)}) collective-permute-start(f32[56,512]{1,0:T(8,128)S(1)} %get-tuple-element.74), channel_id=1, source_target_pairs={{16,0},{32,16},{48,32},{64,48},{80,64},{96,80},{112,96},{128,112},... | collective-permute-start | bytes 344072 | tf_op jit(solution)/shard_map/ppermute | solution.py:55
  105.2 6.3 %copy-start.5 = (f32[8,24,512]{2,1,0:T(8,128)S(1)}, f32[8,24,512]{2,1,0:T(8,128)}, u32[]{:S(2)}) copy-start(f32[8,24,512]{2,1,0:T(8,128)} %get-tuple-element.62.g_ref) | copy-start | bytes 1179652
  105.2 6.3 %copy-start.10 = (f32[1,128,2048]{2,1,0:T(8,128)S(1)}, f32[1,128,2048]{2,1,0:T(8,128)}, u32[]{:S(2)}) copy-start(f32[1,128,2048]{2,1,0:T(8,128)} %inverse_ref.5) | copy-start | bytes 3145732
  112.7 14.7 %all-to-all-start.3 = ((f32[16,2,128]{2,1,0:T(2,128)}), f32[16,2,128]{2,1,0:T(2,128)S(1)}, u32[]{:S(2)}, u32[]{:S(2)}) async-start(f32[16,2,128]{2,1,0:T(2,128)} %get-tuple-element.77), calls=%async_computation.3 | async-start | bytes 32768 | tf_op jit(solution)/shard_map/all_to_all | solution.py:64
  116.2 1.0 copy-start.6
  128.2 11.2 %collective-permute-start.9 = (f32[80,512]{1,0:T(8,128)S(1)}, f32[80,512]{1,0:T(8,128)S(1)}, u32[]{:S(2)}, u32[]{:S(2)}) collective-permute-start(f32[80,512]{1,0:T(8,128)S(1)} %get-tuple-element.81), channel_id=1, source_target_pairs={{0,16},{16,32},{32,48},{48,64},{64,80},{80,96},{96,112},{112,128},... | collective-permute-start | bytes 491528 | tf_op jit(solution)/shard_map/ppermute | solution.py:55
  131.1 8.2 %collective-permute-start.10 = (f32[56,512]{1,0:T(8,128)S(1)}, f32[56,512]{1,0:T(8,128)S(1)}, u32[]{:S(2)}, u32[]{:S(2)}) collective-permute-start(f32[56,512]{1,0:T(8,128)S(1)} %get-tuple-element.82), channel_id=1, source_target_pairs={{16,0},{32,16},{48,32},{64,48},{80,64},{96,80},{112,96},{128,112},... | collective-permute-start | bytes 344072 | tf_op jit(solution)/shard_map/ppermute | solution.py:55
  133.1 6.3 %copy-start.7 = (f32[8,24,512]{2,1,0:T(8,128)S(1)}, f32[8,24,512]{2,1,0:T(8,128)}, u32[]{:S(2)}) copy-start(f32[8,24,512]{2,1,0:T(8,128)} %get-tuple-element.62.g_ref) | copy-start | bytes 1179652
  133.1 6.3 %copy-start.11 = (f32[1,128,2048]{2,1,0:T(8,128)S(1)}, f32[1,128,2048]{2,1,0:T(8,128)}, u32[]{:S(2)}) copy-start(f32[1,128,2048]{2,1,0:T(8,128)} %inverse_ref.5) | copy-start | bytes 3145732
  140.6 14.7 %all-to-all-start.4 = ((f32[16,2,128]{2,1,0:T(2,128)}), f32[16,2,128]{2,1,0:T(2,128)S(1)}, u32[]{:S(2)}, u32[]{:S(2)}) async-start(f32[16,2,128]{2,1,0:T(2,128)} %get-tuple-element.85), calls=%async_computation.4 | async-start | bytes 32768 | tf_op jit(solution)/shard_map/all_to_all | solution.py:64
  144.2 1.0 copy-start.8
  156.1 8.2 %collective-permute-start.11 = (f32[56,512]{1,0:T(8,128)S(1)}, f32[56,512]{1,0:T(8,128)S(1)}, u32[]{:S(2)}, u32[]{:S(2)}) collective-permute-start(f32[56,512]{1,0:T(8,128)S(1)} %get-tuple-element.91), channel_id=1, source_target_pairs={{16,0},{32,16},{48,32},{64,48},{80,64},{96,80},{112,96},{128,112},... | collective-permute-start | bytes 344072 | tf_op jit(solution)/shard_map/ppermute | solution.py:55

commit v6 on v4

--- a/solution.py
+++ b/solution.py
@@ -430,7 +430,9 @@
     state_ref[FROM_BELOW + at : FROM_BELOW + at + 1] = up_ref[3 * GX : 3 * GX + 1, 0:LANES]
     volts = next_volts(state_ref, inverse_ref, n)
     if last:
-        rest[0][...] = volts
+        rest[1][...] = volts
+        sending = pltpu.make_async_copy(rest[1], rest[0], rest[2])
+        sending.start()
     for c in range(3):
         e_ref[c, 0] = up_ref[c * GX : (c + 1) * GX]
     for c in range(2):
@@ -440,6 +442,8 @@
     update_e(e_ref, h_ref, d_ref, g_ref, (2,), GX)
     pre = at_ports(e_ref[2, 1 : NZ + 1, :NX].reshape(NZ * NX, NY), own_ports(cell_ref[...]))
     payload(pay_out, pay_ref, sem, volts, pre).wait()
+    if last:
+        sending.wait()
 
 
 def k_exy_first(top_ref, d_ref, g_ref, e_in, h_in, e_ref, h_ref):
@@ -452,14 +456,15 @@
     update_e(e_ref, h_ref, d_ref, g_ref, (0, 1), GX)
 
 
-def k_last(down_ref, state_ref, e_ref, h_ref, h_in, h_out, wave_out, layer_ref, sem):
+def k_last(down_ref, state_ref, e_ref, h_ref, h_in, h_out, wave_out, layer_ref, wave_ref, sems):
+    above = down_ref[2 * GX : 2 * GX + 1, 0:LANES] + state_ref[WAVE + 1 : WAVE + 2]
+    wave_ref[...] = jnp.concatenate([state_ref[WAVE : WAVE + 1], above], 0)[None]
+    sending = copies([(wave_ref, wave_out)], sems)
     for c, value in enumerate(new_h(e_ref, h_ref, NZ, down_ref[0:GX], down_ref[GX : 2 * GX])):
         layer_ref[c] = value[:NX]
-    copy = pltpu.make_async_copy(layer_ref, h_out.at[:, NZ - 1], sem)
-    copy.start()
-    above = down_ref[2 * GX : 2 * GX + 1, 0:LANES] + state_ref[WAVE + 1 : WAVE + 2]
-    wave_out[...] = jnp.concatenate([state_ref[WAVE : WAVE + 1], above], 0)[None]
-    copy.wait()
+    sending.append(pltpu.make_async_copy(layer_ref, h_out.at[:, NZ - 1], sems.at[1]))
+    sending[1].start()
+    wait(sending)
 
 
 def local(
@@ -554,8 +559,8 @@
             [E_SHAPE, H_SHAPE, (ROWS, LANES), PAY_SHAPE] + ([(1, LANES)] if n + 1 == STEPS - 1 else []),
             up, down, d, g, inverse, port_cell, e, h, state,
             alias={6: 0, 7: 1, 8: 2},
-            far_out=(3,),
-            scratch=[pay_scratch, pltpu.SemaphoreType.DMA],
+            far_out=(3, 4) if n + 1 == STEPS - 1 else (3,),
+            scratch=([line, pltpu.SemaphoreType.DMA] if n + 1 == STEPS - 1 else []) + [pay_scratch, pltpu.SemaphoreType.DMA],
             name="volts",
         )
     h, e_out, h_out = call(
@@ -573,8 +578,8 @@
         down, state, e, h, h_out,
         alias={4: 0},
         far=(4,),
-        far_out=(0,),
-        scratch=[pltpu.VMEM((3, NX, NY), F32), pltpu.SemaphoreType.DMA],
+        far_out=(0, 1),
+        scratch=[pltpu.VMEM((3, NX, NY), F32), pltpu.VMEM((1, 2, LANES), F32), pltpu.SemaphoreType.DMA((2,))],
         name="last",
     )
     return e_out, h_out, node_volt[0], line_wave

time: 162 us -> 161 us (level)
  no operation moved by 1% of the time
where the time goes in v6:
time: 161 us; the launch traced here: 160 us
  starting transfers between devices  71.5 us (44%)
  waiting for transfers between devices  62.6 us (39%)
  Pallas kernels  18 us (11%)
  local copies, waits for them, and re-layouts  6.85 us (4%)
    all_to_all x5, waiting for transfers between devices, exchanged(): return lax.all_to_all(value, 'fxy', 0, 0, tiled=True)  38.8 us
    all_to_all x5, starting transfers between devices, exchanged(): return lax.all_to_all(value, 'fxy', 0, 0, tiled=True)  38.8 us
    ppermute x11, starting transfers between devices, shifted(): return lax.ppermute(value, axis, pairs)  32.7 us
    ppermute x11, waiting for transfers between devices, shifted(): return lax.ppermute(value, axis, pairs)  23.8 us
    pallas_call x19, Pallas kernels, call(): pl.pallas_call(kernel, out_shape=[pltpu.HBM(s, F32) if k in far_out else...  18 us
    unnamed x30, local copies, waits for them, and re-layouts  6.85 us
  transfers between devices with their start and end apart: 16, of which 9 were waited for; matrix products, arithmetic and copies ran while one was open for 0% of the time, Pallas kernels for 5%

profile of v6, /device:TPU:7, one launch (start us, length us, event | category | flops | bytes accessed | tf_op | source)
XLA Modules:
  0.0 160.0 jit_solution(2987820219751535864)
XLA Ops:
  0.6 2.7 %first.1 = (f32[16,2,128]{2,1,0:T(2,128)}, f32[8,256]{1,0:T(8,128)S(1)}, f32[256,512]{1,0:T(8,128)}, f32[256,512]{1,0:T(8,128)}) custom-call(f32[3,8,16,512]{3,2,1,0:T(8,128)} %e_in.3, f32[3,8,16,512]{3,2,1,0:T(8,128)} %h_in.3, f32[8,16,512]{2,1,0:T(8,128)} %d_in.3, f32[8,16,512]{2,1,0:T(8,128)} %g_in.3, s32[1,64]{1,0:T(1,128)} %cell_ref.7, ...), custom_call_target="tpu_custom_call" | custom-call | tf_op jit(solution)/shard_map/first/pallas_call | solution.py:40
  3.3 3.6 %collective-permute-start.1 = (f32[256,512]{1,0:T(8,128)}, f32[256,512]{1,0:T(8,128)S(1)}, u32[]{:S(2)}, u32[]{:S(2)}) collective-permute-start(f32[256,512]{1,0:T(8,128)} %get-tuple-element.53), channel_id=1, source_target_pairs={{0,1},{1,2},{2,3},{3,4},{4,5},{5,6},{6,7},{7,8},{8,9},{9,10},{10,1... | collective-permute-start | bytes 1572872 | tf_op jit(solution)/shard_map/ppermute | solution.py:55
  6.9 1.3 collective-permute-start.2
  8.2 16.6 %all-to-all-start = ((f32[16,2,128]{2,1,0:T(2,128)}), f32[16,2,128]{2,1,0:T(2,128)S(1)}, u32[]{:S(2)}, u32[]{:S(2)}) async-start(f32[16,2,128]{2,1,0:T(2,128)} %get-tuple-element.51), calls=%async_computation | async-start | bytes 32768 | tf_op jit(solution)/shard_map/all_to_all | solution.py:59
  24.8 4.5 %collective-permute-start = (f32[8,256]{1,0:T(8,128)S(1)}, f32[8,256]{1,0:T(8,128)S(1)}, u32[]{:S(2)}, u32[]{:S(2)}) collective-permute-start(f32[8,256]{1,0:T(8,128)S(1)} %get-tuple-element.52), channel_id=1, source_target_pairs={{0,16},{16,32},{32,48},{48,64},{64,80},{80,96},{96,112},{112,128},... | collective-permute-start | bytes 24584 | tf_op jit(solution)/shard_map/ppermute | solution.py:55
  29.3 0.8 collective-permute-done.lines_ref
  30.1 0.0 collective-permute-done.1.right_ref
  30.1 0.8 copy-done.12
  30.9 1.0 copy-done.13
  31.9 2.2 %start.1 = (f32[3,10,24,512]{3,2,1,0:T(8,128)S(1)}, f32[3,9,24,512]{3,2,1,0:T(8,128)S(1)}, f32[8,24,512]{2,1,0:T(8,128)}, f32[8,24,512]{2,1,0:T(8,128)}, f32[8,128]{1,0:T(8,128)S(1)}, /*index=5*/f32[48,512]{1,0:T(8,128)S(1)}) custom-call(f32[3,8,16,512]{3,2,1,0:T(8,128)} %e_in.3, f32[3,8,16,512]{3,2,1,0:T(8,128)} %h_in.3, f32[8,16,512]{2,1,0:T(8,128)} %d_in.3, ...), custom_call_target="tpu_custom_call" | custom-call | tf_op jit(solution)/shard_map/start/pallas_call | solution.py:40
  34.1 6.3 %collective-permute-start.3 = (f32[48,512]{1,0:T(8,128)S(1)}, f32[48,512]{1,0:T(8,128)S(1)}, u32[]{:S(2)}, u32[]{:S(2)}) collective-permute-start(f32[48,512]{1,0:T(8,128)S(1)} %get-tuple-element.57), channel_id=1, source_target_pairs={{0,16},{16,32},{32,48},{48,64},{64,80},{80,96},{96,112},{112,128},... | collective-permute-start | bytes 294920 | tf_op jit(solution)/shard_map/ppermute | solution.py:55
  40.4 2.4 %tables.1 = (f32[16,2,128]{2,1,0:T(2,128)}, f32[112,128]{1,0:T(8,128)S(1)}) custom-call(f32[16,2,128]{2,1,0:T(2,128)S(1)} %all-to-all-done.got_ref, f32[8,256]{1,0:T(8,128)S(1)} %collective-permute-done.lines_ref, f32[8,128]{1,0:T(8,128)S(1)} %get-tuple-element.55.pre_ref, s32[1,128]{1,0:T(1,128)} %near_in.1, s32[1,128]{1,0:T(1,128)} %delay_in.1, ...), custom_call_target="tpu_custom_call" | custom-call | tf_op jit(solution)/shard_map/tables/pallas_call | solution.py:40
  42.8 11.7 %all-to-all-start.1 = ((f32[16,2,128]{2,1,0:T(2,128)}), f32[16,2,128]{2,1,0:T(2,128)S(1)}, u32[]{:S(2)}, u32[]{:S(2)}) async-start(f32[16,2,128]{2,1,0:T(2,128)} %get-tuple-element.56), calls=%async_computation.1 | async-start | bytes 32768 | tf_op jit(solution)/shard_map/all_to_all | solution.py:59
  54.6 0.0 copy-start
  54.6 1.0 copy-done
  55.6 1.0 copy-done.2
  56.6 0.3 exy_first.1
  56.9 9.0 %all-to-all-done.1.got_ref = f32[16,2,128]{2,1,0:T(2,128)S(1)} async-done(((f32[16,2,128]{2,1,0:T(2,128)}), f32[16,2,128]{2,1,0:T(2,128)S(1)}, u32[]{:S(2)}, u32[]{:S(2)}) %all-to-all-start.1) | async-done | bytes 16416 | tf_op jit(solution)/shard_map/all_to_all | solution.py:59
  65.9 0.7 currents.4
  66.7 3.4 %collective-permute-start.4 = (f32[80,512]{1,0:T(8,128)S(1)}, f32[80,512]{1,0:T(8,128)S(1)}, u32[]{:S(2)}, u32[]{:S(2)}) collective-permute-start(f32[80,512]{1,0:T(8,128)S(1)} %get-tuple-element.64), channel_id=1, source_target_pairs={{0,16},{16,32},{32,48},{48,64},{64,80},{80,96},{96,112},{112,128},... | collective-permute-start | bytes 491528 | tf_op jit(solution)/shard_map/ppermute | solution.py:55
  70.0 1.9 %collective-permute-start.5 = (f32[56,512]{1,0:T(8,128)S(1)}, f32[56,512]{1,0:T(8,128)S(1)}, u32[]{:S(2)}, u32[]{:S(2)}) collective-permute-start(f32[56,512]{1,0:T(8,128)S(1)} %get-tuple-element.65), channel_id=1, source_target_pairs={{16,0},{32,16},{48,32},{64,48},{80,64},{96,80},{112,96},{128,112},... | collective-permute-start | bytes 344072 | tf_op jit(solution)/shard_map/ppermute | solution.py:55
  72.0 0.0 copy-start.1
  72.0 0.0 copy-start.3
  72.0 0.0 copy-start.9
  72.0 0.0 copy-start.14
  72.0 0.3 inner_h.3.h_in
  72.3 5.9 %collective-permute-done.5.down_ref = f32[56,512]{1,0:T(8,128)S(1)} collective-permute-done((f32[56,512]{1,0:T(8,128)S(1)}, f32[56,512]{1,0:T(8,128)S(1)}, u32[]{:S(2)}, u32[]{:S(2)}) %collective-permute-start.5) | collective-permute-done | bytes 114720 | tf_op jit(solution)/shard_map/ppermute | solution.py:55
  78.3 1.3 volts.3
  79.6 3.5 %all-to-all-start.2 = ((f32[16,2,128]{2,1,0:T(2,128)}), f32[16,2,128]{2,1,0:T(2,128)S(1)}, u32[]{:S(2)}, u32[]{:S(2)}) async-start(f32[16,2,128]{2,1,0:T(2,128)} %get-tuple-element.69), calls=%async_computation.2 | async-start | bytes 32768 | tf_op jit(solution)/shard_map/all_to_all | solution.py:59
  83.1 0.0 copy-start.4
  83.1 1.0 copy-done.4
  84.1 0.3 exy.3.e_in
  84.4 9.9 %all-to-all-done.2.got_ref = f32[16,2,128]{2,1,0:T(2,128)S(1)} async-done(((f32[16,2,128]{2,1,0:T(2,128)}), f32[16,2,128]{2,1,0:T(2,128)S(1)}, u32[]{:S(2)}, u32[]{:S(2)}) %all-to-all-start.2) | async-done | bytes 16416 | tf_op jit(solution)/shard_map/all_to_all | solution.py:59
  94.3 0.7 currents.5
  95.0 3.0 %collective-permute-start.6 = (f32[80,512]{1,0:T(8,128)S(1)}, f32[80,512]{1,0:T(8,128)S(1)}, u32[]{:S(2)}, u32[]{:S(2)}) collective-permute-start(f32[80,512]{1,0:T(8,128)S(1)} %get-tuple-element.73), channel_id=1, source_target_pairs={{0,16},{16,32},{32,48},{48,64},{64,80},{80,96},{96,112},{112,128},... | collective-permute-start | bytes 491528 | tf_op jit(solution)/shard_map/ppermute | solution.py:55
  98.0 1.9 %collective-permute-start.7 = (f32[56,512]{1,0:T(8,128)S(1)}, f32[56,512]{1,0:T(8,128)S(1)}, u32[]{:S(2)}, u32[]{:S(2)}) collective-permute-start(f32[56,512]{1,0:T(8,128)S(1)} %get-tuple-element.74), channel_id=1, source_target_pairs={{16,0},{32,16},{48,32},{64,48},{80,64},{96,80},{112,96},{128,112},... | collective-permute-start | bytes 344072 | tf_op jit(solution)/shard_map/ppermute | solution.py:55
  100.0 0.0 copy-start.5
  100.0 0.0 copy-start.10
  100.0 0.3 inner_h.4.h_in
  100.3 6.0 %collective-permute-done.7.down_ref = f32[56,512]{1,0:T(8,128)S(1)} collective-permute-done((f32[56,512]{1,0:T(8,128)S(1)}, f32[56,512]{1,0:T(8,128)S(1)}, u32[]{:S(2)}, u32[]{:S(2)}) %collective-permute-start.7) | collective-permute-done | bytes 114720 | tf_op jit(solution)/shard_map/ppermute | solution.py:55
  106.3 1.3 volts.4
  107.5 3.5 %all-to-all-start.3 = ((f32[16,2,128]{2,1,0:T(2,128)}), f32[16,2,128]{2,1,0:T(2,128)S(1)}, u32[]{:S(2)}, u32[]{:S(2)}) async-start(f32[16,2,128]{2,1,0:T(2,128)} %get-tuple-element.77), calls=%async_computation.3 | async-start | bytes 32768 | tf_op jit(solution)/shard_map/all_to_all | solution.py:59
  111.1 0.0 copy-start.6
  111.1 1.0 copy-done.6
  112.1 0.3 exy.4.e_in
  112.4 9.9 %all-to-all-done.3.got_ref = f32[16,2,128]{2,1,0:T(2,128)S(1)} async-done(((f32[16,2,128]{2,1,0:T(2,128)}), f32[16,2,128]{2,1,0:T(2,128)S(1)}, u32[]{:S(2)}, u32[]{:S(2)}) %all-to-all-start.3) | async-done | bytes 16416 | tf_op jit(solution)/shard_map/all_to_all | solution.py:59
  122.3 0.7 currents.6
  123.0 3.0 %collective-permute-start.8 = (f32[80,512]{1,0:T(8,128)S(1)}, f32[80,512]{1,0:T(8,128)S(1)}, u32[]{:S(2)}, u32[]{:S(2)}) collective-permute-start(f32[80,512]{1,0:T(8,128)S(1)} %get-tuple-element.81), channel_id=1, source_target_pairs={{0,16},{16,32},{32,48},{48,64},{64,80},{80,96},{96,112},{112,128},... | collective-permute-start | bytes 491528 | tf_op jit(solution)/shard_map/ppermute | solution.py:55
  125.9 1.9 %collective-permute-start.9 = (f32[56,512]{1,0:T(8,128)S(1)}, f32[56,512]{1,0:T(8,128)S(1)}, u32[]{:S(2)}, u32[]{:S(2)}) collective-permute-start(f32[56,512]{1,0:T(8,128)S(1)} %get-tuple-element.82), channel_id=1, source_target_pairs={{16,0},{32,16},{48,32},{64,48},{80,64},{96,80},{112,96},{128,112},... | collective-permute-start | bytes 344072 | tf_op jit(solution)/shard_map/ppermute | solution.py:55
  127.9 0.0 copy-start.7
  127.9 0.0 copy-start.11
  127.9 0.3 inner_h.5.h_in
  128.2 6.0 %collective-permute-done.9.down_ref = f32[56,512]{1,0:T(8,128)S(1)} collective-permute-done((f32[56,512]{1,0:T(8,128)S(1)}, f32[56,512]{1,0:T(8,128)S(1)}, u32[]{:S(2)}, u32[]{:S(2)}) %collective-permute-start.9) | collective-permute-done | bytes 114720 | tf_op jit(solution)/shard_map/ppermute | solution.py:55
  134.2 1.3 volts.5
  135.5 3.5 %all-to-all-start.4 = ((f32[16,2,128]{2,1,0:T(2,128)}), f32[16,2,128]{2,1,0:T(2,128)S(1)}, u32[]{:S(2)}, u32[]{:S(2)}) async-start(f32[16,2,128]{2,1,0:T(2,128)} %get-tuple-element.85), calls=%async_computation.4 | async-start | bytes 32768 | tf_op jit(solution)/shard_map/all_to_all | solution.py:59
  139.0 0.0 copy-start.8
  139.0 1.0 copy-done.8
  140.0 0.3 exy.5.e_in
  140.3 10.0 %all-to-all-done.4.got_ref = f32[16,2,128]{2,1,0:T(2,128)S(1)} async-done(((f32[16,2,128]{2,1,0:T(2,128)}), f32[16,2,128]{2,1,0:T(2,128)S(1)}, u32[]{:S(2)}, u32[]{:S(2)}) %all-to-all-start.4) | async-done | bytes 16416 | tf_op jit(solution)/shard_map/all_to_all | solution.py:59
  150.3 0.7 currents.7
  151.0 1.9 %collective-permute-start.10 = (f32[56,512]{1,0:T(8,128)S(1)}, f32[56,512]{1,0:T(8,128)S(1)}, u32[]{:S(2)}, u32[]{:S(2)}) collective-permute-start(f32[56,512]{1,0:T(8,128)S(1)} %get-tuple-element.91), channel_id=1, source_target_pairs={{16,0},{32,16},{48,32},{64,48},{80,64},{96,80},{112,96},{128,112},... | collective-permute-start | bytes 344072 | tf_op jit(solution)/shard_map/ppermute | solution.py:55
  153.0 1.2 inner_last.1
  154.1 5.1 %collective-permute-done.10.down_ref = f32[56,512]{1,0:T(8,128)S(1)} collective-permute-done((f32[56,512]{1,0:T(8,128)S(1)}, f32[56,512]{1,0:T(8,128)S(1)}, u32[]{:S(2)}, u32[]{:S(2)}) %collective-permute-start.10) | collective-permute-done | bytes 114720 | tf_op jit(solution)/shard_map/ppermute | solution.py:55
  159.2 0.8 last.1
  (17 shorter events, 0.0 us)
Async XLA Ops:
  3.3 26.7 %collective-permute-start.1 = (f32[256,512]{1,0:T(8,128)}, f32[256,512]{1,0:T(8,128)S(1)}, u32[]{:S(2)}, u32[]{:S(2)}) collective-permute-start(f32[256,512]{1,0:T(8,128)} %get-tuple-element.53), channel_id=1, source_target_pairs={{0,1},{1,2},{2,3},{3,4},{4,5},{5,6},{6,7},{7,8},{8,9},{9,10},{10,1... | collective-permute-start | bytes 1572872 | tf_op jit(solution)/shard_map/ppermute | solution.py:55
  6.9 23.2 %collective-permute-start.2 = (f32[256,512]{1,0:T(8,128)}, f32[256,512]{1,0:T(8,128)S(1)}, u32[]{:S(2)}, u32[]{:S(2)}) collective-permute-start(f32[256,512]{1,0:T(8,128)} %get-tuple-element.54), channel_id=1, source_target_pairs={{1,0},{2,1},{3,2},{4,3},{5,4},{6,5},{7,6},{8,7},{9,8},{10,9},{11,1... | collective-permute-start | bytes 1572872 | tf_op jit(solution)/shard_map/ppermute | solution.py:55
  8.2 32.2 %all-to-all-start = ((f32[16,2,128]{2,1,0:T(2,128)}), f32[16,2,128]{2,1,0:T(2,128)S(1)}, u32[]{:S(2)}, u32[]{:S(2)}) async-start(f32[16,2,128]{2,1,0:T(2,128)} %get-tuple-element.51), calls=%async_computation | async-start | bytes 32768 | tf_op jit(solution)/shard_map/all_to_all | solution.py:59
  24.8 5.3 %collective-permute-start = (f32[8,256]{1,0:T(8,128)S(1)}, f32[8,256]{1,0:T(8,128)S(1)}, u32[]{:S(2)}, u32[]{:S(2)}) collective-permute-start(f32[8,256]{1,0:T(8,128)S(1)} %get-tuple-element.52), channel_id=1, source_target_pairs={{0,16},{16,32},{32,48},{48,64},{64,80},{80,96},{96,112},{112,128},... | collective-permute-start | bytes 24584 | tf_op jit(solution)/shard_map/ppermute | solution.py:55
  30.1 0.8 copy-start.12
  30.9 1.0 copy-start.13
  34.1 20.5 %collective-permute-start.3 = (f32[48,512]{1,0:T(8,128)S(1)}, f32[48,512]{1,0:T(8,128)S(1)}, u32[]{:S(2)}, u32[]{:S(2)}) collective-permute-start(f32[48,512]{1,0:T(8,128)S(1)} %get-tuple-element.57), channel_id=1, source_target_pairs={{0,16},{16,32},{32,48},{48,64},{64,80},{80,96},{96,112},{112,128},... | collective-permute-start | bytes 294920 | tf_op jit(solution)/shard_map/ppermute | solution.py:55
  42.8 23.1 %all-to-all-start.1 = ((f32[16,2,128]{2,1,0:T(2,128)}), f32[16,2,128]{2,1,0:T(2,128)S(1)}, u32[]{:S(2)}, u32[]{:S(2)}) async-start(f32[16,2,128]{2,1,0:T(2,128)} %get-tuple-element.56), calls=%async_computation.1 | async-start | bytes 32768 | tf_op jit(solution)/shard_map/all_to_all | solution.py:59
  54.6 1.0 copy-start
  55.6 1.0 copy-start.2
  66.7 11.6 %collective-permute-start.4 = (f32[80,512]{1,0:T(8,128)S(1)}, f32[80,512]{1,0:T(8,128)S(1)}, u32[]{:S(2)}, u32[]{:S(2)}) collective-permute-start(f32[80,512]{1,0:T(8,128)S(1)} %get-tuple-element.64), channel_id=1, source_target_pairs={{0,16},{16,32},{32,48},{48,64},{64,80},{80,96},{96,112},{112,128},... | collective-permute-start | bytes 491528 | tf_op jit(solution)/shard_map/ppermute | solution.py:55
  70.0 8.2 %collective-permute-start.5 = (f32[56,512]{1,0:T(8,128)S(1)}, f32[56,512]{1,0:T(8,128)S(1)}, u32[]{:S(2)}, u32[]{:S(2)}) collective-permute-start(f32[56,512]{1,0:T(8,128)S(1)} %get-tuple-element.65), channel_id=1, source_target_pairs={{16,0},{32,16},{48,32},{64,48},{80,64},{96,80},{112,96},{128,112},... | collective-permute-start | bytes 344072 | tf_op jit(solution)/shard_map/ppermute | solution.py:55
  72.0 6.3 %copy-start.1 = (f32[8,24,512]{2,1,0:T(8,128)S(1)}, f32[8,24,512]{2,1,0:T(8,128)}, u32[]{:S(2)}) copy-start(f32[8,24,512]{2,1,0:T(8,128)} %get-tuple-element.58.d_ref) | copy-start | bytes 1179652
  72.0 6.3 %copy-start.3 = (f32[8,24,512]{2,1,0:T(8,128)S(1)}, f32[8,24,512]{2,1,0:T(8,128)}, u32[]{:S(2)}) copy-start(f32[8,24,512]{2,1,0:T(8,128)} %get-tuple-element.59.g_ref) | copy-start | bytes 1179652
  72.0 6.3 %copy-start.9 = (f32[1,128,2048]{2,1,0:T(8,128)S(1)}, f32[1,128,2048]{2,1,0:T(8,128)}, u32[]{:S(2)}) copy-start(f32[1,128,2048]{2,1,0:T(8,128)} %inverse_ref.5) | copy-start | bytes 3145732
  72.0 6.3 %copy-start.14 = (s32[1,64]{1,0:T(1,128)S(1)}, s32[1,64]{1,0:T(1,128)}, u32[]{:S(2)}) copy-start(s32[1,64]{1,0:T(1,128)} %cell_ref.7) | copy-start | bytes 772
  79.6 14.7 %all-to-all-start.2 = ((f32[16,2,128]{2,1,0:T(2,128)}), f32[16,2,128]{2,1,0:T(2,128)S(1)}, u32[]{:S(2)}, u32[]{:S(2)}) async-start(f32[16,2,128]{2,1,0:T(2,128)} %get-tuple-element.69), calls=%async_computation.2 | async-start | bytes 32768 | tf_op jit(solution)/shard_map/all_to_all | solution.py:59
  83.1 1.0 copy-start.4
  95.0 11.2 %collective-permute-start.6 = (f32[80,512]{1,0:T(8,128)S(1)}, f32[80,512]{1,0:T(8,128)S(1)}, u32[]{:S(2)}, u32[]{:S(2)}) collective-permute-start(f32[80,512]{1,0:T(8,128)S(1)} %get-tuple-element.73), channel_id=1, source_target_pairs={{0,16},{16,32},{32,48},{48,64},{64,80},{80,96},{96,112},{112,128},... | collective-permute-start | bytes 491528 | tf_op jit(solution)/shard_map/ppermute | solution.py:55
  98.0 8.2 %collective-permute-start.7 = (f32[56,512]{1,0:T(8,128)S(1)}, f32[56,512]{1,0:T(8,128)S(1)}, u32[]{:S(2)}, u32[]{:S(2)}) collective-permute-start(f32[56,512]{1,0:T(8,128)S(1)} %get-tuple-element.74), channel_id=1, source_target_pairs={{16,0},{32,16},{48,32},{64,48},{80,64},{96,80},{112,96},{128,112},... | collective-permute-start | bytes 344072 | tf_op jit(solution)/shard_map/ppermute | solution.py:55
  100.0 6.3 %copy-start.5 = (f32[8,24,512]{2,1,0:T(8,128)S(1)}, f32[8,24,512]{2,1,0:T(8,128)}, u32[]{:S(2)}) copy-start(f32[8,24,512]{2,1,0:T(8,128)} %get-tuple-element.59.g_ref) | copy-start | bytes 1179652
  100.0 6.3 %copy-start.10 = (f32[1,128,2048]{2,1,0:T(8,128)S(1)}, f32[1,128,2048]{2,1,0:T(8,128)}, u32[]{:S(2)}) copy-start(f32[1,128,2048]{2,1,0:T(8,128)} %inverse_ref.5) | copy-start | bytes 3145732
  107.5 14.7 %all-to-all-start.3 = ((f32[16,2,128]{2,1,0:T(2,128)}), f32[16,2,128]{2,1,0:T(2,128)S(1)}, u32[]{:S(2)}, u32[]{:S(2)}) async-start(f32[16,2,128]{2,1,0:T(2,128)} %get-tuple-element.77), calls=%async_computation.3 | async-start | bytes 32768 | tf_op jit(solution)/shard_map/all_to_all | solution.py:59
  111.1 1.0 copy-start.6
  123.0 11.2 %collective-permute-start.8 = (f32[80,512]{1,0:T(8,128)S(1)}, f32[80,512]{1,0:T(8,128)S(1)}, u32[]{:S(2)}, u32[]{:S(2)}) collective-permute-start(f32[80,512]{1,0:T(8,128)S(1)} %get-tuple-element.81), channel_id=1, source_target_pairs={{0,16},{16,32},{32,48},{48,64},{64,80},{80,96},{96,112},{112,128},... | collective-permute-start | bytes 491528 | tf_op jit(solution)/shard_map/ppermute | solution.py:55
  125.9 8.2 %collective-permute-start.9 = (f32[56,512]{1,0:T(8,128)S(1)}, f32[56,512]{1,0:T(8,128)S(1)}, u32[]{:S(2)}, u32[]{:S(2)}) collective-permute-start(f32[56,512]{1,0:T(8,128)S(1)} %get-tuple-element.82), channel_id=1, source_target_pairs={{16,0},{32,16},{48,32},{64,48},{80,64},{96,80},{112,96},{128,112},... | collective-permute-start | bytes 344072 | tf_op jit(solution)/shard_map/ppermute | solution.py:55
  127.9 6.3 %copy-start.7 = (f32[8,24,512]{2,1,0:T(8,128)S(1)}, f32[8,24,512]{2,1,0:T(8,128)}, u32[]{:S(2)}) copy-start(f32[8,24,512]{2,1,0:T(8,128)} %get-tuple-element.59.g_ref) | copy-start | bytes 1179652
  127.9 6.3 %copy-start.11 = (f32[1,128,2048]{2,1,0:T(8,128)S(1)}, f32[1,128,2048]{2,1,0:T(8,128)}, u32[]{:S(2)}) copy-start(f32[1,128,2048]{2,1,0:T(8,128)} %inverse_ref.5) | copy-start | bytes 3145732
  135.5 14.8 %all-to-all-start.4 = ((f32[16,2,128]{2,1,0:T(2,128)}), f32[16,2,128]{2,1,0:T(2,128)S(1)}, u32[]{:S(2)}, u32[]{:S(2)}) async-start(f32[16,2,128]{2,1,0:T(2,128)} %get-tuple-element.85), calls=%async_computation.4 | async-start | bytes 32768 | tf_op jit(solution)/shard_map/all_to_all | solution.py:59
  139.0 1.0 copy-start.8
  151.0 8.2 %collective-permute-start.10 = (f32[56,512]{1,0:T(8,128)S(1)}, f32[56,512]{1,0:T(8,128)S(1)}, u32[]{:S(2)}, u32[]{:S(2)}) collective-permute-start(f32[56,512]{1,0:T(8,128)S(1)} %get-tuple-element.91), channel_id=1, source_target_pairs={{16,0},{32,16},{48,32},{64,48},{80,64},{96,80},{112,96},{128,112},... | collective-permute-start | bytes 344072 | tf_op jit(solution)/shard_map/ppermute | solution.py:55
